TPU v7x, 32 devices: a whole 2x2x4 slice. The times are simulated.
32 devices in a mesh: shard: 2 (over core), ctx: 4 (over y, x), tensor: 4 (over z).
Axes of the slice: x: 2, y: 2, z: 4, core: 2. Of those that a mesh axis runs over, the one named last changes fastest.
Arguments:
- inputs: bfloat16 [2, 2048, 2048], P('shard', ('ctx', 'tensor')), may hold values from -6 to 6
- out_grad: bfloat16 [2, 2048, 2048], P('shard', ('ctx', 'tensor')), may hold values from -6 to 6
- block_order: int32 [2, 8], P('shard'), may hold values from 0 to 7, each once within a row
- gain_attn: bfloat16 [2048], P(('shard', 'ctx')), may hold values from 0.5 to 1.5
- w_query: bfloat16 [2048, 2048], P(('shard', 'ctx'), 'tensor'), may hold values from -0.125 to 0.125
- w_keyval: bfloat16 [2048, 512], P(('shard', 'ctx'), 'tensor'), may hold values from -0.125 to 0.125
- w_output: bfloat16 [2048, 2048], P(('shard', 'ctx'), 'tensor'), may hold values from -3 to 3
- gain_mlp: bfloat16 [2048], P(('shard', 'ctx')), may hold values from 0.5 to 1.5
- w_gate: bfloat16 [2048, 5632], P(('shard', 'ctx'), 'tensor'), may hold values from -0.125 to 0.125
- w_up: bfloat16 [2048, 5632], P(('shard', 'ctx'), 'tensor'), may hold values from -0.125 to 0.125
- w_down: bfloat16 [2048, 5632], P(('shard', 'ctx'), 'tensor'), may hold values from -0.078125 to 0.078125
Outputs:
- layer_out: bfloat16 [2, 2048, 2048], P('shard', ('ctx', 'tensor'))
- input_grad: float32 [2, 2048, 2048], P('shard', ('ctx', 'tensor'))
- grad_gain_attn: float32 [2048], P(('shard', 'ctx'))
- grad_query: float32 [2048, 2048], P(('shard', 'ctx'), 'tensor')
- grad_keyval: float32 [2048, 512], P(('shard', 'ctx'), 'tensor')
- grad_output: float32 [2048, 2048], P(('shard', 'ctx'), 'tensor')
- grad_gain_mlp: float32 [2048], P(('shard', 'ctx'))
- grad_gate: float32 [2048, 5632], P(('shard', 'ctx'), 'tensor')
- grad_up: float32 [2048, 5632], P(('shard', 'ctx'), 'tensor')
- grad_down: float32 [2048, 5632], P(('shard', 'ctx'), 'tensor')
Inputs may be any that keep to these rules, and one draw needn't show every extreme that they name: `block_order`: each row is a permutation of the blocks of one sequence.
All inputs are finite; a program needn't handle non-finite values.
Results may differ from a plain program's by a relative error of at most 0.014.
Values may be sent and summed in bfloat16 or wider, within the bound.
A program may use at most 192 MiB of HBM per device.

v0:
```python
import jax
import jax.numpy as jnp
from jax import lax
from jax.sharding import PartitionSpec as P

HD = 64
BLOCK = 256
BLOCKS = 8


epsilon = 1e-05
blocked = -1e30


def apply_norm(values_in):
    inverse_root_mean = lax.rsqrt(jnp.mean(values_in * values_in, -1, keepdims=True) + epsilon)
    return (values_in * inverse_root_mean, inverse_root_mean)


def norm_backward_pass(normed_gradient, unit_rows, inverse_root_mean, norm_scale):
    unit_rows_gradient = normed_gradient * norm_scale
    scale_gradient = jnp.sum(normed_gradient * unit_rows, axis=(0, 1))
    value_gradients = inverse_root_mean * (
        unit_rows_gradient - unit_rows * jnp.mean(unit_rows_gradient * unit_rows, -1, keepdims=True)
    )
    return (scale_gradient, value_gradients)


def rotary_tables(position, width):
    half_width = width // 2
    frequency = 10000.0 ** (-jnp.arange(half_width, dtype=jnp.float32) * 2.0 / width)
    angles = position.astype(jnp.float32)[..., None] * frequency
    return (jnp.cos(angles)[:, :, None, :], jnp.sin(angles)[:, :, None, :])


def rotate(values_in, cosine_table, sine_table):
    half_width = values_in.shape[-1] // 2
    first_half = values_in[..., :half_width]
    second = values_in[..., half_width:]
    return jnp.concatenate(
        [
            first_half * cosine_table - second * sine_table,
            second * cosine_table + first_half * sine_table,
        ],
        -1,
    )


def unrotate(grad_in, cosine_table, sine_table):
    half_width = grad_in.shape[-1] // 2
    first_half = grad_in[..., :half_width]
    second = grad_in[..., half_width:]
    return jnp.concatenate(
        [
            first_half * cosine_table + second * sine_table,
            second * cosine_table - first_half * sine_table,
        ],
        -1,
    )


def broadcast_rows(values_in):
    return lax.all_gather(values_in, "tensor", axis=1, tiled=True)


def spread_grads(values_in):
    return lax.all_gather(values_in, "tensor", axis=1, tiled=True)


def branch_sum(partial_sum):
    return lax.psum_scatter(partial_sum, "tensor", scatter_dimension=1, tiled=True)


def input_sum(partial_sum):
    return lax.psum_scatter(partial_sum, "tensor", scatter_dimension=1, tiled=True)


def body(
    inputs,
    out_grad,
    block_order,
    gain_attn,
    w_query,
    w_keyval,
    w_output,
    gain_mlp,
    w_gate,
    w_up,
    w_down,
):
    seq_count = inputs.shape[0]
    length = BLOCK * BLOCKS
    query_rows = length // lax.axis_size("ctx")
    heads_here = w_query.shape[1] // HD
    groups_here = w_keyval.shape[1] // (2 * HD)
    per_group = heads_here // groups_here
    inv_root = HD ** (-0.5)
    f32 = jnp.float32
    brain_float_sixteen = jnp.bfloat16
    slot_index = jnp.arange(length, dtype=jnp.int32)
    chooser = (slot_index // BLOCK)[:, None] == jnp.arange(BLOCKS, dtype=jnp.int32)[None, :]
    block_all = jnp.sum(jnp.where(chooser[None, :, :], block_order[:, None, :], 0), axis=-1)
    position_all = block_all * BLOCK + slot_index % BLOCK
    row_start = lax.axis_index("ctx") * query_rows
    block_here = lax.dynamic_slice_in_dim(block_all, row_start, query_rows, 1)
    position_here = lax.dynamic_slice_in_dim(position_all, row_start, query_rows, 1)
    allowed = block_all[:, None, :] <= block_here[:, :, None]
    cosine_table, sine_table = rotary_tables(position_here, HD)
    group_ids = jnp.arange(heads_here, dtype=jnp.int32) // per_group
    attention_norm_scale, query_all, keyval_all, output_all = (
        lax.all_gather(gain_attn, ("shard", "ctx"), axis=0, tiled=True),
        lax.all_gather(w_query, ("shard", "ctx"), axis=0, tiled=True),
        lax.all_gather(w_keyval, ("shard", "ctx"), axis=0, tiled=True),
        lax.all_gather(w_output, ("shard", "ctx"), axis=0, tiled=True),
    )
    feedforward_norm_scale, gate_all, up_all, down_all = (
        lax.all_gather(gain_mlp, ("shard", "ctx"), axis=0, tiled=True),
        lax.all_gather(w_gate, ("shard", "ctx"), axis=0, tiled=True),
        lax.all_gather(w_up, ("shard", "ctx"), axis=0, tiled=True),
        lax.all_gather(w_down, ("shard", "ctx"), axis=0, tiled=True),
    )
    attention_norm_scale = attention_norm_scale.astype(f32)
    feedforward_norm_scale = feedforward_norm_scale.astype(f32)
    residual_stream = inputs.astype(f32)
    first_unit_rows, first_inverse_root = apply_norm(residual_stream)
    first_normed = broadcast_rows(
        (first_unit_rows * attention_norm_scale).astype(brain_float_sixteen)
    )
    query_raw = jnp.einsum("sqd,dh->sqh", first_normed, query_all, preferred_element_type=f32)
    keyval_raw = jnp.einsum("sqd,dh->sqh", first_normed, keyval_all, preferred_element_type=f32)
    query_raw = query_raw.reshape(seq_count, query_rows, heads_here, HD)
    keyval_raw = keyval_raw.reshape(seq_count, query_rows, groups_here, 2 * HD)
    queries = rotate(query_raw, cosine_table, sine_table).astype(brain_float_sixteen)
    keys_here = rotate(keyval_raw[..., :HD], cosine_table, sine_table).astype(brain_float_sixteen)
    values_here = keyval_raw[..., HD:].astype(brain_float_sixteen)
    keyval_here = jnp.concatenate([keys_here, values_here], -1).reshape(
        seq_count, query_rows, groups_here * 2 * HD
    )
    keyval_seq = lax.all_gather(keyval_here, "ctx", axis=1, tiled=True).reshape(
        seq_count, length, groups_here, 2 * HD
    )
    query_heads = jnp.moveaxis(queries, 2, 0)

    def scores_of(query_head, group_id):
        keyval_group = lax.dynamic_index_in_dim(keyval_seq, group_id, 2, keepdims=False)
        keys_group = keyval_group[..., :HD]
        values_group = keyval_group[..., HD:]
        raw_scores = (
            jnp.einsum("sqd,skd->sqk", query_head, keys_group, preferred_element_type=f32)
            * inv_root
        )
        return (jnp.where(allowed, raw_scores, blocked), keys_group, values_group)

    def forward_head(operands):
        query_head, group_id = operands
        masked, keys_group, values_group = scores_of(query_head, group_id)
        row_max = jnp.max(masked, -1, keepdims=True)
        exponent = jnp.exp(masked - row_max)
        expsum = jnp.sum(exponent, -1, keepdims=True)
        weights = (exponent / expsum).astype(brain_float_sixteen)
        head_out = jnp.einsum(
            "sqk,skd->sqd", weights, values_group, preferred_element_type=f32
        ).astype(brain_float_sixteen)
        return (head_out, (row_max + jnp.log(expsum))[..., 0])

    head_outs, log_sums = lax.map(forward_head, (query_heads, group_ids))
    attn_out = jnp.moveaxis(head_outs, 0, 2).reshape(seq_count, query_rows, heads_here * HD)
    attn_branch = branch_sum(
        jnp.einsum("sqh,dh->sqd", attn_out, output_all, preferred_element_type=f32)
    )
    between_rows = residual_stream + attn_branch
    second_unit_rows, second_inverse_root = apply_norm(between_rows)
    second_normed = broadcast_rows(
        (second_unit_rows * feedforward_norm_scale).astype(brain_float_sixteen)
    )
    gate_act = jnp.einsum("sqd,df->sqf", second_normed, gate_all, preferred_element_type=f32)
    up_act = jnp.einsum("sqd,df->sqf", second_normed, up_all, preferred_element_type=f32)
    sig_gate = jax.nn.sigmoid(gate_act)
    silu_gate = gate_act * sig_gate
    hidden = (silu_gate * up_act).astype(brain_float_sixteen)
    mlp_branch = branch_sum(jnp.einsum("sqf,df->sqd", hidden, down_all, preferred_element_type=f32))
    layer_out = (between_rows + mlp_branch).astype(brain_float_sixteen)
    attention_norm_scale, query_all, keyval_all, output_all = (
        lax.all_gather(gain_attn, ("shard", "ctx"), axis=0, tiled=True),
        lax.all_gather(w_query, ("shard", "ctx"), axis=0, tiled=True),
        lax.all_gather(w_keyval, ("shard", "ctx"), axis=0, tiled=True),
        lax.all_gather(w_output, ("shard", "ctx"), axis=0, tiled=True),
    )
    feedforward_norm_scale, gate_all, up_all, down_all = (
        lax.all_gather(gain_mlp, ("shard", "ctx"), axis=0, tiled=True),
        lax.all_gather(w_gate, ("shard", "ctx"), axis=0, tiled=True),
        lax.all_gather(w_up, ("shard", "ctx"), axis=0, tiled=True),
        lax.all_gather(w_down, ("shard", "ctx"), axis=0, tiled=True),
    )
    attention_norm_scale = attention_norm_scale.astype(f32)
    feedforward_norm_scale = feedforward_norm_scale.astype(f32)
    grad_mlp_rows = spread_grads(out_grad)
    d_hidden = jnp.einsum("sqd,df->sqf", grad_mlp_rows, down_all, preferred_element_type=f32)
    grad_down_w = jnp.einsum("sqd,sqf->df", grad_mlp_rows, hidden, preferred_element_type=f32)
    d_gate = (d_hidden * up_act * sig_gate * (1.0 + gate_act * (1.0 - sig_gate))).astype(
        brain_float_sixteen
    )
    d_up = (d_hidden * silu_gate).astype(brain_float_sixteen)
    grad_gate_w = jnp.einsum("sqd,sqf->df", second_normed, d_gate, preferred_element_type=f32)
    grad_up_w = jnp.einsum("sqd,sqf->df", second_normed, d_up, preferred_element_type=f32)
    second_normed_gradient = input_sum(
        jnp.einsum("sqf,df->sqd", d_gate, gate_all, preferred_element_type=f32)
        + jnp.einsum("sqf,df->sqd", d_up, up_all, preferred_element_type=f32)
    )
    feedforward_scale_gradient, middle_gradient = norm_backward_pass(
        second_normed_gradient, second_unit_rows, second_inverse_root, feedforward_norm_scale
    )
    middle_gradient = middle_gradient + out_grad.astype(f32)
    grad_attn_rows = spread_grads(middle_gradient.astype(brain_float_sixteen))
    d_attn = jnp.einsum(
        "sqd,dh->sqh", grad_attn_rows, output_all, preferred_element_type=f32
    ).astype(brain_float_sixteen)
    grad_output_w = jnp.einsum("sqd,sqh->dh", grad_attn_rows, attn_out, preferred_element_type=f32)
    d_heads = jnp.moveaxis(d_attn.reshape(seq_count, query_rows, heads_here, HD), 2, 0)

    def backward_head(accumulated, operands):
        query_head, d_head, log_sum, group_id = operands
        masked, keys_group, values_group = scores_of(query_head, group_id)
        probs_f = jnp.exp(masked - log_sum[..., None])
        d_prob = jnp.einsum("sqd,skd->sqk", d_head, values_group, preferred_element_type=f32)
        row_delta = jnp.sum(probs_f * d_prob, -1, keepdims=True)
        d_score = (probs_f * (d_prob - row_delta)).astype(brain_float_sixteen)
        d_query = (
            jnp.einsum("sqk,skd->sqd", d_score, keys_group, preferred_element_type=f32) * inv_root
        )
        d_key = (
            jnp.einsum("sqk,sqd->skd", d_score, query_head, preferred_element_type=f32) * inv_root
        )
        d_value = jnp.einsum(
            "sqk,sqd->skd", probs_f.astype(brain_float_sixteen), d_head, preferred_element_type=f32
        )
        current = lax.dynamic_index_in_dim(accumulated, group_id, 2, keepdims=False)
        accumulated = lax.dynamic_update_index_in_dim(
            accumulated, current + jnp.concatenate([d_key, d_value], -1), group_id, 2
        )
        return (accumulated, d_query)

    zero_grads = jnp.zeros((seq_count, length, groups_here, 2 * HD), f32)
    d_keyval_seq, d_queries = lax.scan(
        backward_head, zero_grads, (query_heads, d_heads, log_sums, group_ids)
    )
    d_keyval = lax.psum_scatter(
        d_keyval_seq.reshape(seq_count, length, groups_here * 2 * HD),
        "ctx",
        scatter_dimension=1,
        tiled=True,
    ).reshape(seq_count, query_rows, groups_here, 2 * HD)
    d_keyval_raw = (
        jnp.concatenate(
            [unrotate(d_keyval[..., :HD], cosine_table, sine_table), d_keyval[..., HD:]], -1
        )
        .astype(brain_float_sixteen)
        .reshape(seq_count, query_rows, groups_here * 2 * HD)
    )
    d_query_raw = (
        unrotate(jnp.moveaxis(d_queries, 0, 2), cosine_table, sine_table)
        .astype(brain_float_sixteen)
        .reshape(seq_count, query_rows, heads_here * HD)
    )
    grad_query_w = jnp.einsum("sqd,sqh->dh", first_normed, d_query_raw, preferred_element_type=f32)
    grad_keyval_w = jnp.einsum(
        "sqd,sqh->dh", first_normed, d_keyval_raw, preferred_element_type=f32
    )
    first_normed_gradient = input_sum(
        jnp.einsum("sqh,dh->sqd", d_query_raw, query_all, preferred_element_type=f32)
        + jnp.einsum("sqh,dh->sqd", d_keyval_raw, keyval_all, preferred_element_type=f32)
    )
    attention_scale_gradient, residual_gradient = norm_backward_pass(
        first_normed_gradient, first_unit_rows, first_inverse_root, attention_norm_scale
    )
    input_grad = middle_gradient + residual_gradient
    gain_a_sum, grad_query, grad_keyval, grad_output = (
        lax.psum_scatter(
            attention_scale_gradient, ("shard", "ctx"), scatter_dimension=0, tiled=True
        ),
        lax.psum_scatter(grad_query_w, ("shard", "ctx"), scatter_dimension=0, tiled=True),
        lax.psum_scatter(grad_keyval_w, ("shard", "ctx"), scatter_dimension=0, tiled=True),
        lax.psum_scatter(grad_output_w, ("shard", "ctx"), scatter_dimension=0, tiled=True),
    )
    gain_m_sum, grad_gate, grad_up, grad_down = (
        lax.psum_scatter(
            feedforward_scale_gradient, ("shard", "ctx"), scatter_dimension=0, tiled=True
        ),
        lax.psum_scatter(grad_gate_w, ("shard", "ctx"), scatter_dimension=0, tiled=True),
        lax.psum_scatter(grad_up_w, ("shard", "ctx"), scatter_dimension=0, tiled=True),
        lax.psum_scatter(grad_down_w, ("shard", "ctx"), scatter_dimension=0, tiled=True),
    )
    grad_gain_attn, grad_gain_mlp = lax.psum((gain_a_sum, gain_m_sum), "tensor")
    return (
        layer_out,
        input_grad,
        grad_gain_attn,
        grad_query,
        grad_keyval,
        grad_output,
        grad_gain_mlp,
        grad_gate,
        grad_up,
        grad_down,
    )


def solution(mesh):
    return jax.shard_map(
        body,
        mesh=mesh,
        in_specs=(
            P("shard", ("ctx", "tensor"), None),
            P("shard", ("ctx", "tensor"), None),
            P("shard", None),
            P(("shard", "ctx")),
            P(("shard", "ctx"), "tensor"),
            P(("shard", "ctx"), "tensor"),
            P(("shard", "ctx"), "tensor"),
            P(("shard", "ctx")),
            P(("shard", "ctx"), "tensor"),
            P(("shard", "ctx"), "tensor"),
            P(("shard", "ctx"), "tensor"),
        ),
        out_specs=(
            P("shard", ("ctx", "tensor"), None),
            P("shard", ("ctx", "tensor"), None),
            P(("shard", "ctx")),
            P(("shard", "ctx"), "tensor"),
            P(("shard", "ctx"), "tensor"),
            P(("shard", "ctx"), "tensor"),
            P(("shard", "ctx")),
            P(("shard", "ctx"), "tensor"),
            P(("shard", "ctx"), "tensor"),
            P(("shard", "ctx"), "tensor"),
        ),
        check_vma=False,
    )
```

profile of v0, /device:TPU:9, one launch (start us, length us, event | category | flops | bytes accessed | tf_op | source)
XLA Modules:
  0.0 1317.9 jit_solution(5621312489691871391)
XLA Ops:
  7.9 14.2 %all-gather.1 = bf16[8,1,256]{2,1,0:T(2,128)(2,1)S(1)} all-gather(bf16[1,1,256]{2,1,0:T(2,128)(2,1)S(1)} %reshape.754), channel_id=1, replica_groups=mesh['shard'=2,'ctx'=4,'tensor'=4] {'shard','ctx'}, dimensions={0}, use_global_device_ids=true | all-gather | bytes 4608 | tf_op jit(solution)/shard_map/all_gather | solution.py:111
  28.4 25.4 %all_gather.50 = bf16[2048,128]{1,0:T(8,128)(2,1)S(1)} all-gather(bf16[256,128]{1,0:T(8,128)(2,1)} %param.20), channel_id=1, replica_groups=mesh['shard'=2,'ctx'=4,'tensor'=4] {'shard','ctx'}, dimensions={0}, use_global_device_ids=true | all-gather | bytes 589824 | tf_op jit(solution)/shard_map/all_gather | solution.py:113
  54.1 16.2 %all-gather.13.cloned.1.call-done = bf16[1,512,2048]{2,1,0:T(8,128)(2,1)} async-done(((bf16[1,128,2048]{2,1,0:T(8,128)(2,1)}), bf16[1,512,2048]{2,1,0:T(8,128)(2,1)}) %all-gather.13.cloned.1.call-update) | async-done | bytes 2097168 | tf_op jit(solution)/shard_map/all_gather | solution.py:63
  70.3 2.4 fusion.63
  73.1 8.3 all-gather
  81.7 19.4 %all-gather.15.cloned.1.call-done = bf16[2048,512]{1,0:T(8,128)(2,1)} async-done(((bf16[256,512]{1,0:T(8,128)(2,1)}), bf16[2048,512]{1,0:T(8,128)(2,1)}) %all-gather.15.cloned.1.call-update) | async-done | bytes 2097168 | tf_op jit(solution)/shard_map/all_gather | solution.py:112
  101.2 3.9 copy.45
  105.1 2.9 fusion.57
  109.6 29.6 %while.28 = (s32[]{:T(128)}, bf16[8,1,512,64]{2,3,1,0:T(8,128)(2,1)S(1)}, f32[8,1,512]{2,1,0:T(1,128)S(1)}, bf16[8,1,512,64]{3,2,1,0:T(8,128)(2,1)}, bf16[1,2048...) while((s32[]{:T(128)}, ...), condition=%wide.region_5.6_spmd.clone, body=%wide.region_2.5_spmd.clone.sunk | while | flops 277904896 | bytes 13859421 | solution.py:166
  139.2 5.1 convolution_bitcast_fusion.3
  144.9 13.7 %all-gather.2 = bf16[8,1,256]{2,1,0:T(2,128)(2,1)S(1)} all-gather(bf16[1,1,256]{2,1,0:T(2,128)(2,1)S(1)} %reshape.756), channel_id=1, replica_groups=mesh['shard'=2,'ctx'=4,'tensor'=4] {'shard','ctx'}, dimensions={0}, use_global_device_ids=true | all-gather | bytes 4608 | tf_op jit(solution)/shard_map/all_gather | solution.py:117
  158.7 62.1 %reduce-scatter.12.cloned.1.call-done = f32[1,128,2048]{2,1,0:T(8,128)} async-done(((f32[1,512,2048]{2,1,0:T(8,128)}), f32[1,128,2048]{2,1,0:T(8,128)}) %reduce-scatter.12.cloned.1.call-update) | async-done | bytes 1048592 | tf_op jit(solution)/shard_map/reduce_scatter | solution.py:71
  225.9 41.1 %all-gather.23.cloned.1.call-done = bf16[2048,1408]{1,0:T(8,128)(2,1)} async-done(((bf16[256,1408]{1,0:T(8,128)(2,1)}), bf16[2048,1408]{1,0:T(8,128)(2,1)}) %all-gather.23.cloned.1.call-update) | async-done | bytes 5767184 | tf_op jit(solution)/shard_map/all_gather | solution.py:119
  266.9 45.8 %all-gather.19.cloned.1.call-done = bf16[1,512,2048]{2,1,0:T(8,128)(2,1)} async-done(((bf16[1,128,2048]{2,1,0:T(8,128)(2,1)}), bf16[1,512,2048]{2,1,0:T(8,128)(2,1)}) %all-gather.19.cloned.1.call-update) | async-done | bytes 2097168 | tf_op jit(solution)/shard_map/all_gather | solution.py:63
  312.7 8.3 fusion.41
  321.0 38.1 %all-gather.21.cloned.1.call-done = bf16[2048,1408]{1,0:T(8,128)(2,1)} async-done(((bf16[256,1408]{1,0:T(8,128)(2,1)}), bf16[2048,1408]{1,0:T(8,128)(2,1)}) %all-gather.21.cloned.1.call-update) | async-done | bytes 5767184 | tf_op jit(solution)/shard_map/all_gather | solution.py:118
  359.1 8.2 fusion.43
  367.3 37.1 %all-gather.27.cloned.1.call-done = bf16[1,512,2048]{2,1,0:T(8,128)(2,1)} async-done(((bf16[1,128,2048]{2,1,0:T(8,128)(2,1)}), bf16[1,512,2048]{2,1,0:T(8,128)(2,1)}) %all-gather.27.cloned.1.call-update) | async-done | bytes 2097168 | tf_op jit(solution)/shard_map/all_gather | solution.py:67
  404.4 46.4 %all-gather.25.cloned.1.call-done = bf16[2048,1408]{1,0:T(8,128)(2,1)} async-done(((bf16[256,1408]{1,0:T(8,128)(2,1)}), bf16[2048,1408]{1,0:T(8,128)(2,1)}) %all-gather.25.cloned.1.call-update) | async-done | bytes 5767184 | tf_op jit(solution)/shard_map/all_gather | solution.py:120
  450.8 10.4 multiply_convert_fusion.1
  461.3 3.4 fusion.101
  464.7 7.7 add_bitcast_fusion.1
  472.5 76.5 %reduce-scatter.16.cloned.1.call-done = f32[1,128,2048]{2,1,0:T(8,128)} async-done(((f32[1,512,2048]{2,1,0:T(8,128)}), f32[1,128,2048]{2,1,0:T(8,128)}) %reduce-scatter.16.cloned.1.call-update) | async-done | bytes 1048592 | tf_op jit(solution)/shard_map/reduce_scatter | solution.py:75
  550.6 2.4 fusion.99
  553.3 44.4 %all-gather.29.cloned.1.call-done = bf16[1,512,2048]{2,1,0:T(8,128)(2,1)} async-done(((bf16[1,128,2048]{2,1,0:T(8,128)(2,1)}), bf16[1,512,2048]{2,1,0:T(8,128)(2,1)}) %all-gather.29.cloned.1.call-update) | async-done | bytes 2097168 | tf_op jit(solution)/shard_map/all_gather | solution.py:67
  597.7 3.5 fusion.60
  602.5 96.6 %while.29 = (s32[]{:T(128)}, f32[1,2048,1,128]{1,3,2,0:T(8,128)}, f32[8,1,512,64]{2,3,1,0:T(8,128)}, bf16[8,1,512,64]{3,2,1,0:T(8,128)(2,1)}, bf16[1,2048,1,128]...) while((s32[]{:T(128)}, f32[1,2048,1,128]{1,3,2,0:T(8,128)}, ...), condition=%wide.region_13.14_spmd.clone, body=%wide.region_11.13_spmd.clone.sunk | while | flops 682524160 | bytes 37902968 | solution.py:244
  604.3 2.4 multiply_reduce_fusion.5
  616.0 2.4 multiply_reduce_fusion.5
  618.9 2.2 fusion.149
  622.5 2.5 maximum_add_fusion.2
  628.1 2.4 multiply_reduce_fusion.5
  634.7 2.5 maximum_add_fusion.2
  640.3 2.4 multiply_reduce_fusion.5
  646.8 2.5 maximum_add_fusion.2
  652.4 2.4 multiply_reduce_fusion.5
  658.9 2.5 maximum_add_fusion.2
  664.5 2.4 multiply_reduce_fusion.5
  671.0 2.5 maximum_add_fusion.2
  676.6 2.4 multiply_reduce_fusion.5
  683.2 2.5 maximum_add_fusion.2
  688.8 2.4 multiply_reduce_fusion.5
  695.3 2.5 maximum_add_fusion.2
  699.3 9.5 convolution_bitcast_fusion.1
  710.8 3.2 fusion.102
  714.0 13.6 %reduce-scatter.18.cloned.1.call-done = f32[1,512,128]{1,2,0:T(8,128)} async-done(((f32[1,2048,128]{1,2,0:T(8,128)}), f32[1,512,128]{1,2,0:T(8,128)}) %reduce-scatter.18.cloned.1.call-update) | async-done | bytes 262160 | tf_op jit(solution)/shard_map/reduce_scatter | solution.py:247
  729.8 4.8 add_bitcast_fusion
  736.0 8.5 convolution_bitcast_fusion.2
  748.5 10.1 fusion.39
  758.6 10.5 fusion.37
  770.2 5.0 fusion.30
  775.6 3.4 fusion.47
  780.8 37.5 %reduce-scatter.32.cloned.1.call-done = f32[256,1408]{0,1:T(8,128)} async-done(((f32[2048,1408]{0,1:T(8,128)}), f32[256,1408]{0,1:T(8,128)}) %reduce-scatter.32.cloned.1.call-update) | async-done | bytes 1441808 | tf_op jit(solution)/shard_map/reduce_scatter | solution.py:291
  818.4 2.9 copy.52
  821.3 76.2 %reduce-scatter.20.cloned.1.call-done = f32[1,128,2048]{2,1,0:T(8,128)} async-done(((f32[1,512,2048]{2,1,0:T(8,128)}), f32[1,128,2048]{2,1,0:T(8,128)}) %reduce-scatter.20.cloned.1.call-update) | async-done | bytes 1048592 | tf_op jit(solution)/shard_map/reduce_scatter | solution.py:75
  899.0 27.3 %all-reduce.2 = (f32[2048]{0:T(1024)S(1)}, f32[2048]{0:T(1024)S(1)}) all-reduce(f32[2048]{0:T(1024)S(1)} %get-tuple-element.284, f32[2048]{0:T(1024)S(1)} %get-tuple-element.282), channel_id=8, replica_groups=mesh['shard'=2,'ctx'=4,'tensor'=4] {'shard','ctx'}, use_global_device_ids=true, to_apply=%region_18.19.clone | all-reduce | flops 4096 | bytes 32768
  926.5 8.7 all-reduce.3
  935.2 42.0 %reduce-scatter.14.cloned.1.call-done = f32[1,128,2048]{2,1,0:T(8,128)} async-done(((f32[1,512,2048]{2,1,0:T(8,128)}), f32[1,128,2048]{2,1,0:T(8,128)}) %reduce-scatter.14.cloned.1.call-update) | async-done | bytes 1048592 | tf_op jit(solution)/shard_map/reduce_scatter | solution.py:71
  977.2 3.2 fusion.70
  980.3 37.1 %reduce-scatter.24.cloned.1.call-done = f32[256,128]{1,0:T(8,128)} async-done(((f32[2048,128]{1,0:T(8,128)}), f32[256,128]{1,0:T(8,128)}) %reduce-scatter.24.cloned.1.call-update) | async-done | bytes 131088 | tf_op jit(solution)/shard_map/reduce_scatter | solution.py:282
  1017.5 91.3 %reduce-scatter.28.cloned.1.call-done = f32[256,1408]{1,0:T(8,128)} async-done(((f32[2048,1408]{1,0:T(8,128)}), f32[256,1408]{1,0:T(8,128)}) %reduce-scatter.28.cloned.1.call-update) | async-done | bytes 1441808 | tf_op jit(solution)/shard_map/reduce_scatter | solution.py:289
  1108.7 91.1 %reduce-scatter.30.cloned.1.call-done = f32[256,1408]{1,0:T(8,128)} async-done(((f32[2048,1408]{1,0:T(8,128)}), f32[256,1408]{1,0:T(8,128)}) %reduce-scatter.30.cloned.1.call-update) | async-done | bytes 1441808 | tf_op jit(solution)/shard_map/reduce_scatter | solution.py:290
  1199.8 55.7 %reduce-scatter.26.cloned.1.call-done = f32[256,512]{1,0:T(8,128)} async-done(((f32[2048,512]{1,0:T(8,128)}), f32[256,512]{1,0:T(8,128)}) %reduce-scatter.26.cloned.1.call-update) | async-done | bytes 524304 | tf_op jit(solution)/shard_map/reduce_scatter | solution.py:283
  1255.5 55.1 %reduce-scatter.22.cloned.1.call-done = f32[256,512]{1,0:T(8,128)} async-done(((f32[2048,512]{1,0:T(8,128)}), f32[256,512]{1,0:T(8,128)}) %reduce-scatter.22.cloned.1.call-update) | async-done | bytes 524304 | tf_op jit(solution)/shard_map/reduce_scatter | solution.py:281
  (228 shorter events, 119.0 us)
Async XLA Ops:
  7.2 63.2 %all-gather.13.cloned.1.call-start = ((), (), s32[]{:S(2)}) async-start(), calls=%async_computation.11 | async-start | bytes 2621440 | tf_op jit(solution)/shard_map/all_gather | solution.py:63
  22.1 1.3 copy-start.15
  23.3 0.5 copy-start.19
  25.9 75.3 %all-gather.15.cloned.1.call-start = ((), (), s32[]{:S(2)}) async-start(), calls=%async_computation.12 | async-start | bytes 2359296 | tf_op jit(solution)/shard_map/all_gather | solution.py:112
  26.7 112.5 %all-gather.17.cloned.1.call-start = ((), (), s32[]{:S(2)}) async-start(), calls=%async_computation.13 | async-start | bytes 2359296 | tf_op jit(solution)/shard_map/all_gather | solution.py:114
  27.4 193.4 %reduce-scatter.12.cloned.1.call-start = ((), (), s32[]{:S(2)}) async-start(), calls=%async_computation.14 | async-start | bytes 5242880 | tf_op jit(solution)/shard_map/reduce_scatter | solution.py:71
  27.5 54.2 %copy-start.21 = (f32[32]{0:T(128)}, f32[32]{0:T(128)S(1)}, u32[]{:S(2)}) copy-start(f32[32]{0:T(128)S(1)} %multiply_power_fusion) | copy-start | bytes 388
  28.4 53.4 %copy-start.17 = (f32[1,512]{1,0:T(1,128)}, f32[1,512]{1,0:T(1,128)S(1)}, u32[]{:S(2)}) copy-start(f32[1,512]{1,0:T(1,128)S(1)} %fusion.96) | copy-start | bytes 6148
  53.8 19.3 %copy-start.10 = (bf16[2048,128]{1,0:T(8,128)(2,1)}, bf16[2048,128]{1,0:T(8,128)(2,1)S(1)}, u32[]{:S(2)}) copy-start(bf16[2048,128]{1,0:T(8,128)(2,1)S(1)} %all_gather.50) | copy-start | bytes 1572868
  73.1 32.0 %copy-start = (bf16[1,512,2048]{2,1,0:T(8,128)(2,1)S(1)}, bf16[1,512,2048]{2,1,0:T(8,128)(2,1)}, u32[]{:S(2)}) copy-start(bf16[1,512,2048]{2,1,0:T(8,128)(2,1)} %all-gather.13.cloned.1.call-done) | copy-start | bytes 6291460
  108.0 1.6 copy-start.12
  139.1 5.1 copy-start.13
  144.2 0.7 copy-start.24
  144.2 76.6 %copy-start.4 = (bf16[1,128,2048]{2,1,0:T(8,128)(2,1)S(1)}, bf16[1,128,2048]{2,1,0:T(8,128)(2,1)}, u32[]{:S(2)}) copy-start(bf16[1,128,2048]{2,1,0:T(8,128)(2,1)} %param.15) | copy-start | bytes 1572868
  144.3 122.7 %all-gather.23.cloned.1.call-start = ((), (), s32[]{:S(2)}) async-start(), calls=%async_computation.17 | async-start | bytes 6488064 | tf_op jit(solution)/shard_map/all_gather | solution.py:119
  144.9 167.8 %all-gather.19.cloned.1.call-start = ((), (), s32[]{:S(2)}) async-start(), calls=%async_computation.15 | async-start | bytes 2621440 | tf_op jit(solution)/shard_map/all_gather | solution.py:63
  222.3 328.3 %copy-start.2 = (f32[1,128,2048]{2,1,0:T(8,128)}, f32[1,128,2048]{2,1,0:T(8,128)S(1)}, u32[]{:S(2)}) copy-start(f32[1,128,2048]{2,1,0:T(8,128)S(1)} %get-tuple-element.323) | copy-start | bytes 3145732
  223.4 135.7 %all-gather.21.cloned.1.call-start = ((), (), s32[]{:S(2)}) async-start(), calls=%async_computation.16 | async-start | bytes 6488064 | tf_op jit(solution)/shard_map/all_gather | solution.py:118
  224.2 180.3 %all-gather.27.cloned.1.call-start = ((), (), s32[]{:S(2)}) async-start(), calls=%async_computation.20 | async-start | bytes 2621440 | tf_op jit(solution)/shard_map/all_gather | solution.py:67
  224.9 225.9 %all-gather.25.cloned.1.call-start = ((), (), s32[]{:S(2)}) async-start(), calls=%async_computation.18 | async-start | bytes 6488064 | tf_op jit(solution)/shard_map/all_gather | solution.py:120
  225.6 323.3 %reduce-scatter.16.cloned.1.call-start = ((), (), s32[]{:S(2)}) async-start(), calls=%async_computation.21 | async-start | bytes 5242880 | tf_op jit(solution)/shard_map/reduce_scatter | solution.py:75
  450.8 10.4 copy-start.23
  461.3 3.5 copy-start.28
  461.3 3.5 copy-start.27
  472.4 78.2 %copy-start.8 = (bf16[1,128,2048]{2,1,0:T(8,128)(2,1)S(1)}, bf16[1,128,2048]{2,1,0:T(8,128)(2,1)}, u32[]{:S(2)}) copy-start(bf16[1,128,2048]{2,1,0:T(8,128)(2,1)} %param.16) | copy-start | bytes 1572868
  472.4 125.2 %all-gather.29.cloned.1.call-start = ((), (), s32[]{:S(2)}) async-start(), calls=%async_computation.22 | async-start | bytes 2621440 | tf_op jit(solution)/shard_map/all_gather | solution.py:67
  553.0 174.7 %reduce-scatter.18.cloned.1.call-start = ((), (), s32[]{:S(2)}) async-start(), calls=%async_computation.23 | async-start | bytes 1310720 | tf_op jit(solution)/shard_map/reduce_scatter | solution.py:247
  699.2 119.2 %reduce-scatter.32.cloned.1.call-start = ((), (), s32[]{:S(2)}) async-start(), calls=%async_computation.30 | async-start | bytes 12976128 | tf_op jit(solution)/shard_map/reduce_scatter | solution.py:291
  708.8 2.0 copy-start.7
  708.8 188.6 %reduce-scatter.20.cloned.1.call-start = ((), (), s32[]{:S(2)}) async-start(), calls=%async_computation.24 | async-start | bytes 5242880 | tf_op jit(solution)/shard_map/reduce_scatter | solution.py:75
  710.8 16.9 %copy-start.18 = (f32[1,512]{1,0:T(1,128)S(1)}, f32[1,512]{1,0:T(1,128)}, u32[]{:S(2)}) copy-start(f32[1,512]{1,0:T(1,128)} %copy-done.17) | copy-start | bytes 6148
  710.8 16.9 %copy-start.22 = (f32[32]{0:T(128)S(1)}, f32[32]{0:T(128)}, u32[]{:S(2)}) copy-start(f32[32]{0:T(128)} %copy-done.21) | copy-start | bytes 388
  710.8 19.0 %copy-start.11 = (bf16[2048,128]{1,0:T(8,128)(2,1)S(1)}, bf16[2048,128]{1,0:T(8,128)(2,1)}, u32[]{:S(2)}) copy-start(bf16[2048,128]{1,0:T(8,128)(2,1)} %copy-done.10) | copy-start | bytes 1572868
  734.6 1.4 copy-start.26
  734.6 242.5 %reduce-scatter.14.cloned.1.call-start = ((), (), s32[]{:S(2)}) async-start(), calls=%async_computation.19 | async-start | bytes 5242880 | tf_op jit(solution)/shard_map/reduce_scatter | solution.py:71
  744.5 2.2 copy-start.1
  744.5 272.9 %reduce-scatter.24.cloned.1.call-start = ((), (), s32[]{:S(2)}) async-start(), calls=%async_computation.26 | async-start | bytes 1179648 | tf_op jit(solution)/shard_map/reduce_scatter | solution.py:282
  748.4 360.3 %reduce-scatter.28.cloned.1.call-start = ((), (), s32[]{:S(2)}) async-start(), calls=%async_computation.28 | async-start | bytes 12976128 | tf_op jit(solution)/shard_map/reduce_scatter | solution.py:289
  758.6 441.3 %reduce-scatter.30.cloned.1.call-start = ((), (), s32[]{:S(2)}) async-start(), calls=%async_computation.29 | async-start | bytes 12976128 | tf_op jit(solution)/shard_map/reduce_scatter | solution.py:290
  769.1 1.0 copy-start.14
  769.1 486.4 %reduce-scatter.26.cloned.1.call-start = ((), (), s32[]{:S(2)}) async-start(), calls=%async_computation.27 | async-start | bytes 4718592 | tf_op jit(solution)/shard_map/reduce_scatter | solution.py:283
  775.2 535.4 %reduce-scatter.22.cloned.1.call-start = ((), (), s32[]{:S(2)}) async-start(), calls=%async_computation.25 | async-start | bytes 4718592 | tf_op jit(solution)/shard_map/reduce_scatter | solution.py:281
  779.0 0.7 copy-start.25
  779.0 118.5 %copy-start.5 = (bf16[1,128,2048]{2,1,0:T(8,128)(2,1)S(1)}, bf16[1,128,2048]{2,1,0:T(8,128)(2,1)}, u32[]{:S(2)}) copy-start(bf16[1,128,2048]{2,1,0:T(8,128)(2,1)} %param.15) | copy-start | bytes 1572868
  779.0 118.5 %copy-start.16 = (f32[8,1,256]{2,1,0:T(1,128)S(1)}, f32[8,1,256]{2,1,0:T(1,128)}, u32[]{:S(2)}) copy-start(f32[8,1,256]{2,1,0:T(1,128)} %copy-done.15) | copy-start | bytes 24580
  779.0 118.5 %copy-start.20 = (f32[128]{0:T(128)S(1)}, f32[128]{0:T(128)}, u32[]{:S(2)}) copy-start(f32[128]{0:T(128)} %copy-done.19) | copy-start | bytes 1540
  779.0 198.2 %copy-start.3 = (f32[1,128,2048]{2,1,0:T(8,128)S(1)}, f32[1,128,2048]{2,1,0:T(8,128)}, u32[]{:S(2)}) copy-start(f32[1,128,2048]{2,1,0:T(8,128)} %copy-done.2) | copy-start | bytes 3145732
  779.0 198.2 %copy-start.6 = (f32[1,128,2048]{2,1,0:T(8,128)S(1)}, f32[1,128,2048]{2,1,0:T(8,128)}, u32[]{:S(2)}) copy-start(f32[1,128,2048]{2,1,0:T(8,128)} %reduce-scatter.16.cloned.1.call-done) | copy-start | bytes 3145732
  779.0 198.2 %copy-start.9 = (bf16[1,128,2048]{2,1,0:T(8,128)(2,1)S(1)}, bf16[1,128,2048]{2,1,0:T(8,128)(2,1)}, u32[]{:S(2)}) copy-start(bf16[1,128,2048]{2,1,0:T(8,128)(2,1)} %param.16) | copy-start | bytes 1572868
Sparse Core Ops, SparseCore 0:
  26.0 44.2 all-gather.12
  72.2 28.8 all-gather.14
  103.1 27.8 all-gather.16
  144.4 76.3 reduce-scatter.11
  222.7 44.2 all-gather.22
  269.0 43.6 all-gather.18
  314.7 44.3 all-gather.20
  360.7 43.6 all-gather.26
  406.5 44.3 all-gather.24
  472.6 76.3 reduce-scatter.15
  553.1 44.5 all-gather.28
  699.3 28.2 reduce-scatter.17
  731.5 86.7 reduce-scatter.31
  820.6 76.7 reduce-scatter.19
  899.6 77.5 reduce-scatter.13
  981.1 36.3 reduce-scatter.23
  1021.8 86.8 reduce-scatter.27
  1113.0 86.7 reduce-scatter.29
  1204.1 51.3 reduce-scatter.25
  1259.3 51.2 reduce-scatter.21
where the time goes:
time: 1330 us; the launch traced here: 1320 us
  waiting for transfers between devices  931 us (70%)
  matrix products  206 us (15%)
  blocking collectives  97.6 us (7%)
  other arithmetic  47.6 us (4%)
  local copies, waits for them, and re-layouts  18 us (1%)
  between operations  15.9 us (1%)
    reduce_scatter x2, waiting for transfers between devices, input_sum(): lax.psum_scatter(partial_sum, 'tensor', scatter_dimension=1, tiled=True)  153 us
    reduce_scatter x2, waiting for transfers between devices, branch_sum(): lax.psum_scatter(partial_sum, 'tensor', scatter_dimension=1, tiled=True)  104 us
    reduce_scatter x1, waiting for transfers between devices, body(): lax.psum_scatter(grad_gate_w, ('shard', 'ctx'), scatter_dimension=0, tile...  91.3 us
    reduce_scatter x1, waiting for transfers between devices, body(): lax.psum_scatter(grad_up_w, ('shard', 'ctx'), scatter_dimension=0, tiled=...  91.1 us
    all_gather x2, waiting for transfers between devices, spread_grads(): return lax.all_gather(values_in, 'tensor', axis=1, tiled=True)  81.5 us
    all_gather x2, waiting for transfers between devices, broadcast_rows(): return lax.all_gather(values_in, 'tensor', axis=1, tiled=True)  62 us
    reduce_scatter x1, waiting for transfers between devices, body(): lax.psum_scatter(grad_output_w, ('shard', 'ctx'), scatter_dimension=0, ti...  55.7 us
    reduce_scatter x1, waiting for transfers between devices, body(): lax.psum_scatter(grad_query_w, ('shard', 'ctx'), scatter_dimension=0, til...  55.1 us
  transfers between devices with their start and end apart: 20, of which 19 were waited for; matrix products, arithmetic and copies ran while one was open for 10% of the time, Pallas kernels for 0%

commit v1 on v0

v1 whole, which is shorter than its diff:
```python
import functools

import jax
import jax.numpy as jnp
import numpy as np
from jax import lax
from jax.experimental import pallas as pl
from jax.experimental.pallas import tpu as pltpu
from jax.sharding import PartitionSpec as P

HD = 64
BLOCK = 256
BLOCKS = 8
ROWS = 16
CTX = 4
LINE = 4

epsilon = 1e-05
blocked = -1e30

f32 = jnp.float32
bf16 = jnp.bfloat16
MESH = pl.DeviceIdType.MESH


def nn_dot(left, right):
    return jnp.dot(left, right, preferred_element_type=f32)


def nt_dot(left, right):
    return lax.dot_general(left, right, (((1,), (1,)), ((), ())), preferred_element_type=f32)


def tn_dot(left, right):
    return lax.dot_general(left, right, (((0,), (0,)), ((), ())), preferred_element_type=f32)


class Links:
    def __init__(self, shards, send_sems, recv_sems, local_sems):
        self.shards = shards
        self.send_sems, self.recv_sems, self.local_sems = send_sems, recv_sems, local_sems
        self.s = lax.axis_index("shard")
        self.c = lax.axis_index("ctx")
        self.t = lax.axis_index("tensor")
        self.c_x = self.c + 1 - 2 * lax.rem(self.c, 2)
        self.c_y = lax.rem(self.c + 2, CTX)
        self.c_d = CTX - 1 - self.c
        self.x_dev = (self.s, self.c_x, self.t)
        self.y_dev = (self.s, self.c_y, self.t)
        self.right = (self.s, self.c, self.t + 1)
        self.left = (self.s, self.c, self.t - 1)
        self.used = 0
        self.local_used = 0
        self.sends = []
        self.locals = []

    def slots(self, count):
        first = self.used
        self.used += count
        assert self.used <= self.send_sems.shape[0]
        return first

    def plane_peer(self, step):
        index = lax.rem(self.s * CTX + self.c + step, self.shards * CTX)
        return (index // CTX, lax.rem(index, CTX), self.t)

    def core_peer(self, step):
        return (lax.rem(self.s + step, self.shards), self.c, self.t)

    def barrier(self):
        sem = pltpu.get_barrier_semaphore()
        count = self.shards * CTX - 1
        for step in range(1, count + 1):
            pl.semaphore_signal(
                sem, inc=1, device_id=self.plane_peer(step), device_id_type=MESH
            )

        @pl.when(self.t > 0)
        def _():
            pl.semaphore_signal(sem, inc=1, device_id=self.left, device_id_type=MESH)

        @pl.when(self.t < LINE - 1)
        def _():
            pl.semaphore_signal(sem, inc=1, device_id=self.right, device_id_type=MESH)

        beside = (self.t + LINE - 1) // LINE + (2 * LINE - 2 - self.t) // LINE
        pl.semaphore_wait(sem, count + beside)

    def copy(self, src, dst, device, slot):
        return pltpu.make_async_remote_copy(
            src_ref=src,
            dst_ref=dst,
            send_sem=self.send_sems.at[slot],
            recv_sem=self.recv_sems.at[slot],
            device_id=device,
            device_id_type=MESH,
        )

    def send(self, src, dst, device, slot, cond=None):
        if cond is None:
            self.copy(src, dst, device, slot).start()
        else:

            @pl.when(cond)
            def _():
                self.copy(src, dst, device, slot).start()

        self.sends.append((src, dst, device, slot, cond))

    def recv(self, dst, slot):
        self.copy(dst, dst, self.x_dev, slot).wait_recv()

    def keep(self, src, dst):
        copy = pltpu.make_async_copy(src, dst, self.local_sems.at[self.local_used])
        self.local_used += 1
        assert self.local_used <= self.local_sems.shape[0]
        copy.start()
        return copy

    def keep_later(self, src, dst):
        self.locals.append(self.keep(src, dst))

    def finish(self):
        for src, dst, device, slot, cond in self.sends:
            if cond is None:
                self.copy(src, dst, device, slot).wait_send()
            else:

                @pl.when(cond)
                def _():
                    self.copy(src, dst, device, slot).wait_send()

        for copy in self.locals:
            copy.wait()


class PlaneGather:
    def __init__(self, links, src, full):
        self.links, self.src, self.full = links, src, full
        self.rows = src.shape[0]
        self.first = links.slots(4 + 4 * (links.shards - 1))

    def block(self, s, c):
        start = pl.multiple_of((s * CTX + c) * self.rows, self.rows)
        return self.full.at[pl.ds(start, self.rows)]

    def half(self, s, c, which):
        size = self.rows // 2
        start = pl.multiple_of((s * CTX + c) * self.rows + which * size, size)
        return self.full.at[pl.ds(start, size)]

    def core_slot(self, step, part):
        return self.first + 4 + (step - 1) * 4 + part

    def core_send(self, src, c, part):
        links = self.links
        for step in range(1, links.shards):
            links.send(
                src,
                self.block(links.s, c),
                links.core_peer(step),
                self.core_slot(step, part),
            )

    def start(self):
        links = self.links
        own = self.block(links.s, links.c)
        links.send(self.src, own, links.x_dev, self.first)
        links.send(self.src, own, links.y_dev, self.first + 1)
        self.core_send(self.src, links.c, 0)
        self.local = links.keep(self.src, own)

    def forward(self):
        links = self.links
        links.recv(self.block(links.s, links.c_x), self.first)
        links.recv(self.block(links.s, links.c_y), self.first + 1)
        from_x = self.half(links.s, links.c_x, 0)
        from_y = self.half(links.s, links.c_y, 1)
        links.send(from_x, from_x, links.y_dev, self.first + 2)
        links.send(from_y, from_y, links.x_dev, self.first + 3)
        self.core_send(self.block(links.s, links.c_x), links.c_x, 1)
        self.core_send(self.block(links.s, links.c_y), links.c_y, 2)

    def diagonal(self):
        links = self.links
        links.recv(self.half(links.s, links.c_d, 0), self.first + 2)
        links.recv(self.half(links.s, links.c_d, 1), self.first + 3)
        self.core_send(self.block(links.s, links.c_d), links.c_d, 3)

    def done(self):
        links = self.links
        for step in range(1, links.shards):
            other = lax.rem(links.s + links.shards - step, links.shards)
            for part, c in enumerate((links.c, links.c_x, links.c_y, links.c_d)):
                links.recv(self.block(other, c), self.core_slot(step, part))
        self.local.wait()


class LineGather:
    def __init__(self, links, own, full, tokens):
        self.links, self.own, self.full, self.tokens = links, own, full, tokens
        self.first = links.slots(2 * (LINE - 1))

    def block(self, owner):
        return self.full.at[pl.ds(pl.multiple_of(owner * self.tokens, self.tokens), self.tokens)]

    def send(self, k):
        links = self.links
        t, u = links.t, LINE - 1 - links.t
        right, left = self.block(t - k + 1), self.block(t + k - 1)
        links.send(
            self.own if k == 1 else right,
            right,
            links.right,
            self.first + k - 1,
            jnp.logical_and(t >= k - 1, t < LINE - 1),
        )
        links.send(
            self.own if k == 1 else left,
            left,
            links.left,
            self.first + LINE - 1 + k - 1,
            jnp.logical_and(u >= k - 1, u < LINE - 1),
        )

    def recv(self, k, use=None):
        links = self.links
        t, u = links.t, LINE - 1 - links.t

        @pl.when(t >= k)
        def _():
            links.recv(self.block(t - k), self.first + k - 1)

        @pl.when(u >= k)
        def _():
            links.recv(self.block(t + k), self.first + LINE - 1 + k - 1)

        if use is not None:

            @pl.when(t >= k)
            def _():
                use(t - k)

            @pl.when(u >= k)
            def _():
                use(t + k)


class LineScatter:
    def __init__(self, links, part, tokens, to_right, to_left, from_left, from_right):
        self.links, self.part, self.tokens = links, part, tokens
        self.to_right, self.to_left = to_right, to_left
        self.from_left, self.from_right = from_left, from_right
        self.first = links.slots(2 * (LINE - 1))

    def clear(self):
        for cond, ref in (
            (self.links.t == 0, self.from_left),
            (self.links.t == LINE - 1, self.from_right),
        ):

            @pl.when(cond)
            def _():
                @pl.loop(0, self.tokens // ROWS)
                def _(i):
                    r = pl.multiple_of(i * ROWS, ROWS)
                    for k in range(LINE - 1):
                        ref[k, pl.ds(r, ROWS), :] = jnp.zeros((ROWS, ref.shape[2]), ref.dtype)

    def total(self, owner, k, out, arrived):
        @pl.loop(0, self.tokens // ROWS)
        def _(i):
            r = pl.multiple_of(i * ROWS, ROWS)
            q = pl.multiple_of(owner * self.tokens + i * ROWS, ROWS)
            summed = self.part[pl.ds(q, ROWS), :].astype(f32) + arrived[
                k, pl.ds(r, ROWS), :
            ].astype(f32)
            out[k, pl.ds(r, ROWS), :] = summed.astype(out.dtype)

    def step(self, k):
        links = self.links
        t = links.t
        slot_r, slot_l = self.first + k, self.first + LINE - 1 + k
        owner_r, owner_l = LINE - 1 - k, k

        @pl.when(t < owner_r)
        def _():
            @pl.when(t > 0)
            def _():
                links.recv(self.from_left.at[k], slot_r)

            self.total(owner_r, k, self.to_right, self.from_left)

        links.send(self.to_right.at[k], self.from_left.at[k], links.right, slot_r, t < owner_r)

        @pl.when(t > owner_l)
        def _():
            @pl.when(t < LINE - 1)
            def _():
                links.recv(self.from_right.at[k], slot_l)

            self.total(owner_l, k, self.to_left, self.from_right)

        links.send(self.to_left.at[k], self.from_right.at[k], links.left, slot_l, t > owner_l)

    def arrive(self):
        links = self.links
        t = links.t

        @pl.when(t > 0)
        def _():
            links.recv(self.from_left.at[LINE - 1 - t], self.first + LINE - 1 - t)

        @pl.when(t < LINE - 1)
        def _():
            links.recv(self.from_right.at[t], self.first + LINE - 1 + t)

    def rows(self, i):
        t = self.links.t
        r = pl.multiple_of(i * ROWS, ROWS)
        q = pl.multiple_of(t * self.tokens + i * ROWS, ROWS)
        k_l = jnp.minimum(LINE - 1 - t, LINE - 2)
        k_r = jnp.minimum(t, LINE - 2)
        return (
            self.part[pl.ds(q, ROWS), :].astype(f32)
            + self.from_left[k_l, pl.ds(r, ROWS), :].astype(f32)
            + self.from_right[k_r, pl.ds(r, ROWS), :].astype(f32)
        )


def any_spec():
    return pl.BlockSpec(memory_space=pl.ANY)


def vmem_spec():
    return pl.BlockSpec(memory_space=pltpu.VMEM)


def struct(shape, dtype):
    return jax.ShapeDtypeStruct(shape, dtype)


def forward_kernel(
    shards,
    x, og, wq, wkv, wo, wg, wu, wd, gpad, cos, sin, bias,
    wq_o, wkv_o, wo_o, wg_o, wu_o, wd_o, n1_o, og_o, n2_o, mid_o, qaug_o, kaug_o, kv_o, att_o,
    lse, gains,
    x_all, n1_all, wq_all, wkv_all, wo_all, gains_all, qaug, kv_all, kaug, v_all, scores, weights,
    attn, part, to_right, to_left, from_left, from_right, mid, n2,
    send_sems, recv_sems, local_sems,
):
    tokens, width = x.shape
    queries = tokens * LINE
    heads = qaug.shape[0]
    links = Links(shards, send_sems, recv_sems, local_sems)
    s, c, t = links.s, links.c, links.t

    gather_x = LineGather(links, x, x_all, tokens)
    gather_og = LineGather(links, og, og_o, tokens)
    gather_n2 = LineGather(links, n2, n2_o, tokens)
    small = [PlaneGather(links, *pair) for pair in ((wq, wq_all), (wkv, wkv_all), (wo, wo_all))]
    large = [PlaneGather(links, *pair) for pair in ((wg, wg_o), (wu, wu_o), (wd, wd_o))]
    scatter = LineScatter(
        links, part, tokens, to_right, to_left, from_left, from_right
    )
    plane = shards * CTX
    gain_slot = links.slots(plane - 1)
    kv_slot = links.slots(3)

    links.barrier()
    me = s * CTX + c
    for step in range(1, plane):
        links.send(gpad, gains_all.at[me], links.plane_peer(step), gain_slot + step - 1)
    own_gain = links.keep(gpad, gains_all.at[me])
    gather_x.send(1)
    own_x = links.keep(x, x_all.at[pl.ds(pl.multiple_of(t * tokens, tokens), tokens)])
    for gather in small:
        gather.start()
    scatter.clear()
    own_gain.wait()
    for step in range(1, plane):
        other = lax.rem(me + plane - step, plane)
        links.recv(gains_all.at[other], gain_slot + step - 1)
    total = gains_all[0]
    for index in range(1, plane):
        total = total + gains_all[index]
    gains[...] = total
    own_x.wait()

    def norm_block(owner):
        @pl.loop(0, tokens // ROWS)
        def _(i):
            r = pl.multiple_of(owner * tokens + i * ROWS, ROWS)
            v = x_all[pl.ds(r, ROWS), :].astype(f32)
            inverse = lax.rsqrt(jnp.mean(v * v, -1, keepdims=True) + epsilon)
            n1_all[pl.ds(r, ROWS), :] = (v * inverse * gains[0:1, :]).astype(bf16)

    norm_block(t)
    gather_x.recv(1)
    gather_x.send(2)
    for gather in small:
        gather.forward()
    norm_pair(gather_x, norm_block, 1)
    large[0].start()
    gather_x.recv(2)
    gather_x.send(3)
    for gather in small:
        gather.diagonal()
    norm_pair(gather_x, norm_block, 2)
    large[1].start()
    large[2].start()
    gather_x.recv(3)
    gather_og.send(1)
    own_og = links.keep(og, og_o.at[pl.ds(pl.multiple_of(t * tokens, tokens), tokens)])
    norm_pair(gather_x, norm_block, 3)
    for gather in small:
        gather.done()

    kv_t = nn_dot(n1_all[...], wkv_all[...]).T
    half = HD // 2
    cosine, sine = cos[...], sin[...]
    k1, k2 = kv_t[0:half], kv_t[half:HD]
    kv_all[c, 0:half, :] = (k1 * cosine - k2 * sine).astype(bf16)
    kv_all[c, half:HD, :] = (k2 * cosine + k1 * sine).astype(bf16)
    kv_all[c, HD : 2 * HD, :] = kv_t[HD:].astype(bf16)
    for step in range(1, CTX):
        peer = lax.rem(c + step, CTX)
        links.send(kv_all.at[c], kv_all.at[c], (s, peer, t), kv_slot + step - 1)

    q_t = nn_dot(n1_all[...], wq_all[...]).T
    scale = HD ** (-0.5)
    for h in range(heads):
        v1, v2 = q_t[h * HD : h * HD + half], q_t[h * HD + half : (h + 1) * HD]
        qaug[h, 0:half, :] = ((v1 * cosine - v2 * sine).astype(bf16) * scale).astype(bf16)
        qaug[h, half:HD, :] = ((v2 * cosine + v1 * sine).astype(bf16) * scale).astype(bf16)
        qaug[h, HD:, :] = bias[...]
    links.keep_later(n1_all, n1_o)
    links.keep_later(wq_all, wq_o)
    links.keep_later(wkv_all, wkv_o)
    links.keep_later(wo_all, wo_o)
    links.keep_later(qaug, qaug_o)
    for step in range(1, CTX):
        other = lax.rem(c + CTX - step, CTX)
        links.recv(kv_all.at[other], kv_slot + step - 1)
    for other in range(CTX):
        row = lax.broadcasted_iota(jnp.int32, (HD, queries), 0)
        lane = lax.broadcasted_iota(jnp.int32, (HD, queries), 1)
        mark = (row == other * (queries // BLOCK) + lane // BLOCK).astype(f32).astype(bf16)
        both = jnp.concatenate([kv_all[other, 0:HD, :], mark], 0)
        kaug[other * queries : (other + 1) * queries, :] = both.T
        v_all[:, other * queries : (other + 1) * queries] = kv_all[other, HD : 2 * HD, :]
    links.keep_later(kaug, kaug_o)
    links.keep_later(kv_all, kv_o)

    length = queries * CTX

    def head(h):
        query = qaug[h]
        top = jnp.full((1, queries), -jnp.inf, f32)
        for b in range(0, length, BLOCK):
            block_scores = nn_dot(kaug[b : b + BLOCK, :], query)
            scores[b : b + BLOCK, :] = block_scores
            top = jnp.maximum(top, jnp.max(block_scores, 0, keepdims=True))
        norm = jnp.zeros((1, queries), f32)
        for b in range(0, length, BLOCK):
            exponent = jnp.exp(scores[b : b + BLOCK, :] - top)
            norm = norm + jnp.sum(exponent, 0, keepdims=True)
            weights[b : b + BLOCK, :] = exponent.astype(bf16)
        out = nn_dot(v_all[...], weights[...]) / norm
        attn[pl.ds(pl.multiple_of(h * HD, HD), HD), :] = out.astype(bf16)
        lse[pl.ds(h, 1), :] = top + jnp.log(norm)

    pl.loop(0, heads // 2)(head)
    gather_og.recv(1)
    gather_og.send(2)
    pl.loop(heads // 2, heads)(head)
    links.keep_later(attn, att_o)

    attn_rows = attn[...].T
    for b in range(0, width, 512):
        part[:, b : b + 512] = nt_dot(attn_rows, wo_all[b : b + 512, :])
    scatter.step(0)
    gather_og.recv(2)
    gather_og.send(3)
    for gather in large:
        gather.forward()
    scatter.step(1)
    scatter.step(2)
    for gather in large:
        gather.diagonal()
    scatter.arrive()

    @pl.loop(0, tokens // ROWS)
    def _(i):
        r = pl.multiple_of(i * ROWS, ROWS)
        q = pl.multiple_of(t * tokens + i * ROWS, ROWS)
        middle = x_all[pl.ds(q, ROWS), :].astype(f32) + scatter.rows(i)
        mid[pl.ds(r, ROWS), :] = middle
        inverse = lax.rsqrt(jnp.mean(middle * middle, -1, keepdims=True) + epsilon)
        n2[pl.ds(r, ROWS), :] = (middle * inverse * gains[1:2, :]).astype(bf16)

    gather_n2.send(1)
    links.keep_later(n2, n2_o.at[pl.ds(pl.multiple_of(t * tokens, tokens), tokens)])
    links.keep_later(mid, mid_o)
    gather_og.recv(3)
    own_og.wait()
    gather_n2.recv(1)
    gather_n2.send(2)
    for gather in large:
        gather.done()
    gather_n2.recv(2)
    gather_n2.send(3)
    gather_n2.recv(3)
    links.finish()


def norm_pair(gather, norm_block, k):
    t, u = gather.links.t, LINE - 1 - gather.links.t

    @pl.when(t >= k)
    def _():
        norm_block(t - k)

    @pl.when(u >= k)
    def _():
        norm_block(t + k)


def forward_call(shards, x, og, weights_in, gpad, cos, sin, bias):
    wq, wkv, wo, wg, wu, wd = weights_in
    tokens, width = x.shape
    queries = tokens * LINE
    length = queries * CTX
    heads = wq.shape[1] // HD
    plane = shards * CTX
    full = [struct((width, w.shape[1]), bf16) for w in weights_in]
    outs = full + [
        struct((queries, width), bf16),
        struct((queries, width), bf16),
        struct((queries, width), bf16),
        struct((tokens, width), f32),
        struct((heads, 2 * HD, queries), bf16),
        struct((length, 2 * HD), bf16),
        struct((CTX, 2 * HD, queries), bf16),
        struct((heads * HD, queries), bf16),
        struct((heads, queries), f32),
        struct((2, width), f32),
    ]
    block = (LINE - 1, tokens, width)
    count = 3 * 6 + 6 * (4 + 4 * (shards - 1)) + 6 + plane - 1 + 3
    return pl.pallas_call(
        functools.partial(forward_kernel, shards),
        out_shape=outs,
        in_specs=[any_spec()] * 8 + [vmem_spec()] * 4,
        out_specs=[any_spec()] * 14 + [vmem_spec()] * 2,
        scratch_shapes=[
            pltpu.VMEM((queries, width), bf16),
            pltpu.VMEM((queries, width), bf16),
            pltpu.VMEM((width, wq.shape[1]), bf16),
            pltpu.VMEM((width, wkv.shape[1]), bf16),
            pltpu.VMEM((width, wo.shape[1]), bf16),
            pltpu.VMEM((plane, 2, width), f32),
            pltpu.VMEM((heads, 2 * HD, queries), bf16),
            pltpu.VMEM((CTX, 2 * HD, queries), bf16),
            pltpu.VMEM((length, 2 * HD), bf16),
            pltpu.VMEM((HD, length), bf16),
            pltpu.VMEM((length, queries), f32),
            pltpu.VMEM((length, queries), bf16),
            pltpu.VMEM((heads * HD, queries), bf16),
            pltpu.VMEM((queries, width), f32),
            pltpu.VMEM(block, bf16),
            pltpu.VMEM(block, bf16),
            pltpu.VMEM(block, bf16),
            pltpu.VMEM(block, bf16),
            pltpu.VMEM((tokens, width), f32),
            pltpu.VMEM((tokens, width), bf16),
            pltpu.SemaphoreType.DMA((count,)),
            pltpu.SemaphoreType.DMA((count,)),
            pltpu.SemaphoreType.DMA((32,)),
        ],
        compiler_params=pltpu.CompilerParams(
            collective_id=0, has_side_effects=True, vmem_limit_bytes=60 * 2**20
        ),
        name="forward",
    )(x, og, wq, wkv, wo, wg, wu, wd, gpad, cos, sin, bias)


def norm_backward_pass(normed_gradient, unit_rows, inverse_root_mean, norm_scale):
    unit_rows_gradient = normed_gradient * norm_scale
    scale_gradient = jnp.sum(normed_gradient * unit_rows, axis=0)
    value_gradients = inverse_root_mean * (
        unit_rows_gradient - unit_rows * jnp.mean(unit_rows_gradient * unit_rows, -1, keepdims=True)
    )
    return (scale_gradient, value_gradients)


def apply_norm(values_in):
    inverse_root_mean = lax.rsqrt(jnp.mean(values_in * values_in, -1, keepdims=True) + epsilon)
    return (values_in * inverse_root_mean, inverse_root_mean)


def body(
    inputs, out_grad, block_order, gain_attn, w_query, w_keyval, w_output, gain_mlp, w_gate, w_up, w_down
):
    shards = lax.axis_size("shard")
    x, og = inputs[0], out_grad[0]
    tokens, width = x.shape
    queries = tokens * LINE
    order = block_order[0]
    s, c = lax.axis_index("shard"), lax.axis_index("ctx")
    per = queries // BLOCK
    here = lax.dynamic_slice_in_dim(order, c * per, per)
    block_here = jnp.repeat(here, BLOCK)
    position = block_here * BLOCK + jnp.tile(jnp.arange(BLOCK, dtype=jnp.int32), per)
    half = HD // 2
    frequency = 10000.0 ** (-jnp.arange(half, dtype=f32) * 2.0 / HD)
    angles = frequency[:, None] * position.astype(f32)[None, :]
    cos, sin = jnp.cos(angles), jnp.sin(angles)
    bias = jnp.where(order[:, None] <= block_here[None, :], 0.0, blocked).astype(bf16)
    bias = jnp.concatenate([bias, jnp.zeros((HD - BLOCKS, queries), bf16)], 0)
    start = (s * CTX + c) * gain_attn.shape[0]
    gpad = lax.dynamic_update_slice(
        jnp.zeros((2, width), f32), jnp.stack([gain_attn, gain_mlp]).astype(f32), (0, start)
    )
    (wq, wkv, wo, wg, wu, wd, n1, og_all, n2, mid, qaug, kaug, kv, att, lse, gains) = forward_call(
        shards, x, og, (w_query, w_keyval, w_output, w_gate, w_up, w_down), gpad, cos, sin, bias
    )
    rs = lambda v: lax.psum_scatter(v, "tensor", scatter_dimension=0, tiled=True)
    ws = lambda v: lax.psum_scatter(
        v.astype(bf16), ("shard", "ctx"), scatter_dimension=0, tiled=True
    ).astype(f32)
    gate = nn_dot(n2, wg)
    up = nn_dot(n2, wu)
    sg = jax.nn.sigmoid(gate)
    silu = gate * sg
    hidden = (silu * up).astype(bf16)
    layer_out = (mid + rs(nt_dot(hidden, wd).astype(bf16)).astype(f32)).astype(bf16)
    dh = nn_dot(og_all, wd)
    grad_down = ws(tn_dot(og_all, hidden))
    dgate = (dh * up * sg * (1.0 + gate * (1.0 - sg))).astype(bf16)
    dup = (dh * silu).astype(bf16)
    grad_gate = ws(tn_dot(n2, dgate))
    grad_up = ws(tn_dot(n2, dup))
    dn2 = rs((nt_dot(dgate, wg) + nt_dot(dup, wu)).astype(bf16)).astype(f32)
    unit2, inv2 = apply_norm(mid)
    gm, dmid = norm_backward_pass(dn2, unit2, inv2, gains[1:2])
    dmid = dmid + og.astype(f32)
    dmid_all = lax.all_gather(dmid.astype(bf16), "tensor", axis=0, tiled=True)
    datt = nn_dot(dmid_all, wo).astype(bf16)
    grad_output = ws(nt_dot(dmid_all.T, att))
    heads = wq.shape[1] // HD
    datt_t = datt.T.reshape(heads, HD, queries)
    att_t = att.reshape(heads, HD, queries)
    k_all = kaug[:, :HD]
    v_all = jnp.moveaxis(kv[:, HD:], 1, 2).reshape(-1, HD)

    def back(acc, ops):
        q, do, o, l = ops
        p = jnp.exp(nn_dot(kaug, q) - l[None, :])
        dp = nn_dot(v_all, do)
        delta = jnp.sum(do.astype(f32) * o.astype(f32), 0, keepdims=True)
        ds = (p * (dp - delta)).astype(bf16)
        dq = tn_dot(k_all, ds) * (HD ** (-0.5))
        dk = nt_dot(ds, q[:HD])
        dv = nt_dot(p.astype(bf16), do)
        return (acc + jnp.concatenate([dk, dv], 1), dq)

    dkv, dq = lax.scan(back, jnp.zeros((k_all.shape[0], 2 * HD), f32), (qaug, datt_t, att_t, lse))
    dkv = lax.psum_scatter(dkv, "ctx", scatter_dimension=0, tiled=True)

    def unrotate(v):
        v1, v2 = v[..., :half, :], v[..., half:, :]
        return jnp.concatenate([v1 * cos + v2 * sin, v2 * cos - v1 * sin], -2)

    dkv_t = dkv.T
    dkv_raw = jnp.concatenate([unrotate(dkv_t[:HD]), dkv_t[HD:]], 0).astype(bf16).T
    dq_raw = unrotate(dq).astype(bf16).reshape(heads * HD, queries).T
    grad_query = ws(tn_dot(n1, dq_raw))
    grad_keyval = ws(tn_dot(n1, dkv_raw))
    dn1 = rs((nt_dot(dq_raw, wq) + nt_dot(dkv_raw, wkv)).astype(bf16)).astype(f32)
    unit1, inv1 = apply_norm(x.astype(f32))
    ga, dres = norm_backward_pass(dn1, unit1, inv1, gains[0:1])
    input_grad = dmid + dres
    both = lax.psum(jnp.stack([ga, gm]), ("shard", "ctx", "tensor"))
    both = lax.dynamic_slice(both, (0, start), (2, gain_attn.shape[0]))
    return (
        layer_out[None], input_grad[None], both[0], grad_query, grad_keyval, grad_output,
        both[1], grad_gate, grad_up, grad_down,
    )


def solution(mesh):
    plane = P(("shard", "ctx"), "tensor")
    gain = P(("shard", "ctx"))
    token = P("shard", ("ctx", "tensor"), None)
    return jax.shard_map(
        body,
        mesh=mesh,
        in_specs=(token, token, P("shard", None), gain, plane, plane, plane, gain, plane, plane, plane),
        out_specs=(token, token, gain, plane, plane, plane, gain, plane, plane, plane),
        check_vma=False,
    )
```

time: 1330 us -> 871 us (0.65)
  waiting for transfers between devices: 931 us -> 412 us
  Pallas kernels: 0 us -> 179 us
  matrix products: 206 us -> 141 us
  blocking collectives: 97.6 us -> 45 us
    reduce_scatter x11 -> x10, waiting for transfers between devices: 638 us -> 367 us  [the longest x6 276 us: body(): lax.psum_scatter(v.astype(bf16), ('shard', 'ctx'), scatter_dimension=0, t...]
    all_gather x9 -> x1, waiting for transfers between devices: 289 us -> 45.3 us  [body(): dmid_all = lax.all_gather(dmid.astype(bf16), 'tensor', axis=0, tiled=True)]
    pallas_call x0 -> x1, Pallas kernels: none -> 179 us  [forward_call(): pl.pallas_call(functools.partial(forward_kernel, shards), out_shape=outs,...]
    dot_general x74 -> x55, matrix products: 206 us -> 141 us  [the longest x22 53.7 us: nt_dot(): lax.dot_general(left, right, (((1,), (1,)), ((), ())), preferred_element_...]
    all_gather x4 -> x0, blocking collectives: 61.6 us -> none  [the longest x1 25.4 us: body(): lax.all_gather(w_keyval, ('shard', 'ctx'), axis=0, tiled=True)]
    psum x1, blocking collectives: 8.71 us -> 45 us  [body(): both = lax.psum(jnp.stack([ga, gm]), ('shard', 'ctx', 'tensor'))]
    unnamed x1 -> x0, blocking collectives: 27.3 us -> none
  transfers between devices with their start and end apart: 20 -> 11, of which waited for: 19 -> 10; matrix products, arithmetic and copies ran while one was open for 10% -> 7% of each run, Pallas kernels for 0% -> 0%
where the time goes in v1:
time: 871 us; the launch traced here: 859 us
  waiting for transfers between devices  412 us (47%)
  Pallas kernels  179 us (21%)
  matrix products  141 us (16%)
  other arithmetic  51.6 us (6%)
  blocking collectives  45 us (5%)
  local copies, waits for them, and re-layouts  14.7 us (2%)
  between operations  14.7 us (2%)
    reduce_scatter x6, waiting for transfers between devices, body(): lax.psum_scatter(v.astype(bf16), ('shard', 'ctx'), scatter_dimension=0, t...  276 us
    pallas_call x1, Pallas kernels, forward_call(): pl.pallas_call(functools.partial(forward_kernel, shards), out_shape=outs,...  179 us
    reduce_scatter x3, waiting for transfers between devices, body(): lax.psum_scatter(v, 'tensor', scatter_dimension=0, tiled=True)  86.5 us
    dot_general x22, matrix products, nt_dot(): lax.dot_general(left, right, (((1,), (1,)), ((), ())), preferred_element_...  53.7 us
    dot_general x20, matrix products, nn_dot(): return jnp.dot(left, right, preferred_element_type=f32)  50.4 us
    all_gather x1, waiting for transfers between devices, body(): dmid_all = lax.all_gather(dmid.astype(bf16), 'tensor', axis=0, tiled=True)  45.3 us
    psum x1, blocking collectives, body(): both = lax.psum(jnp.stack([ga, gm]), ('shard', 'ctx', 'tensor'))  45 us
    dot_general x13, matrix products, tn_dot(): lax.dot_general(left, right, (((0,), (0,)), ((), ())), preferred_element_...  36.7 us
  transfers between devices with their start and end apart: 11, of which 10 were waited for; matrix products, arithmetic and copies ran while one was open for 7% of the time, Pallas kernels for 0%

profile of v1, /device:TPU:9, one launch (start us, length us, event | category | flops | bytes accessed | tf_op | source)
XLA Modules:
  0.0 858.9 jit_solution(17012697011128572194)
XLA Ops:
  12.3 178.9 %forward.1 = (bf16[2048,512]{1,0:T(8,128)(2,1)}, bf16[2048,128]{1,0:T(8,128)(2,1)}, bf16[2048,512]{1,0:T(8,128)(2,1)}, bf16[2048,1408]{1,0:T(8,128)(2,1)}, bf16[...) custom-call(bf16[128,2048]{1,0:T(8,128)(2,1)} %bitcast.123, ...), custom_call_target="tpu_custom_call" | custom-call | tf_op jit(solution)/shard_map/forward/pallas_call | solution.py:551
  191.3 6.5 fusion.43
  197.9 3.4 fusion.42
  201.4 5.2 multiply_convert_fusion.1
  206.6 3.4 fusion.44
  210.1 4.7 add_convert_fusion.1
  216.2 44.7 %reduce-scatter.13.cloned.1.call-done = bf16[128,2048]{1,0:T(8,128)(2,1)} async-done(((bf16[512,2048]{1,0:T(8,128)(2,1)}), bf16[128,2048]{1,0:T(8,128)(2,1)}) %reduce-scatter.13.cloned.1.call-update) | async-done | bytes 524304 | tf_op jit(solution)/shard_map/reduce_scatter | solution.py:628
  262.5 2.2 fusion.39
  265.3 45.3 %all-gather.2.cloned.1.call-done = bf16[512,2048]{1,0:T(8,128)(2,1)} async-done(((bf16[128,2048]{1,0:T(8,128)(2,1)}), bf16[512,2048]{1,0:T(8,128)(2,1)}) %all-gather.2.cloned.1.call-update) | async-done | bytes 2097168 | tf_op jit(solution)/shard_map/all_gather | solution.py:648
  310.6 4.3 convolution_convert_fusion.7
  314.9 99.8 %while.13 = (s32[]{:T(128)}, f32[2048,128]{0,1:T(8,128)}, f32[8,64,512]{2,1,0:T(8,128)}, bf16[8,128,512]{2,1,0:T(8,128)(2,1)}, bf16[2048,128]{1,0:T(8,128)(2,1)S...) while((s32[]{:T(128)}, f32[2048,128]{0,1:T(8,128)}, ...), condition=%wide.region_7.8_spmd.clone, body=%wide.region_5.0_spmd.clone.sunk | while | flops 812547584 | bytes 26819260 | solution.py:668
  317.6 2.1 multiply_convert_fusion.5
  319.7 2.1 fusion.105
  323.5 2.1 maximum_add_fusion.2
  327.1 1.8 fusion.102
  329.8 2.1 multiply_convert_fusion.5
  331.9 2.1 fusion.105
  335.7 2.5 maximum_add_fusion.2
  339.6 1.8 fusion.102
  342.3 2.1 multiply_convert_fusion.5
  344.4 2.1 fusion.105
  348.2 2.5 maximum_add_fusion.2
  352.1 1.8 fusion.102
  354.8 2.1 multiply_convert_fusion.5
  356.9 2.1 fusion.105
  360.7 2.5 maximum_add_fusion.2
  364.6 1.8 fusion.102
  367.3 2.1 multiply_convert_fusion.5
  369.4 2.1 fusion.105
  373.2 2.5 maximum_add_fusion.2
  379.8 2.1 multiply_convert_fusion.5
  382.0 2.1 fusion.105
  385.8 2.5 maximum_add_fusion.2
  389.7 1.8 fusion.102
  392.4 2.1 multiply_convert_fusion.5
  394.5 2.1 fusion.105
  398.3 2.5 maximum_add_fusion.2
  402.2 1.8 fusion.102
  404.9 2.1 multiply_convert_fusion.5
  407.0 2.1 fusion.105
  410.8 2.5 maximum_add_fusion.2
  414.8 8.0 convolution_convert_fusion.1
  424.3 6.6 convolution_convert_fusion
  432.6 6.6 convolution_convert_fusion.2
  439.5 3.7 reduce-scatter.15.cloned.1.call-done
  446.9 4.4 convolution_convert_fusion.3
  453.7 2.6 convolution_convert_fusion.4
  456.4 1.8 copy-done.9
  459.5 2.1 add_convert_fusion
  463.0 7.3 convolution_convert_fusion.5
  471.7 33.9 %reduce-scatter.27.cloned.1.call-done = bf16[256,1408]{1,0:T(8,128)(2,1)} async-done(((bf16[2048,1408]{1,0:T(8,128)(2,1)}), bf16[256,1408]{1,0:T(8,128)(2,1)}) %reduce-scatter.27.cloned.1.call-update) | async-done | bytes 720912 | tf_op jit(solution)/shard_map/reduce_scatter | solution.py:629
  505.6 2.3 convert_element_type.142
  507.9 60.4 %reduce-scatter.29.cloned.1.call-done = bf16[256,1408]{1,0:T(8,128)(2,1)} async-done(((bf16[2048,1408]{1,0:T(8,128)(2,1)}), bf16[256,1408]{1,0:T(8,128)(2,1)}) %reduce-scatter.29.cloned.1.call-update) | async-done | bytes 720912 | tf_op jit(solution)/shard_map/reduce_scatter | solution.py:629
  568.3 2.3 convert_element_type.144
  570.6 60.1 %reduce-scatter.25.cloned.1.call-done = bf16[256,1408]{1,0:T(8,128)(2,1)} async-done(((bf16[2048,1408]{1,0:T(8,128)(2,1)}), bf16[256,1408]{1,0:T(8,128)(2,1)}) %reduce-scatter.25.cloned.1.call-update) | async-done | bytes 720912 | tf_op jit(solution)/shard_map/reduce_scatter | solution.py:629
  630.7 2.3 convert_element_type.140
  633.0 35.3 %reduce-scatter.21.cloned.1.call-done = bf16[256,128]{1,0:T(8,128)(2,1)} async-done(((bf16[2048,128]{1,0:T(8,128)(2,1)}), bf16[256,128]{1,0:T(8,128)(2,1)}) %reduce-scatter.21.cloned.1.call-update) | async-done | bytes 65552 | tf_op jit(solution)/shard_map/reduce_scatter | solution.py:629
  669.9 43.5 %reduce-scatter.23.cloned.1.call-done = bf16[256,512]{1,0:T(8,128)(2,1)} async-done(((bf16[2048,512]{1,0:T(8,128)(2,1)}), bf16[256,512]{1,0:T(8,128)(2,1)}) %reduce-scatter.23.cloned.1.call-update) | async-done | bytes 262160 | tf_op jit(solution)/shard_map/reduce_scatter | solution.py:629
  713.3 1.8 convert_element_type.138
  715.2 43.1 %reduce-scatter.19.cloned.1.call-done = bf16[256,512]{1,0:T(8,128)(2,1)} async-done(((bf16[2048,512]{1,0:T(8,128)(2,1)}), bf16[256,512]{1,0:T(8,128)(2,1)}) %reduce-scatter.19.cloned.1.call-update) | async-done | bytes 262160 | tf_op jit(solution)/shard_map/reduce_scatter | solution.py:629
  758.3 1.8 convert_element_type.134
  760.1 41.8 %reduce-scatter.17.cloned.1.call-done = bf16[128,2048]{1,0:T(8,128)(2,1)} async-done(((bf16[512,2048]{1,0:T(8,128)(2,1)}), bf16[128,2048]{1,0:T(8,128)(2,1)}) %reduce-scatter.17.cloned.1.call-update) | async-done | bytes 524304 | tf_op jit(solution)/shard_map/reduce_scatter | solution.py:628
  803.4 45.0 %psum.7 = f32[2,2048]{1,0:T(2,128)S(1)} all-reduce(f32[2,2048]{1,0:T(2,128)S(1)} %pad_maximum_fusion.4), channel_id=1, replica_groups=mesh['shard'=2,'ctx'=4,'tensor'=4] {'shard','ctx','tensor'}, use_global_device_ids=true, to_apply=%region_13.14 | all-reduce | flops 4096 | bytes 32768 | tf_op jit(solution)/shard_map/psum | solution.py:684
  849.0 2.9 fusion.27
  (178 shorter events, 61.7 us)
Async XLA Ops:
  7.2 253.8 %reduce-scatter.13.cloned.1.call-start = ((), (), s32[]{:S(2)}) async-start(), calls=%async_computation.11 | async-start | bytes 2621440 | tf_op jit(solution)/shard_map/reduce_scatter | solution.py:628
  11.7 0.6 copy-start.14
  191.3 6.6 copy-start.16
  191.3 6.6 copy-start.17
  191.3 10.0 %slice-start = ((s8[5767168]{0:T(1024)(128)(4,1)}), s8[4194304]{0:T(1024)(128)(4,1)S(1)}, s32[]{:S(2)}) async-start(s8[5767168]{0:T(1024)(128)(4,1)} %bitcast.144), calls=%async_computation.21 | async-start | bytes 8388608
  197.9 3.5 slice-start.1
  197.9 3.5 copy-start.19
  197.9 12.2 %slice-start.2 = ((s8[5767168]{0:T(1024)(128)(4,1)}), s8[4194304]{0:T(1024)(128)(4,1)S(1)}, s32[]{:S(2)}) async-start(s8[5767168]{0:T(1024)(128)(4,1)} %bitcast.146), calls=%async_computation.23 | async-start | bytes 8388608
  201.4 8.7 %slice-start.3 = ((s8[5767168]{0:T(1024)(128)(4,1)}), s8[1572864]{0:T(1024)(128)(4,1)S(1)}, s32[]{:S(2)}) async-start(s8[5767168]{0:T(1024)(128)(4,1)} %bitcast.146), calls=%async_computation.24 | async-start | bytes 3145728
  206.6 3.5 copy-start.22
  206.6 3.5 copy-start.23
  214.8 1.2 copy-start.2
  214.8 1.4 copy-start.15
  214.8 47.6 %copy-start.6 = (bf16[1,128,2048]{2,1,0:T(8,128)(2,1)S(1)}, bf16[1,128,2048]{2,1,0:T(8,128)(2,1)}, u32[]{:S(2)}) copy-start(bf16[1,128,2048]{2,1,0:T(8,128)(2,1)} %param.14) | copy-start | bytes 1572868
  214.9 95.7 %all-gather.2.cloned.1.call-start = ((), (), s32[]{:S(2)}) async-start(), calls=%async_computation.12 | async-start | bytes 2621440 | tf_op jit(solution)/shard_map/all_gather | solution.py:648
  260.9 4.0 copy-start.13
  264.7 178.5 %reduce-scatter.15.cloned.1.call-start = ((), (), s32[]{:S(2)}) async-start(), calls=%async_computation.13 | async-start | bytes 1310720 | tf_op jit(solution)/shard_map/reduce_scatter | solution.py:669
  314.9 2.7 copy-start
  325.7 1.4 copy-start.1
  327.1 2.7 copy-start
  338.2 1.4 copy-start.1
  339.6 2.7 copy-start
  350.7 1.4 copy-start.1
  352.1 2.7 copy-start
  363.2 1.4 copy-start.1
  364.6 2.7 copy-start
  375.7 1.4 copy-start.1
  377.2 2.7 copy-start
  388.3 1.4 copy-start.1
  389.7 2.7 copy-start
  400.8 1.4 copy-start.1
  402.2 2.7 copy-start
  413.3 1.4 copy-start.1
  414.7 90.9 %reduce-scatter.27.cloned.1.call-start = ((), (), s32[]{:S(2)}) async-start(), calls=%async_computation.19 | async-start | bytes 6488064 | tf_op jit(solution)/shard_map/reduce_scatter | solution.py:629
  422.8 1.6 copy-start.20
  422.8 145.6 %reduce-scatter.29.cloned.1.call-start = ((), (), s32[]{:S(2)}) async-start(), calls=%async_computation.20 | async-start | bytes 6488064 | tf_op jit(solution)/shard_map/reduce_scatter | solution.py:629
  431.0 1.6 copy-start.18
  431.0 199.7 %reduce-scatter.25.cloned.1.call-start = ((), (), s32[]{:S(2)}) async-start(), calls=%async_computation.18 | async-start | bytes 6488064 | tf_op jit(solution)/shard_map/reduce_scatter | solution.py:629
  439.2 6.1 copy-start.5
  439.2 229.2 %reduce-scatter.21.cloned.1.call-start = ((), (), s32[]{:S(2)}) async-start(), calls=%async_computation.16 | async-start | bytes 589824 | tf_op jit(solution)/shard_map/reduce_scatter | solution.py:629
  446.9 266.5 %reduce-scatter.23.cloned.1.call-start = ((), (), s32[]{:S(2)}) async-start(), calls=%async_computation.17 | async-start | bytes 2359296 | tf_op jit(solution)/shard_map/reduce_scatter | solution.py:629
  451.3 0.8 copy-start.10
  451.3 0.9 copy-start.11
  451.3 306.9 %reduce-scatter.19.cloned.1.call-start = ((), (), s32[]{:S(2)}) async-start(), calls=%async_computation.15 | async-start | bytes 2359296 | tf_op jit(solution)/shard_map/reduce_scatter | solution.py:629
  456.3 1.8 copy-start.9
  456.3 345.5 %reduce-scatter.17.cloned.1.call-start = ((), (), s32[]{:S(2)}) async-start(), calls=%async_computation.14 | async-start | bytes 2621440 | tf_op jit(solution)/shard_map/reduce_scatter | solution.py:628
  458.2 1.3 copy-start.12
  461.6 1.4 copy-start.21
  461.6 387.4 %reduce-scatter.11.cloned.1.call-start = ((), (), s32[]{:S(2)}) async-start(), calls=%async_computation.10 | async-start | bytes 2621440 | tf_op jit(solution)/shard_map/reduce_scatter | solution.py:628
  470.3 1.2 copy-start.4
  570.6 278.4 %copy-start.3 = (f32[128,2048]{1,0:T(8,128)S(1)}, f32[128,2048]{1,0:T(8,128)}, u32[]{:S(2)}) copy-start(f32[128,2048]{1,0:T(8,128)} %get-tuple-element.79) | copy-start | bytes 3145732
  570.6 278.4 %copy-start.7 = (bf16[1,128,2048]{2,1,0:T(8,128)(2,1)S(1)}, bf16[1,128,2048]{2,1,0:T(8,128)(2,1)}, u32[]{:S(2)}) copy-start(bf16[1,128,2048]{2,1,0:T(8,128)(2,1)} %param.14) | copy-start | bytes 1572868
  570.6 278.4 %copy-start.8 = (bf16[128,2048]{1,0:T(8,128)(2,1)S(1)}, bf16[128,2048]{1,0:T(8,128)(2,1)}, u32[]{:S(2)}) copy-start(bf16[128,2048]{1,0:T(8,128)(2,1)} %reduce-scatter.13.cloned.1.call-done) | copy-start | bytes 1572868
Sparse Core Ops, SparseCore 0:
  215.0 45.9 reduce-scatter.12
  264.8 45.7 all-gather.1
  414.8 28.2 reduce-scatter.14
  446.5 59.0 reduce-scatter.26
  509.3 59.0 reduce-scatter.28
  571.6 59.0 reduce-scatter.24
  634.7 33.6 reduce-scatter.20
  671.7 41.6 reduce-scatter.22
  717.0 41.2 reduce-scatter.18
  760.4 41.4 reduce-scatter.16
  804.3 44.2 reduce-scatter.10

commit v2 on v1

--- a/solution.py
+++ b/solution.py
@@ -67,13 +67,24 @@
     def core_peer(self, step):
         return (lax.rem(self.s + step, self.shards), self.c, self.t)
 
-    def barrier(self):
+    def line_peer(self, step):
+        return (self.s, self.c, lax.rem(self.t + step, LINE))
+
+    def barrier(self, whole_line=False):
         sem = pltpu.get_barrier_semaphore()
         count = self.shards * CTX - 1
         for step in range(1, count + 1):
             pl.semaphore_signal(
                 sem, inc=1, device_id=self.plane_peer(step), device_id_type=MESH
             )
+
+        if whole_line:
+            for step in range(1, LINE):
+                pl.semaphore_signal(
+                    sem, inc=1, device_id=self.line_peer(step), device_id_type=MESH
+                )
+            pl.semaphore_wait(sem, count + LINE - 1)
+            return
 
         @pl.when(self.t > 0)
         def _():
@@ -105,7 +116,13 @@
             def _():
                 self.copy(src, dst, device, slot).start()
 
-        self.sends.append((src, dst, device, slot, cond))
+        handle = (src, dst, device, slot, cond)
+        self.sends.append(handle)
+        return handle
+
+    def sent(self, handle):
+        self.sends = [other for other in self.sends if other is not handle]
+        self.copy(*handle[:4]).wait_send()
 
     def recv(self, dst, slot):
         self.copy(dst, dst, self.x_dev, slot).wait_recv()
@@ -247,9 +264,8 @@
 
 
 class LineScatter:
-    def __init__(self, links, part, tokens, to_right, to_left, from_left, from_right):
+    def __init__(self, links, part, tokens, from_left, from_right):
         self.links, self.part, self.tokens = links, part, tokens
-        self.to_right, self.to_left = to_right, to_left
         self.from_left, self.from_right = from_left, from_right
         self.first = links.slots(2 * (LINE - 1))
 
@@ -267,15 +283,14 @@
                     for k in range(LINE - 1):
                         ref[k, pl.ds(r, ROWS), :] = jnp.zeros((ROWS, ref.shape[2]), ref.dtype)
 
-    def total(self, owner, k, out, arrived):
+    def total(self, owner, k, arrived):
         @pl.loop(0, self.tokens // ROWS)
         def _(i):
             r = pl.multiple_of(i * ROWS, ROWS)
             q = pl.multiple_of(owner * self.tokens + i * ROWS, ROWS)
-            summed = self.part[pl.ds(q, ROWS), :].astype(f32) + arrived[
-                k, pl.ds(r, ROWS), :
-            ].astype(f32)
-            out[k, pl.ds(r, ROWS), :] = summed.astype(out.dtype)
+            mine = self.part[pl.ds(q, ROWS), :].astype(f32)
+            summed = mine + arrived[k, pl.ds(r, ROWS), :].astype(f32)
+            arrived[k, pl.ds(r, ROWS), :] = summed.astype(arrived.dtype)
 
     def step(self, k):
         links = self.links
@@ -289,9 +304,9 @@
             def _():
                 links.recv(self.from_left.at[k], slot_r)
 
-            self.total(owner_r, k, self.to_right, self.from_left)
-
-        links.send(self.to_right.at[k], self.from_left.at[k], links.right, slot_r, t < owner_r)
+            self.total(owner_r, k, self.from_left)
+
+        links.send(self.from_left.at[k], self.from_left.at[k], links.right, slot_r, t < owner_r)
 
         @pl.when(t > owner_l)
         def _():
@@ -299,9 +314,9 @@
             def _():
                 links.recv(self.from_right.at[k], slot_l)
 
-            self.total(owner_l, k, self.to_left, self.from_right)
-
-        links.send(self.to_left.at[k], self.from_right.at[k], links.left, slot_l, t > owner_l)
+            self.total(owner_l, k, self.from_right)
+
+        links.send(self.from_right.at[k], self.from_right.at[k], links.left, slot_l, t > owner_l)
 
     def arrive(self):
         links = self.links
@@ -321,11 +336,114 @@
         q = pl.multiple_of(t * self.tokens + i * ROWS, ROWS)
         k_l = jnp.minimum(LINE - 1 - t, LINE - 2)
         k_r = jnp.minimum(t, LINE - 2)
+        zero = jnp.zeros((ROWS, self.part.shape[1]), f32)
         return (
             self.part[pl.ds(q, ROWS), :].astype(f32)
-            + self.from_left[k_l, pl.ds(r, ROWS), :].astype(f32)
-            + self.from_right[k_r, pl.ds(r, ROWS), :].astype(f32)
+            + jnp.where(t > 0, self.from_left[k_l, pl.ds(r, ROWS), :].astype(f32), zero)
+            + jnp.where(t < LINE - 1, self.from_right[k_r, pl.ds(r, ROWS), :].astype(f32), zero)
         )
+
+
+class PlaneScatter:
+    def __init__(self, links, left, right, rows, core_in, x_in, y_in, x_last, y_last, out):
+        self.links, self.left, self.right, self.rows = links, left, right, rows
+        self.core_in, self.x_in, self.y_in = core_in, x_in, y_in
+        self.x_last, self.y_last, self.out = x_last, y_last, out
+        self.first = links.slots(links.shards - 1 + 6)
+        self.tile = min(256, CTX * rows)
+
+    def product(self, shard, i):
+        start = pl.multiple_of(shard * (CTX * self.rows) + i * self.tile, self.tile)
+        return tn_dot(self.left[:, pl.ds(start, self.tile)], self.right[...])
+
+    def other(self, step, stage):
+        links = self.links
+        target = lax.rem(links.s + step, links.shards)
+
+        @pl.loop(0, CTX * self.rows // self.tile)
+        def _(i):
+            r = pl.multiple_of(i * self.tile, self.tile)
+            stage[pl.ds(r, self.tile), :] = self.product(target, i).astype(bf16)
+
+        return links.send(
+            stage, self.core_in.at[step - 1], links.core_peer(step), self.first + step - 1
+        )
+
+    def own(self):
+        links = self.links
+        for step in range(1, links.shards):
+            links.recv(self.core_in.at[step - 1], self.first + step - 1)
+
+        @pl.loop(0, CTX * self.rows // self.tile)
+        def _(i):
+            r = pl.multiple_of(i * self.tile, self.tile)
+            summed = self.product(links.s, i)
+            for step in range(1, links.shards):
+                summed = summed + self.core_in[step - 1, pl.ds(r, self.tile), :].astype(f32)
+            self.core_in[0, pl.ds(r, self.tile), :] = summed.astype(bf16)
+
+    def half(self, c, which):
+        size = self.rows // 2
+        start = pl.multiple_of(c * self.rows + which * size, size)
+        return self.core_in.at[0, pl.ds(start, size)]
+
+    def exchange(self):
+        links, first = self.links, self.first + self.links.shards - 1
+        links.send(self.half(links.c_d, 0), self.x_in.at[1], links.x_dev, first)
+        links.send(self.half(links.c_d, 1), self.y_in.at[1], links.y_dev, first + 1)
+        links.send(self.half(links.c_x, 0), self.x_in.at[0], links.x_dev, first + 2)
+        links.send(self.half(links.c_y, 1), self.y_in.at[0], links.y_dev, first + 3)
+
+    def add(self, c, which, arrived):
+        size = self.rows // 2
+
+        @pl.loop(0, size // ROWS)
+        def _(i):
+            r = pl.multiple_of(i * ROWS, ROWS)
+            q = pl.multiple_of(c * self.rows + which * size + i * ROWS, ROWS)
+            mine = self.core_in[0, pl.ds(q, ROWS), :].astype(f32)
+            summed = mine + arrived[1, pl.ds(r, ROWS), :].astype(f32)
+            self.core_in[0, pl.ds(q, ROWS), :] = summed.astype(bf16)
+
+    def fold(self):
+        links, first = self.links, self.first + self.links.shards - 1
+        links.recv(self.x_in.at[1], first)
+        self.add(links.c_y, 0, self.x_in)
+        links.send(self.half(links.c_y, 0), self.y_last, links.y_dev, first + 4)
+        links.recv(self.y_in.at[1], first + 1)
+        self.add(links.c_x, 1, self.y_in)
+        links.send(self.half(links.c_x, 1), self.x_last, links.x_dev, first + 5)
+
+    def total(self):
+        links, first = self.links, self.first + self.links.shards - 1
+        size = self.rows // 2
+        links.recv(self.x_in.at[0], first + 2)
+        links.recv(self.y_in.at[0], first + 3)
+        links.recv(self.y_last, first + 4)
+        links.recv(self.x_last, first + 5)
+        for which, arrived, last in ((0, self.x_in, self.y_last), (1, self.y_in, self.x_last)):
+
+            @pl.loop(0, size // ROWS)
+            def _(i):
+                r = pl.multiple_of(i * ROWS, ROWS)
+                q = pl.multiple_of(links.c * self.rows + which * size + i * ROWS, ROWS)
+                self.out[pl.ds(which * size + r, ROWS), :] = (
+                    self.core_in[0, pl.ds(q, ROWS), :].astype(f32)
+                    + arrived[0, pl.ds(r, ROWS), :].astype(f32)
+                    + last[pl.ds(r, ROWS), :].astype(f32)
+                )
+
+    @staticmethod
+    def scratch(shards, rows, columns):
+        half = (rows // 2, columns)
+        return [
+            pltpu.VMEM((shards - 1, CTX * rows, columns), bf16),
+            pltpu.VMEM((2,) + half, bf16),
+            pltpu.VMEM((2,) + half, bf16),
+            pltpu.VMEM(half, bf16),
+            pltpu.VMEM(half, bf16),
+            pltpu.VMEM((rows, columns), f32),
+        ]
 
 
 def any_spec():
@@ -346,7 +464,7 @@
     wq_o, wkv_o, wo_o, wg_o, wu_o, wd_o, n1_o, og_o, n2_o, mid_o, qaug_o, kaug_o, kv_o, att_o,
     lse, gains,
     x_all, n1_all, wq_all, wkv_all, wo_all, gains_all, qaug, kv_all, kaug, v_all, scores, weights,
-    attn, part, to_right, to_left, from_left, from_right, mid, n2,
+    attn, part, from_left, from_right, mid, n2,
     send_sems, recv_sems, local_sems,
 ):
     tokens, width = x.shape
@@ -360,9 +478,7 @@
     gather_n2 = LineGather(links, n2, n2_o, tokens)
     small = [PlaneGather(links, *pair) for pair in ((wq, wq_all), (wkv, wkv_all), (wo, wo_all))]
     large = [PlaneGather(links, *pair) for pair in ((wg, wg_o), (wu, wu_o), (wd, wd_o))]
-    scatter = LineScatter(
-        links, part, tokens, to_right, to_left, from_left, from_right
-    )
+    scatter = LineScatter(links, part, tokens, from_left, from_right)
     plane = shards * CTX
     gain_slot = links.slots(plane - 1)
     kv_slot = links.slots(3)
@@ -570,8 +686,6 @@
             pltpu.VMEM((queries, width), f32),
             pltpu.VMEM(block, bf16),
             pltpu.VMEM(block, bf16),
-            pltpu.VMEM(block, bf16),
-            pltpu.VMEM(block, bf16),
             pltpu.VMEM((tokens, width), f32),
             pltpu.VMEM((tokens, width), bf16),
             pltpu.SemaphoreType.DMA((count,)),
@@ -585,18 +699,425 @@
     )(x, og, wq, wkv, wo, wg, wu, wd, gpad, cos, sin, bias)
 
 
-def norm_backward_pass(normed_gradient, unit_rows, inverse_root_mean, norm_scale):
-    unit_rows_gradient = normed_gradient * norm_scale
-    scale_gradient = jnp.sum(normed_gradient * unit_rows, axis=0)
-    value_gradients = inverse_root_mean * (
-        unit_rows_gradient - unit_rows * jnp.mean(unit_rows_gradient * unit_rows, -1, keepdims=True)
+def middle_kernel(
+    shards, rows,
+    n2_in, og_in, wg_in, wu_in, wd_in, mid_in, gains,
+    out_o, dmid_o, dmid_all_o, gg_o, gu_o, gd_o, gain_sum,
+    n2, og, wg, wu, wd, mid, hidden, dgate, dup, part, branch,
+    left_a, right_a, left_b, right_b, dmid, dsend, layer, gain_rows,
+    *rest,
+):
+    grads, (send_sems, recv_sems, local_sems) = rest[:-3], rest[-3:]
+    tokens, width = mid.shape
+    queries = n2.shape[0]
+    columns = wg.shape[1]
+    links = Links(shards, send_sems, recv_sems, local_sems)
+    t = links.t
+
+    loads = [
+        links.keep(src, dst)
+        for src, dst in (
+            (n2_in, n2), (wg_in, wg), (wu_in, wu), (og_in, og), (wd_in, wd), (mid_in, mid)
+        )
+    ]
+    scatter = LineScatter(links, part, tokens, left_a, right_a)
+    scatter_out = LineScatter(links, branch, tokens, left_b, right_b)
+    gather = LineGather(links, dsend, dmid_all_o, tokens)
+    down = PlaneScatter(links, og, hidden, rows, *grads[0:6])
+    gate = PlaneScatter(links, n2, dgate, rows, *grads[6:12])
+    up = PlaneScatter(links, n2, dup, rows, *grads[12:18])
+    links.barrier()
+    scatter.clear()
+    scatter_out.clear()
+    for load in loads:
+        load.wait()
+
+    for b in range(0, columns, 256):
+        e = min(b + 256, columns)
+        gate_act = nn_dot(n2[...], wg[:, b:e])
+        up_act = nn_dot(n2[...], wu[:, b:e])
+        d_hidden = nn_dot(og[...], wd[:, b:e])
+        sig = jax.nn.sigmoid(gate_act)
+        silu = gate_act * sig
+        hidden[:, b:e] = (silu * up_act).astype(bf16)
+        dgate[:, b:e] = (d_hidden * up_act * sig * (1.0 + gate_act * (1.0 - sig))).astype(bf16)
+        dup[:, b:e] = (d_hidden * silu).astype(bf16)
+
+    @pl.loop(0, width // 512)
+    def _(j):
+        at = pl.ds(pl.multiple_of(j * 512, 512), 512)
+        part[:, at] = (nt_dot(dgate[...], wg[at, :]) + nt_dot(dup[...], wu[at, :])).astype(bf16)
+
+    scatter.step(0)
+
+    @pl.loop(0, width // 512)
+    def _(j):
+        at = pl.ds(pl.multiple_of(j * 512, 512), 512)
+        branch[:, at] = nt_dot(hidden[...], wd[at, :]).astype(bf16)
+
+    piece = CTX * rows
+    room = (width // piece) // (shards - 1)
+
+    def others(grad, index, before):
+        handles = []
+        for step in range(1, shards):
+            at = ((index % room) * (shards - 1) + step - 1) * piece
+            if before:
+                links.sent(before[step - 1])
+            handles.append(grad.other(step, wd.at[pl.ds(at, piece)]))
+        return handles
+
+    held = [others(down, 0, None)]
+    held.append(others(gate, 1, held[1 - room] if room <= 1 else None))
+    scatter.step(1)
+    down.own()
+    down.exchange()
+    gate.own()
+    gate.exchange()
+    others(up, 2, held[2 - room] if room <= 2 else None)
+    scatter.step(2)
+    up.own()
+    up.exchange()
+    scatter.arrive()
+    gain_rows[...] = jnp.zeros_like(gain_rows)
+
+    @pl.loop(0, tokens // ROWS)
+    def _(i):
+        r = pl.ds(pl.multiple_of(i * ROWS, ROWS), ROWS)
+        q = pl.ds(pl.multiple_of(t * tokens + i * ROWS, ROWS), ROWS)
+        middle = mid[r, :]
+        inverse = lax.rsqrt(jnp.mean(middle * middle, -1, keepdims=True) + epsilon)
+        unit = middle * inverse
+        d_normed = scatter.rows(i)
+        gain_rows[...] += d_normed * unit
+        d_unit = d_normed * gains[1:2, :]
+        back = inverse * (d_unit - unit * jnp.mean(d_unit * unit, -1, keepdims=True))
+        d_middle = og[q, :].astype(f32) + back
+        dmid[r, :] = d_middle
+        dsend[r, :] = d_middle.astype(bf16)
+
+    gather.send(1)
+    scatter_out.step(0)
+    links.keep_later(dsend, dmid_all_o.at[pl.ds(pl.multiple_of(t * tokens, tokens), tokens)])
+    links.keep_later(dmid, dmid_o)
+    gain_sum[...] = jnp.sum(gain_rows[...], 0, keepdims=True)
+    down.fold()
+    gather.recv(1)
+    gather.send(2)
+    scatter_out.step(1)
+    gate.fold()
+    gather.recv(2)
+    gather.send(3)
+    scatter_out.step(2)
+    up.fold()
+    down.total()
+    links.keep_later(down.out, gd_o)
+    gate.total()
+    links.keep_later(gate.out, gg_o)
+    scatter_out.arrive()
+
+    @pl.loop(0, tokens // ROWS)
+    def _(i):
+        r = pl.ds(pl.multiple_of(i * ROWS, ROWS), ROWS)
+        layer[r, :] = (mid[r, :] + scatter_out.rows(i)).astype(bf16)
+
+    links.keep_later(layer, out_o)
+    gather.recv(3)
+    up.total()
+    links.keep_later(up.out, gu_o)
+    links.finish()
+
+
+def middle_call(shards, rows, n2, og, wg, wu, wd, mid, gains):
+    queries, width = n2.shape
+    tokens = mid.shape[0]
+    columns = wg.shape[1]
+    token = (tokens, width)
+    wide = (queries, columns)
+    block = (LINE - 1,) + token
+    outs = [
+        struct(token, bf16),
+        struct(token, f32),
+        struct((queries, width), bf16),
+        struct((rows, columns), f32),
+        struct((rows, columns), f32),
+        struct((rows, columns), f32),
+        struct((1, width), f32),
+    ]
+    count = 3 * 6 + 3 * (shards - 1 + 6)
+    return pl.pallas_call(
+        functools.partial(middle_kernel, shards, rows),
+        out_shape=outs,
+        in_specs=[any_spec()] * 6 + [vmem_spec()],
+        out_specs=[any_spec()] * 6 + [vmem_spec()],
+        scratch_shapes=[
+            pltpu.VMEM((queries, width), bf16),
+            pltpu.VMEM((queries, width), bf16),
+            pltpu.VMEM((width, columns), bf16),
+            pltpu.VMEM((width, columns), bf16),
+            pltpu.VMEM((width, columns), bf16),
+            pltpu.VMEM(token, f32),
+            pltpu.VMEM(wide, bf16),
+            pltpu.VMEM(wide, bf16),
+            pltpu.VMEM(wide, bf16),
+            pltpu.VMEM((queries, width), bf16),
+            pltpu.VMEM((queries, width), bf16),
+            pltpu.VMEM(block, bf16),
+            pltpu.VMEM(block, bf16),
+            pltpu.VMEM(block, bf16),
+            pltpu.VMEM(block, bf16),
+            pltpu.VMEM(token, f32),
+            pltpu.VMEM(token, bf16),
+            pltpu.VMEM(token, bf16),
+            pltpu.VMEM((ROWS, width), f32),
+            *PlaneScatter.scratch(shards, rows, columns),
+            *PlaneScatter.scratch(shards, rows, columns),
+            *PlaneScatter.scratch(shards, rows, columns),
+            pltpu.SemaphoreType.DMA((count,)),
+            pltpu.SemaphoreType.DMA((count,)),
+            pltpu.SemaphoreType.DMA((16,)),
+        ],
+        compiler_params=pltpu.CompilerParams(
+            collective_id=1, has_side_effects=True, vmem_limit_bytes=63 * 2**20
+        ),
+        name="middle",
+    )(n2, og, wg, wu, wd, mid, gains)
+
+
+def backward_kernel(
+    shards, rows,
+    dmid_all_in, wo_in, wq_in, wkv_in, n1_in, qaug_in, kaug_in, kv_in, att_in, x_in, dmid_in,
+    lse, gains, gain_mlp, cos, sin,
+    in_o, gq_o, gkv_o, go_o, gain_o,
+    dmid_all, wo, wq, wkv, n1, qaug, kaug, kv, att, x, dmid,
+    d_out, attn_rows, v_rows, d_keys, d_values, d_query, d_query_rows, kv_send, kv_recv, d_kv, part,
+    left, right, gain_rows, pair, plane_in, line_in, total, stage_o, stage_q, stage_kv,
+    *rest,
+):
+    grads, (send_sems, recv_sems, local_sems) = rest[:-3], rest[-3:]
+    tokens, width = x.shape
+    queries = n1.shape[0]
+    heads = qaug.shape[0]
+    length = kaug.shape[0]
+    half = HD // 2
+    plane = shards * CTX
+    links = Links(shards, send_sems, recv_sems, local_sems)
+    s, c, t = links.s, links.c, links.t
+
+    loads = [
+        links.keep(src, dst)
+        for src, dst in (
+            (dmid_all_in, dmid_all), (wo_in, wo), (att_in, att), (kv_in, kv), (qaug_in, qaug),
+            (kaug_in, kaug), (n1_in, n1), (wq_in, wq), (wkv_in, wkv), (x_in, x), (dmid_in, dmid),
+        )
+    ]
+    scatter = LineScatter(links, part, tokens, left, right)
+    g_o = PlaneScatter(links, dmid_all, attn_rows, rows, *grads[0:6])
+    g_q = PlaneScatter(links, n1, d_query_rows, rows, *grads[6:12])
+    g_kv = PlaneScatter(links, n1, d_kv, rows, *grads[12:18])
+    kv_slot = links.slots(CTX - 1)
+    plane_slot = links.slots(plane - 1)
+    line_slot = links.slots(LINE - 1)
+    piece = CTX * rows
+
+    def others(grad, stage):
+        for step in range(1, shards):
+            grad.other(step, stage.at[pl.ds((step - 1) * piece, piece)])
+
+    links.barrier(whole_line=True)
+    scatter.clear()
+    for load in loads:
+        load.wait()
+
+    d_out[...] = nn_dot(dmid_all[...], wo[...]).astype(bf16).T
+    attn_rows[...] = att[...].T
+    for other in range(CTX):
+        v_rows[other * queries : (other + 1) * queries, :] = kv[other, HD : 2 * HD, :].T
+    d_keys[...] = jnp.zeros_like(d_keys)
+    d_values[...] = jnp.zeros_like(d_values)
+    others(g_o, stage_o)
+
+    def head(h):
+        at = pl.ds(pl.multiple_of(h * HD, HD), HD)
+        query = qaug[h]
+        d_head = d_out[at, :]
+        delta = jnp.sum(d_head.astype(f32) * att[at, :].astype(f32), 0, keepdims=True)
+        log_sum = lse[pl.ds(h, 1), :]
+        d_q = jnp.zeros((HD, queries), f32)
+        for b in range(0, length, BLOCK):
+            e = b + BLOCK
+            probs = jnp.exp(nn_dot(kaug[b:e, :], query) - log_sum)
+            d_probs = nn_dot(v_rows[b:e, :], d_head)
+            d_scores = (probs * (d_probs - delta)).astype(bf16)
+            d_values[b:e, :] += nt_dot(probs.astype(bf16), d_head)
+            d_keys[b:e, :] += nt_dot(d_scores, query[0:HD])
+            at_b = b % queries
+            d_q = d_q + nn_dot(kv[b // queries, 0:HD, at_b : at_b + BLOCK], d_scores)
+        d_query[at, :] = d_q * (HD ** (-0.5))
+
+    pl.loop(0, heads // 2)(head)
+    g_o.own()
+    g_o.exchange()
+    pl.loop(heads // 2, heads)(head)
+    g_o.fold()
+
+    for other in range(CTX):
+        block = slice(other * queries, (other + 1) * queries)
+        both = jnp.concatenate([d_keys[block, :], d_values[block, :]], 1)
+        kv_send[other] = both.astype(bf16)
+    for step in range(1, CTX):
+        peer = lax.rem(c + step, CTX)
+        links.send(kv_send.at[peer], kv_recv.at[step - 1], (s, peer, t), kv_slot + step - 1)
+
+    cosine, sine = cos[...], sin[...]
+    for h in range(heads):
+        at = h * HD
+        d1, d2 = d_query[at : at + half, :], d_query[at + half : at + HD, :]
+        d_query[at : at + half, :] = d1 * cosine + d2 * sine
+        d_query[at + half : at + HD, :] = d2 * cosine - d1 * sine
+    d_query_rows[...] = d_query[...].astype(bf16).T
+    others(g_q, stage_q)
+    for step in range(1, CTX):
+        links.recv(kv_recv.at[step - 1], kv_slot + step - 1)
+    d_pair = kv_send[c].astype(f32)
+    for step in range(1, CTX):
+        d_pair = d_pair + kv_recv[step - 1].astype(f32)
+    d_pair = d_pair.T
+    d1, d2 = d_pair[0:half], d_pair[half:HD]
+    turned = jnp.concatenate(
+        [d1 * cosine + d2 * sine, d2 * cosine - d1 * sine, d_pair[HD:]], 0
     )
-    return (scale_gradient, value_gradients)
-
-
-def apply_norm(values_in):
-    inverse_root_mean = lax.rsqrt(jnp.mean(values_in * values_in, -1, keepdims=True) + epsilon)
-    return (values_in * inverse_root_mean, inverse_root_mean)
+    d_kv[...] = turned.astype(bf16).T
+
+    @pl.loop(0, width // 512)
+    def _(j):
+        at = pl.ds(pl.multiple_of(j * 512, 512), 512)
+        summed = nt_dot(d_query_rows[...], wq[at, :]) + nt_dot(d_kv[...], wkv[at, :])
+        part[:, at] = summed.astype(bf16)
+
+    scatter.step(0)
+    others(g_kv, stage_kv)
+    g_q.own()
+    g_q.exchange()
+    g_kv.own()
+    g_kv.exchange()
+    g_o.total()
+    links.keep_later(g_o.out, go_o)
+    scatter.step(1)
+    g_q.fold()
+    g_kv.fold()
+    scatter.step(2)
+    g_q.total()
+    links.keep_later(g_q.out, gq_o)
+    g_kv.total()
+    links.keep_later(g_kv.out, gkv_o)
+    gain_rows[...] = jnp.zeros_like(gain_rows)
+    scatter.arrive()
+
+    @pl.loop(0, tokens // ROWS)
+    def _(i):
+        r = pl.ds(pl.multiple_of(i * ROWS, ROWS), ROWS)
+        v = x[r, :].astype(f32)
+        inverse = lax.rsqrt(jnp.mean(v * v, -1, keepdims=True) + epsilon)
+        unit = v * inverse
+        d_normed = scatter.rows(i)
+        gain_rows[...] += d_normed * unit
+        d_unit = d_normed * gains[0:1, :]
+        back = inverse * (d_unit - unit * jnp.mean(d_unit * unit, -1, keepdims=True))
+        dmid[r, :] = dmid[r, :] + back
+
+    pair[0:1, :] = jnp.sum(gain_rows[...], 0, keepdims=True)
+    pair[1:2, :] = gain_mlp[...]
+    for step in range(1, plane):
+        links.send(pair, plane_in.at[step - 1], links.plane_peer(step), plane_slot + step - 1)
+    links.keep_later(dmid, in_o)
+    summed = pair[...]
+    for step in range(1, plane):
+        links.recv(plane_in.at[step - 1], plane_slot + step - 1)
+        summed = summed + plane_in[step - 1]
+    total[...] = summed
+    for step in range(1, LINE):
+        links.send(total, line_in.at[step - 1], links.line_peer(step), line_slot + step - 1)
+    for step in range(1, LINE):
+        links.recv(line_in.at[step - 1], line_slot + step - 1)
+        summed = summed + line_in[step - 1]
+    gain_o[...] = summed
+    links.finish()
+
+
+def backward_call(
+    shards, rows, dmid_all, wo, wq, wkv, n1, qaug, kaug, kv, att, x, dmid, lse, gains, gain_mlp,
+    cos, sin,
+):
+    tokens, width = x.shape
+    queries = n1.shape[0]
+    heads = qaug.shape[0]
+    length = kaug.shape[0]
+    inner = heads * HD
+    plane = shards * CTX
+    piece = CTX * rows * (shards - 1)
+    token = (tokens, width)
+    block = (LINE - 1,) + token
+    outs = [
+        struct(token, f32),
+        struct((rows, inner), f32),
+        struct((rows, 2 * HD), f32),
+        struct((rows, inner), f32),
+        struct((2, width), f32),
+    ]
+    count = 6 + 3 * (shards - 1 + 6) + CTX - 1 + plane - 1 + LINE - 1
+    return pl.pallas_call(
+        functools.partial(backward_kernel, shards, rows),
+        out_shape=outs,
+        in_specs=[any_spec()] * 11 + [vmem_spec()] * 5,
+        out_specs=[any_spec()] * 4 + [vmem_spec()],
+        scratch_shapes=[
+            pltpu.VMEM((queries, width), bf16),
+            pltpu.VMEM((width, inner), bf16),
+            pltpu.VMEM((width, inner), bf16),
+            pltpu.VMEM((width, 2 * HD), bf16),
+            pltpu.VMEM((queries, width), bf16),
+            pltpu.VMEM(qaug.shape, bf16),
+            pltpu.VMEM(kaug.shape, bf16),
+            pltpu.VMEM(kv.shape, bf16),
+            pltpu.VMEM((inner, queries), bf16),
+            pltpu.VMEM(token, bf16),
+            pltpu.VMEM(token, f32),
+            pltpu.VMEM((inner, queries), bf16),
+            pltpu.VMEM((queries, inner), bf16),
+            pltpu.VMEM((length, HD), bf16),
+            pltpu.VMEM((length, HD), f32),
+            pltpu.VMEM((length, HD), f32),
+            pltpu.VMEM((inner, queries), f32),
+            pltpu.VMEM((queries, inner), bf16),
+            pltpu.VMEM((CTX, queries, 2 * HD), bf16),
+            pltpu.VMEM((CTX - 1, queries, 2 * HD), bf16),
+            pltpu.VMEM((queries, 2 * HD), bf16),
+            pltpu.VMEM((queries, width), bf16),
+            pltpu.VMEM(block, bf16),
+            pltpu.VMEM(block, bf16),
+            pltpu.VMEM((ROWS, width), f32),
+            pltpu.VMEM((2, width), f32),
+            pltpu.VMEM((plane - 1, 2, width), f32),
+            pltpu.VMEM((LINE - 1, 2, width), f32),
+            pltpu.VMEM((2, width), f32),
+            pltpu.VMEM((piece, inner), bf16),
+            pltpu.VMEM((piece, inner), bf16),
+            pltpu.VMEM((piece, 2 * HD), bf16),
+            *PlaneScatter.scratch(shards, rows, inner),
+            *PlaneScatter.scratch(shards, rows, inner),
+            *PlaneScatter.scratch(shards, rows, 2 * HD),
+            pltpu.SemaphoreType.DMA((count,)),
+            pltpu.SemaphoreType.DMA((count,)),
+            pltpu.SemaphoreType.DMA((16,)),
+        ],
+        compiler_params=pltpu.CompilerParams(
+            collective_id=2, has_side_effects=True, vmem_limit_bytes=60 * 2**20
+        ),
+        name="backward",
+    )(
+        dmid_all, wo, wq, wkv, n1, qaug, kaug, kv, att, x, dmid, lse, gains, gain_mlp, cos, sin
+    )
 
 
 def body(
@@ -625,63 +1146,13 @@
     (wq, wkv, wo, wg, wu, wd, n1, og_all, n2, mid, qaug, kaug, kv, att, lse, gains) = forward_call(
         shards, x, og, (w_query, w_keyval, w_output, w_gate, w_up, w_down), gpad, cos, sin, bias
     )
-    rs = lambda v: lax.psum_scatter(v, "tensor", scatter_dimension=0, tiled=True)
-    ws = lambda v: lax.psum_scatter(
-        v.astype(bf16), ("shard", "ctx"), scatter_dimension=0, tiled=True
-    ).astype(f32)
-    gate = nn_dot(n2, wg)
-    up = nn_dot(n2, wu)
-    sg = jax.nn.sigmoid(gate)
-    silu = gate * sg
-    hidden = (silu * up).astype(bf16)
-    layer_out = (mid + rs(nt_dot(hidden, wd).astype(bf16)).astype(f32)).astype(bf16)
-    dh = nn_dot(og_all, wd)
-    grad_down = ws(tn_dot(og_all, hidden))
-    dgate = (dh * up * sg * (1.0 + gate * (1.0 - sg))).astype(bf16)
-    dup = (dh * silu).astype(bf16)
-    grad_gate = ws(tn_dot(n2, dgate))
-    grad_up = ws(tn_dot(n2, dup))
-    dn2 = rs((nt_dot(dgate, wg) + nt_dot(dup, wu)).astype(bf16)).astype(f32)
-    unit2, inv2 = apply_norm(mid)
-    gm, dmid = norm_backward_pass(dn2, unit2, inv2, gains[1:2])
-    dmid = dmid + og.astype(f32)
-    dmid_all = lax.all_gather(dmid.astype(bf16), "tensor", axis=0, tiled=True)
-    datt = nn_dot(dmid_all, wo).astype(bf16)
-    grad_output = ws(nt_dot(dmid_all.T, att))
-    heads = wq.shape[1] // HD
-    datt_t = datt.T.reshape(heads, HD, queries)
-    att_t = att.reshape(heads, HD, queries)
-    k_all = kaug[:, :HD]
-    v_all = jnp.moveaxis(kv[:, HD:], 1, 2).reshape(-1, HD)
-
-    def back(acc, ops):
-        q, do, o, l = ops
-        p = jnp.exp(nn_dot(kaug, q) - l[None, :])
-        dp = nn_dot(v_all, do)
-        delta = jnp.sum(do.astype(f32) * o.astype(f32), 0, keepdims=True)
-        ds = (p * (dp - delta)).astype(bf16)
-        dq = tn_dot(k_all, ds) * (HD ** (-0.5))
-        dk = nt_dot(ds, q[:HD])
-        dv = nt_dot(p.astype(bf16), do)
-        return (acc + jnp.concatenate([dk, dv], 1), dq)
-
-    dkv, dq = lax.scan(back, jnp.zeros((k_all.shape[0], 2 * HD), f32), (qaug, datt_t, att_t, lse))
-    dkv = lax.psum_scatter(dkv, "ctx", scatter_dimension=0, tiled=True)
-
-    def unrotate(v):
-        v1, v2 = v[..., :half, :], v[..., half:, :]
-        return jnp.concatenate([v1 * cos + v2 * sin, v2 * cos - v1 * sin], -2)
-
-    dkv_t = dkv.T
-    dkv_raw = jnp.concatenate([unrotate(dkv_t[:HD]), dkv_t[HD:]], 0).astype(bf16).T
-    dq_raw = unrotate(dq).astype(bf16).reshape(heads * HD, queries).T
-    grad_query = ws(tn_dot(n1, dq_raw))
-    grad_keyval = ws(tn_dot(n1, dkv_raw))
-    dn1 = rs((nt_dot(dq_raw, wq) + nt_dot(dkv_raw, wkv)).astype(bf16)).astype(f32)
-    unit1, inv1 = apply_norm(x.astype(f32))
-    ga, dres = norm_backward_pass(dn1, unit1, inv1, gains[0:1])
-    input_grad = dmid + dres
-    both = lax.psum(jnp.stack([ga, gm]), ("shard", "ctx", "tensor"))
+    (layer_out, dmid, dmid_all, grad_gate, grad_up, grad_down, gm) = middle_call(
+        shards, w_gate.shape[0], n2, og_all, wg, wu, wd, mid, gains
+    )
+    (input_grad, grad_query, grad_keyval, grad_output, both) = backward_call(
+        shards, w_query.shape[0], dmid_all, wo, wq, wkv, n1, qaug, kaug, kv, att, x, dmid,
+        lse, gains, gm, cos, sin,
+    )
     both = lax.dynamic_slice(both, (0, start), (2, gain_attn.shape[0]))
     return (
         layer_out[None], input_grad[None], both[0], grad_query, grad_keyval, grad_output,

time: 871 us -> 457 us (0.52)
  waiting for transfers between devices: 412 us -> 0 us
  Pallas kernels: 179 us -> 437 us
  matrix products: 141 us -> 0 us
  other arithmetic: 51.6 us -> 1.73 us
  blocking collectives: 45 us -> 0 us
  between operations: 14.7 us -> 0.72 us
    reduce_scatter x10 -> x0, waiting for transfers between devices: 367 us -> none  [the longest x6 276 us: body(): lax.psum_scatter(v.astype(bf16), ('shard', 'ctx'), scatter_dimension=0, t...]
    pallas_call x0 -> x2, Pallas kernels: none -> 258 us  [the longest x1 146 us: middle_call(): pl.pallas_call(functools.partial(middle_kernel, shards, rows), out_shape=...]
    dot_general x55 -> x0, matrix products: 141 us -> none  [the longest x22 53.7 us: nt_dot(): lax.dot_general(left, right, (((1,), (1,)), ((), ())), preferred_element_...]
    all_gather x1 -> x0, waiting for transfers between devices: 45.3 us -> none  [body(): dmid_all = lax.all_gather(dmid.astype(bf16), 'tensor', axis=0, tiled=True)]
    psum x1 -> x0, blocking collectives: 45 us -> none  [body(): both = lax.psum(jnp.stack([ga, gm]), ('shard', 'ctx', 'tensor'))]
    add x8 -> x0, other arithmetic: 19.5 us -> none  [back(): return (acc + jnp.concatenate([dk, dv], 1), dq)]
    convert_element_type x7 -> x0, other arithmetic: 14.2 us -> none  [the longest x6 12 us: body(): ws = lambda v: lax.psum_scatter(v.astype(bf16), ('shard', 'ctx'), scatter...]
    reduce_sum x12 -> x0, other arithmetic: 10.6 us -> none  [the longest x8 7.3 us: back(): delta = jnp.sum(do.astype(f32) * o.astype(f32), 0, keepdims=True)]
  transfers between devices with their start and end apart: 11 -> 0, of which waited for: 10 -> 0; matrix products, arithmetic and copies ran while one was open for 7% -> 0% of each run, Pallas kernels for 0% -> 0%
where the time goes in v2:
time: 457 us; the launch traced here: 453 us
  Pallas kernels  437 us (96%)
  local copies, waits for them, and re-layouts  13.7 us (3%)
    pallas_call x1, Pallas kernels, forward_call(): pl.pallas_call(functools.partial(forward_kernel, shards), out_shape=outs,...  179 us
    pallas_call x1, Pallas kernels, middle_call(): pl.pallas_call(functools.partial(middle_kernel, shards, rows), out_shape=...  146 us
    pallas_call x1, Pallas kernels, backward_call(): pl.pallas_call(functools.partial(backward_kernel, shards, rows), out_shap...  113 us
    unnamed x28, local copies, waits for them, and re-layouts  9.64 us

profile of v2, /device:TPU:9, one launch (start us, length us, event | category | flops | bytes accessed | tf_op | source)
XLA Modules:
  0.0 453.3 jit_solution(15739157832753344253)
XLA Ops:
  0.6 0.7 stack.10
  1.3 0.7 stack.9
  2.0 0.0 copy-start.7
  2.0 0.7 fusion
  2.7 0.1 broadcast_bitcast_fusion
  2.8 1.0 multiply_sine_fusion
  3.8 0.7 select_convert_fusion
  4.5 0.6 concatenate.3.bias
  5.2 0.0 copy-done.7
  5.2 178.8 %forward.1 = (bf16[2048,512]{1,0:T(8,128)(2,1)}, bf16[2048,128]{1,0:T(8,128)(2,1)}, bf16[2048,512]{1,0:T(8,128)(2,1)}, bf16[2048,1408]{1,0:T(8,128)(2,1)}, bf16[...) custom-call(bf16[128,2048]{1,0:T(8,128)(2,1)} %bitcast.15, ...), custom_call_target="tpu_custom_call" | custom-call | tf_op jit(solution)/shard_map/forward/pallas_call | solution.py:667
  184.0 145.7 %middle.1 = (bf16[128,2048]{1,0:T(8,128)(2,1)}, f32[128,2048]{1,0:T(8,128)}, bf16[512,2048]{1,0:T(8,128)(2,1)}, f32[256,1408]{1,0:T(8,128)}, f32[256,1408]{1,0:T...) custom-call(bf16[512,2048]{1,0:T(8,128)(2,1)} %get-tuple-element.38.n2_in, bf16[512,2048]{1,0:T(8,128)(2,1)} %get-tuple-element.39.og_in, ...), custom_call_target="tpu_custom_call" | custom-call | tf_op jit(solution)/shard_map/middle/pallas_call | solution.py:848
  329.7 0.0 copy-start.3
  329.7 112.7 %backward.1 = (f32[128,2048]{1,0:T(8,128)}, f32[256,512]{1,0:T(8,128)}, f32[256,128]{1,0:T(8,128)}, f32[256,512]{1,0:T(8,128)}, f32[2,2048]{1,0:T(2,128)}) custom-call(bf16[512,2048]{1,0:T(8,128)(2,1)} %get-tuple-element.46.dmid_all_in, bf16[2048,512]{1,0:T(8,128)(2,1)} %get-tuple-element.47.wo_in, bf16[2048,512]{1,0:T(8,128)(2,1)} %get-tuple-element.48.wq_in, ...), custom_call_target="tpu_custom_call" | custom-call | tf_op jit(solution)/shard_map/backward/pallas_call | solution.py:1069
  442.4 0.0 copy-start.5
  442.4 1.4 fusion.1
  443.8 0.0 copy-done.3
  443.8 0.0 copy-start.6
  443.8 0.0 copy-start.4
  443.8 0.8 copy.32
  444.6 0.0 copy-start.2
  444.6 2.4 copy.33
  447.0 0.0 copy-done.5
  447.0 0.8 copy.34
  447.8 0.0 copy-done.6
  447.8 0.0 copy-start.1
  447.8 0.7 copy.35
  448.5 0.0 copy-done.4
  448.5 0.8 copy.36
  449.3 0.0 copy-done.2
  449.3 1.1 copy.37
  450.4 0.0 copy-done.1
  450.4 0.0 copy-start
  450.4 1.1 copy.38
  451.5 0.8 copy-done
  452.2 1.1 copy.39
  (7 shorter events, 0.1 us)
Async XLA Ops:
  2.0 3.2 copy-start.7
  329.7 114.1 %copy-start.3 = (bf16[128,2048]{1,0:T(8,128)(2,1)S(1)}, bf16[128,2048]{1,0:T(8,128)(2,1)}, u32[]{:S(2)}) copy-start(bf16[128,2048]{1,0:T(8,128)(2,1)} %get-tuple-element.45) | copy-start | bytes 1572868
  442.4 4.6 %copy-start.5 = (f32[256,512]{1,0:T(8,128)S(1)}, f32[256,512]{1,0:T(8,128)}, u32[]{:S(2)}) copy-start(f32[256,512]{1,0:T(8,128)} %get-tuple-element.83) | copy-start | bytes 1572868
  443.8 4.0 copy-start.6
  443.8 4.7 %copy-start.4 = (f32[256,512]{1,0:T(8,128)S(1)}, f32[256,512]{1,0:T(8,128)}, u32[]{:S(2)}) copy-start(f32[256,512]{1,0:T(8,128)} %get-tuple-element.85) | copy-start | bytes 1572868
  444.6 4.7 %copy-start.2 = (f32[256,1408]{1,0:T(8,128)S(1)}, f32[256,1408]{1,0:T(8,128)}, u32[]{:S(2)}) copy-start(f32[256,1408]{1,0:T(8,128)} %get-tuple-element.87) | copy-start | bytes 4325380
  447.8 2.6 copy-start.1
  450.4 1.9 copy-start

commit v3 on v2

--- a/solution.py
+++ b/solution.py
@@ -14,6 +14,7 @@
 ROWS = 16
 CTX = 4
 LINE = 4
+PIECES = 2
 
 epsilon = 1e-05
 blocked = -1e30
@@ -21,6 +22,12 @@
 f32 = jnp.float32
 bf16 = jnp.bfloat16
 MESH = pl.DeviceIdType.MESH
+
+
+def place(owner):
+    return (owner + (owner + 1) // 2) % LINE if isinstance(owner, int) else lax.rem(
+        owner + (owner + 1) // 2, LINE
+    )
 
 
 def nn_dot(left, right):
@@ -152,8 +159,8 @@
 
 
 class PlaneGather:
-    def __init__(self, links, src, full):
-        self.links, self.src, self.full = links, src, full
+    def __init__(self, links, src, full, stage=None):
+        self.links, self.src, self.full, self.stage = links, src, full, stage
         self.rows = src.shape[0]
         self.first = links.slots(4 + 4 * (links.shards - 1))
 
@@ -185,7 +192,11 @@
         links.send(self.src, own, links.x_dev, self.first)
         links.send(self.src, own, links.y_dev, self.first + 1)
         self.core_send(self.src, links.c, 0)
-        self.local = links.keep(self.src, own)
+        self.local = links.keep(self.src, own if self.stage is None else self.stage)
+
+    def settle(self):
+        self.local.wait()
+        self.local = self.links.keep(self.stage, self.block(self.links.s, self.links.c))
 
     def forward(self):
         links = self.links
@@ -214,60 +225,63 @@
 
 
 class LineGather:
-    def __init__(self, links, own, full, tokens):
+    def __init__(self, links, own, full, tokens, pieces=1):
         self.links, self.own, self.full, self.tokens = links, own, full, tokens
-        self.first = links.slots(2 * (LINE - 1))
-
-    def block(self, owner):
-        return self.full.at[pl.ds(pl.multiple_of(owner * self.tokens, self.tokens), self.tokens)]
-
-    def send(self, k):
+        self.pieces, self.size = pieces, tokens // pieces
+        self.first = links.slots(2 * (LINE - 1) * pieces)
+
+    def block(self, owner, p):
+        start = pl.multiple_of(place(owner) * self.tokens + p * self.size, self.size)
+        return self.full.at[pl.ds(start, self.size)]
+
+    def slot(self, side, k, p):
+        return self.first + (side * (LINE - 1) + k - 1) * self.pieces + p
+
+    def send(self, k, p=0):
         links = self.links
         t, u = links.t, LINE - 1 - links.t
-        right, left = self.block(t - k + 1), self.block(t + k - 1)
+        own = self.own.at[pl.ds(p * self.size, self.size)]
+        right, left = self.block(t - k + 1, p), self.block(t + k - 1, p)
         links.send(
-            self.own if k == 1 else right,
+            own if k == 1 else right,
             right,
             links.right,
-            self.first + k - 1,
+            self.slot(0, k, p),
             jnp.logical_and(t >= k - 1, t < LINE - 1),
         )
         links.send(
-            self.own if k == 1 else left,
+            own if k == 1 else left,
             left,
             links.left,
-            self.first + LINE - 1 + k - 1,
+            self.slot(1, k, p),
             jnp.logical_and(u >= k - 1, u < LINE - 1),
         )
 
-    def recv(self, k, use=None):
+    def recv(self, k, p=0):
         links = self.links
         t, u = links.t, LINE - 1 - links.t
 
         @pl.when(t >= k)
         def _():
-            links.recv(self.block(t - k), self.first + k - 1)
+            links.recv(self.block(t - k, p), self.slot(0, k, p))
 
         @pl.when(u >= k)
         def _():
-            links.recv(self.block(t + k), self.first + LINE - 1 + k - 1)
-
-        if use is not None:
-
-            @pl.when(t >= k)
-            def _():
-                use(t - k)
-
-            @pl.when(u >= k)
-            def _():
-                use(t + k)
+            links.recv(self.block(t + k, p), self.slot(1, k, p))
 
 
 class LineScatter:
-    def __init__(self, links, part, tokens, from_left, from_right):
+    def __init__(self, links, part, tokens, from_left, from_right, pieces=1):
         self.links, self.part, self.tokens = links, part, tokens
         self.from_left, self.from_right = from_left, from_right
-        self.first = links.slots(2 * (LINE - 1))
+        self.pieces, self.size = pieces, tokens // pieces
+        self.first = links.slots(2 * (LINE - 1) * pieces)
+
+    def slot(self, side, k, p):
+        return self.first + (side * (LINE - 1) + k) * self.pieces + p
+
+    def piece(self, ref, k, p):
+        return ref.at[k, pl.ds(p * self.size, self.size)]
 
     def clear(self):
         for cond, ref in (
@@ -283,57 +297,59 @@
                     for k in range(LINE - 1):
                         ref[k, pl.ds(r, ROWS), :] = jnp.zeros((ROWS, ref.shape[2]), ref.dtype)
 
-    def total(self, owner, k, arrived):
-        @pl.loop(0, self.tokens // ROWS)
+    def total(self, owner, k, p, arrived):
+        @pl.loop(0, self.size // ROWS)
         def _(i):
-            r = pl.multiple_of(i * ROWS, ROWS)
-            q = pl.multiple_of(owner * self.tokens + i * ROWS, ROWS)
+            r = pl.multiple_of(p * self.size + i * ROWS, ROWS)
+            q = pl.multiple_of(place(owner) * self.tokens + p * self.size + i * ROWS, ROWS)
             mine = self.part[pl.ds(q, ROWS), :].astype(f32)
             summed = mine + arrived[k, pl.ds(r, ROWS), :].astype(f32)
             arrived[k, pl.ds(r, ROWS), :] = summed.astype(arrived.dtype)
 
-    def step(self, k):
+    def step(self, k, p=0):
         links = self.links
         t = links.t
-        slot_r, slot_l = self.first + k, self.first + LINE - 1 + k
+        slot_r, slot_l = self.slot(0, k, p), self.slot(1, k, p)
         owner_r, owner_l = LINE - 1 - k, k
+        piece_r, piece_l = self.piece(self.from_left, k, p), self.piece(self.from_right, k, p)
 
         @pl.when(t < owner_r)
         def _():
             @pl.when(t > 0)
             def _():
-                links.recv(self.from_left.at[k], slot_r)
-
-            self.total(owner_r, k, self.from_left)
-
-        links.send(self.from_left.at[k], self.from_left.at[k], links.right, slot_r, t < owner_r)
+                links.recv(piece_r, slot_r)
+
+            self.total(owner_r, k, p, self.from_left)
+
+        links.send(piece_r, piece_r, links.right, slot_r, t < owner_r)
 
         @pl.when(t > owner_l)
         def _():
             @pl.when(t < LINE - 1)
             def _():
-                links.recv(self.from_right.at[k], slot_l)
-
-            self.total(owner_l, k, self.from_right)
-
-        links.send(self.from_right.at[k], self.from_right.at[k], links.left, slot_l, t > owner_l)
-
-    def arrive(self):
+                links.recv(piece_l, slot_l)
+
+            self.total(owner_l, k, p, self.from_right)
+
+        links.send(piece_l, piece_l, links.left, slot_l, t > owner_l)
+
+    def arrive(self, p=0):
         links = self.links
         t = links.t
 
         @pl.when(t > 0)
         def _():
-            links.recv(self.from_left.at[LINE - 1 - t], self.first + LINE - 1 - t)
+            links.recv(
+                self.piece(self.from_left, LINE - 1 - t, p), self.slot(0, LINE - 1 - t, p)
+            )
 
         @pl.when(t < LINE - 1)
         def _():
-            links.recv(self.from_right.at[t], self.first + LINE - 1 + t)
-
-    def rows(self, i):
+            links.recv(self.piece(self.from_right, t, p), self.slot(1, t, p))
+
+    def rows(self, r):
         t = self.links.t
-        r = pl.multiple_of(i * ROWS, ROWS)
-        q = pl.multiple_of(t * self.tokens + i * ROWS, ROWS)
+        q = pl.multiple_of(place(t) * self.tokens + r, ROWS)
         k_l = jnp.minimum(LINE - 1 - t, LINE - 2)
         k_r = jnp.minimum(t, LINE - 2)
         zero = jnp.zeros((ROWS, self.part.shape[1]), f32)
@@ -343,6 +359,34 @@
             + jnp.where(t < LINE - 1, self.from_right[k_r, pl.ds(r, ROWS), :].astype(f32), zero)
         )
 
+    def owned(self, p, use):
+        @pl.loop(0, self.size // ROWS)
+        def _(i):
+            r = pl.multiple_of(p * self.size + i * ROWS, ROWS)
+            use(r, self.rows(r))
+
+
+def line_steps(scatter, k, hooks=()):
+    for p in range(scatter.pieces):
+        scatter.step(k, p)
+    for hook in hooks:
+        hook()
+
+
+def line_finish(scatter, use, gather=None):
+    for p in range(scatter.pieces):
+        scatter.arrive(p)
+        scatter.owned(p, use)
+        if gather is not None:
+            gather.send(1, p)
+
+
+def line_spread(gather, k):
+    for p in range(gather.pieces):
+        gather.recv(k, p)
+        if k < LINE - 1:
+            gather.send(k + 1, p)
+
 
 class PlaneScatter:
     def __init__(self, links, left, right, rows, core_in, x_in, y_in, x_last, y_last, out):
@@ -356,25 +400,33 @@
         start = pl.multiple_of(shard * (CTX * self.rows) + i * self.tile, self.tile)
         return tn_dot(self.left[:, pl.ds(start, self.tile)], self.right[...])
 
-    def other(self, step, stage):
+    @property
+    def tiles(self):
+        return CTX * self.rows // self.tile
+
+    def other(self, step, stage, part=None):
         links = self.links
         target = lax.rem(links.s + step, links.shards)
-
-        @pl.loop(0, CTX * self.rows // self.tile)
+        low, high = (0, self.tiles) if part is None else part
+
+        @pl.loop(low, high)
         def _(i):
             r = pl.multiple_of(i * self.tile, self.tile)
             stage[pl.ds(r, self.tile), :] = self.product(target, i).astype(bf16)
 
-        return links.send(
-            stage, self.core_in.at[step - 1], links.core_peer(step), self.first + step - 1
-        )
-
-    def own(self):
+        if high == self.tiles:
+            return links.send(
+                stage, self.core_in.at[step - 1], links.core_peer(step), self.first + step - 1
+            )
+
+    def own(self, part=None):
         links = self.links
-        for step in range(1, links.shards):
-            links.recv(self.core_in.at[step - 1], self.first + step - 1)
-
-        @pl.loop(0, CTX * self.rows // self.tile)
+        low, high = (0, self.tiles) if part is None else part
+        if low == 0:
+            for step in range(1, links.shards):
+                links.recv(self.core_in.at[step - 1], self.first + step - 1)
+
+        @pl.loop(low, high)
         def _(i):
             r = pl.multiple_of(i * self.tile, self.tile)
             summed = self.product(links.s, i)
@@ -461,10 +513,10 @@
 def forward_kernel(
     shards,
     x, og, wq, wkv, wo, wg, wu, wd, gpad, cos, sin, bias,
-    wq_o, wkv_o, wo_o, wg_o, wu_o, wd_o, n1_o, og_o, n2_o, mid_o, qaug_o, kaug_o, kv_o, att_o,
+    wq_o, wkv_o, wo_o, wg_o, wu_o, wd_o, n1_o, og_o, n2_o, mid_o, qaug_o, kaug_o, kv_o, att_o, x_o,
     lse, gains,
     x_all, n1_all, wq_all, wkv_all, wo_all, gains_all, qaug, kv_all, kaug, v_all, scores, weights,
-    attn, part, from_left, from_right, mid, n2,
+    attn, part, from_left, from_right, mid, n2, og_stage, wg_stage, wu_stage, wd_stage,
     send_sems, recv_sems, local_sems,
 ):
     tokens, width = x.shape
@@ -475,10 +527,13 @@
 
     gather_x = LineGather(links, x, x_all, tokens)
     gather_og = LineGather(links, og, og_o, tokens)
-    gather_n2 = LineGather(links, n2, n2_o, tokens)
+    gather_n2 = LineGather(links, n2, n2_o, tokens, PIECES)
     small = [PlaneGather(links, *pair) for pair in ((wq, wq_all), (wkv, wkv_all), (wo, wo_all))]
-    large = [PlaneGather(links, *pair) for pair in ((wg, wg_o), (wu, wu_o), (wd, wd_o))]
-    scatter = LineScatter(links, part, tokens, from_left, from_right)
+    large = [
+        PlaneGather(links, *three)
+        for three in ((wg, wg_o, wg_stage), (wu, wu_o, wu_stage), (wd, wd_o, wd_stage))
+    ]
+    scatter = LineScatter(links, part, tokens, from_left, from_right, PIECES)
     plane = shards * CTX
     gain_slot = links.slots(plane - 1)
     kv_slot = links.slots(3)
@@ -489,7 +544,8 @@
         links.send(gpad, gains_all.at[me], links.plane_peer(step), gain_slot + step - 1)
     own_gain = links.keep(gpad, gains_all.at[me])
     gather_x.send(1)
-    own_x = links.keep(x, x_all.at[pl.ds(pl.multiple_of(t * tokens, tokens), tokens)])
+    own_rows = pl.ds(pl.multiple_of(place(t) * tokens, tokens), tokens)
+    own_x = links.keep(x, x_all.at[own_rows])
     for gather in small:
         gather.start()
     scatter.clear()
@@ -506,28 +562,28 @@
     def norm_block(owner):
         @pl.loop(0, tokens // ROWS)
         def _(i):
-            r = pl.multiple_of(owner * tokens + i * ROWS, ROWS)
+            r = pl.multiple_of(place(owner) * tokens + i * ROWS, ROWS)
             v = x_all[pl.ds(r, ROWS), :].astype(f32)
             inverse = lax.rsqrt(jnp.mean(v * v, -1, keepdims=True) + epsilon)
             n1_all[pl.ds(r, ROWS), :] = (v * inverse * gains[0:1, :]).astype(bf16)
 
+    own_og = links.keep(og, og_stage)
     norm_block(t)
     gather_x.recv(1)
     gather_x.send(2)
     for gather in small:
         gather.forward()
+    large[0].start()
     norm_pair(gather_x, norm_block, 1)
-    large[0].start()
     gather_x.recv(2)
     gather_x.send(3)
+    gather_og.send(1)
     for gather in small:
         gather.diagonal()
     norm_pair(gather_x, norm_block, 2)
-    large[1].start()
-    large[2].start()
+    own_og.wait()
+    links.keep_later(og_stage, og_o.at[own_rows])
     gather_x.recv(3)
-    gather_og.send(1)
-    own_og = links.keep(og, og_o.at[pl.ds(pl.multiple_of(t * tokens, tokens), tokens)])
     norm_pair(gather_x, norm_block, 3)
     for gather in small:
         gather.done()
@@ -542,6 +598,10 @@
     for step in range(1, CTX):
         peer = lax.rem(c + step, CTX)
         links.send(kv_all.at[c], kv_all.at[c], (s, peer, t), kv_slot + step - 1)
+    large[0].settle()
+    large[0].forward()
+    large[1].start()
+    large[2].start()
 
     q_t = nn_dot(n1_all[...], wq_all[...]).T
     scale = HD ** (-0.5)
@@ -551,6 +611,7 @@
         qaug[h, half:HD, :] = ((v2 * cosine + v1 * sine).astype(bf16) * scale).astype(bf16)
         qaug[h, HD:, :] = bias[...]
     links.keep_later(n1_all, n1_o)
+    links.keep_later(x_all, x_o)
     links.keep_later(wq_all, wq_o)
     links.keep_later(wkv_all, wkv_o)
     links.keep_later(wo_all, wo_o)
@@ -561,7 +622,7 @@
     for other in range(CTX):
         row = lax.broadcasted_iota(jnp.int32, (HD, queries), 0)
         lane = lax.broadcasted_iota(jnp.int32, (HD, queries), 1)
-        mark = (row == other * (queries // BLOCK) + lane // BLOCK).astype(f32).astype(bf16)
+        mark = (row == other * (queries // BLOCK) + lax.rem(lane // tokens, 2)).astype(f32).astype(bf16)
         both = jnp.concatenate([kv_all[other, 0:HD, :], mark], 0)
         kaug[other * queries : (other + 1) * queries, :] = both.T
         v_all[:, other * queries : (other + 1) * queries] = kv_all[other, HD : 2 * HD, :]
@@ -570,63 +631,67 @@
 
     length = queries * CTX
 
-    def head(h):
-        query = qaug[h]
-        top = jnp.full((1, queries), -jnp.inf, f32)
+    side = queries // 2
+
+    def head(half, h):
+        lanes = slice(half * side, (half + 1) * side)
+        query = qaug[h, :, lanes]
+        top = jnp.full((1, side), -jnp.inf, f32)
         for b in range(0, length, BLOCK):
             block_scores = nn_dot(kaug[b : b + BLOCK, :], query)
             scores[b : b + BLOCK, :] = block_scores
             top = jnp.maximum(top, jnp.max(block_scores, 0, keepdims=True))
-        norm = jnp.zeros((1, queries), f32)
+        norm = jnp.zeros((1, side), f32)
         for b in range(0, length, BLOCK):
             exponent = jnp.exp(scores[b : b + BLOCK, :] - top)
             norm = norm + jnp.sum(exponent, 0, keepdims=True)
             weights[b : b + BLOCK, :] = exponent.astype(bf16)
         out = nn_dot(v_all[...], weights[...]) / norm
-        attn[pl.ds(pl.multiple_of(h * HD, HD), HD), :] = out.astype(bf16)
-        lse[pl.ds(h, 1), :] = top + jnp.log(norm)
-
-    pl.loop(0, heads // 2)(head)
+        attn[pl.ds(pl.multiple_of(h * HD, HD), HD), lanes] = out.astype(bf16)
+        lse[pl.ds(h, 1), lanes] = top + jnp.log(norm)
+
+    def project(half):
+        rows = slice(half * side, (half + 1) * side)
+        attn_rows = attn[:, rows].T
+        for b in range(0, width, 512):
+            part[rows, b : b + 512] = nt_dot(attn_rows, wo_all[b : b + 512, :])
+
+    pl.loop(0, heads)(functools.partial(head, 0))
     gather_og.recv(1)
     gather_og.send(2)
-    pl.loop(heads // 2, heads)(head)
+    project(0)
+    line_steps(scatter, 0)
+    large[1].settle()
+    large[2].settle()
+    pl.loop(0, heads)(functools.partial(head, 1))
+    project(1)
     links.keep_later(attn, att_o)
 
-    attn_rows = attn[...].T
-    for b in range(0, width, 512):
-        part[:, b : b + 512] = nt_dot(attn_rows, wo_all[b : b + 512, :])
-    scatter.step(0)
-    gather_og.recv(2)
-    gather_og.send(3)
-    for gather in large:
-        gather.forward()
-    scatter.step(1)
-    scatter.step(2)
-    for gather in large:
-        gather.diagonal()
-    scatter.arrive()
-
-    @pl.loop(0, tokens // ROWS)
-    def _(i):
-        r = pl.multiple_of(i * ROWS, ROWS)
-        q = pl.multiple_of(t * tokens + i * ROWS, ROWS)
-        middle = x_all[pl.ds(q, ROWS), :].astype(f32) + scatter.rows(i)
+    def finish_rows(r, summed):
+        q = pl.multiple_of(place(t) * tokens + r, ROWS)
+        middle = x_all[pl.ds(q, ROWS), :].astype(f32) + summed
         mid[pl.ds(r, ROWS), :] = middle
         inverse = lax.rsqrt(jnp.mean(middle * middle, -1, keepdims=True) + epsilon)
         n2[pl.ds(r, ROWS), :] = (middle * inverse * gains[1:2, :]).astype(bf16)
 
-    gather_n2.send(1)
-    links.keep_later(n2, n2_o.at[pl.ds(pl.multiple_of(t * tokens, tokens), tokens)])
+    line_steps(scatter, 1)
+    gather_og.recv(2)
+    gather_og.send(3)
+    large[0].diagonal()
+    line_steps(scatter, 2)
+    large[1].forward()
+    large[2].forward()
+    line_finish(scatter, finish_rows, gather_n2)
+    links.keep_later(n2, n2_o.at[own_rows])
     links.keep_later(mid, mid_o)
     gather_og.recv(3)
-    own_og.wait()
-    gather_n2.recv(1)
-    gather_n2.send(2)
+    line_spread(gather_n2, 1)
+    large[1].diagonal()
+    large[2].diagonal()
+    line_spread(gather_n2, 2)
     for gather in large:
         gather.done()
-    gather_n2.recv(2)
-    gather_n2.send(3)
-    gather_n2.recv(3)
+    line_spread(gather_n2, 3)
     links.finish()
 
 
@@ -659,16 +724,17 @@
         struct((length, 2 * HD), bf16),
         struct((CTX, 2 * HD, queries), bf16),
         struct((heads * HD, queries), bf16),
+        struct((queries, width), bf16),
         struct((heads, queries), f32),
         struct((2, width), f32),
     ]
     block = (LINE - 1, tokens, width)
-    count = 3 * 6 + 6 * (4 + 4 * (shards - 1)) + 6 + plane - 1 + 3
+    count = 12 * (1 + PIECES) + 6 * (4 + 4 * (shards - 1)) + plane - 1 + 3
     return pl.pallas_call(
         functools.partial(forward_kernel, shards),
         out_shape=outs,
         in_specs=[any_spec()] * 8 + [vmem_spec()] * 4,
-        out_specs=[any_spec()] * 14 + [vmem_spec()] * 2,
+        out_specs=[any_spec()] * 15 + [vmem_spec()] * 2,
         scratch_shapes=[
             pltpu.VMEM((queries, width), bf16),
             pltpu.VMEM((queries, width), bf16),
@@ -680,14 +746,18 @@
             pltpu.VMEM((CTX, 2 * HD, queries), bf16),
             pltpu.VMEM((length, 2 * HD), bf16),
             pltpu.VMEM((HD, length), bf16),
-            pltpu.VMEM((length, queries), f32),
-            pltpu.VMEM((length, queries), bf16),
+            pltpu.VMEM((length, queries // 2), f32),
+            pltpu.VMEM((length, queries // 2), bf16),
             pltpu.VMEM((heads * HD, queries), bf16),
             pltpu.VMEM((queries, width), f32),
             pltpu.VMEM(block, bf16),
             pltpu.VMEM(block, bf16),
             pltpu.VMEM((tokens, width), f32),
             pltpu.VMEM((tokens, width), bf16),
+            pltpu.VMEM((tokens, width), bf16),
+            pltpu.VMEM(wg.shape, bf16),
+            pltpu.VMEM(wu.shape, bf16),
+            pltpu.VMEM(wd.shape, bf16),
             pltpu.SemaphoreType.DMA((count,)),
             pltpu.SemaphoreType.DMA((count,)),
             pltpu.SemaphoreType.DMA((32,)),
@@ -702,129 +772,127 @@
 def middle_kernel(
     shards, rows,
     n2_in, og_in, wg_in, wu_in, wd_in, mid_in, gains,
-    out_o, dmid_o, dmid_all_o, gg_o, gu_o, gd_o, gain_sum,
+    dmid_o, dmid_all_o, gg_o, gd_o, branch_o, gu_part_o, gain_sum,
     n2, og, wg, wu, wd, mid, hidden, dgate, dup, part, branch,
-    left_a, right_a, left_b, right_b, dmid, dsend, layer, gain_rows,
+    left, right, dmid, dsend, gain_rows, up_in,
     *rest,
 ):
     grads, (send_sems, recv_sems, local_sems) = rest[:-3], rest[-3:]
     tokens, width = mid.shape
     queries = n2.shape[0]
     columns = wg.shape[1]
+    side = queries // 2
     links = Links(shards, send_sems, recv_sems, local_sems)
     t = links.t
-
-    loads = [
-        links.keep(src, dst)
-        for src, dst in (
-            (n2_in, n2), (wg_in, wg), (wu_in, wu), (og_in, og), (wd_in, wd), (mid_in, mid)
-        )
-    ]
-    scatter = LineScatter(links, part, tokens, left_a, right_a)
-    scatter_out = LineScatter(links, branch, tokens, left_b, right_b)
-    gather = LineGather(links, dsend, dmid_all_o, tokens)
+    own_rows = pl.ds(pl.multiple_of(place(t) * tokens, tokens), tokens)
+
+    spans = [slice(b, min(b + 256, columns)) for b in range(0, columns, 256)]
+    sides = [slice(0, side), slice(side, queries)]
+    loads = {"n2": links.keep(n2_in.at[sides[0]], n2.at[sides[0]])}
+    for index, span in enumerate(spans):
+        loads["g", index] = links.keep(wg_in.at[:, span], wg.at[:, span])
+        loads["u", index] = links.keep(wu_in.at[:, span], wu.at[:, span])
+        if index == 0:
+            loads["og"] = links.keep(og_in.at[sides[0]], og.at[sides[0]])
+        loads["d", index] = links.keep(wd_in.at[:, span], wd.at[:, span])
+    loads["n2b"] = links.keep(n2_in.at[sides[1]], n2.at[sides[1]])
+    loads["ogb"] = links.keep(og_in.at[sides[1]], og.at[sides[1]])
+    loads["mid"] = links.keep(mid_in, mid)
+    scatter = LineScatter(links, part, tokens, left, right, PIECES)
+    gather = LineGather(links, dsend, dmid_all_o, tokens, PIECES)
     down = PlaneScatter(links, og, hidden, rows, *grads[0:6])
     gate = PlaneScatter(links, n2, dgate, rows, *grads[6:12])
-    up = PlaneScatter(links, n2, dup, rows, *grads[12:18])
+    up = PlaneScatter(links, n2, dup, rows, up_in, None, None, None, None, None)
     links.barrier()
     scatter.clear()
-    scatter_out.clear()
-    for load in loads:
-        load.wait()
-
-    for b in range(0, columns, 256):
-        e = min(b + 256, columns)
-        gate_act = nn_dot(n2[...], wg[:, b:e])
-        up_act = nn_dot(n2[...], wu[:, b:e])
-        d_hidden = nn_dot(og[...], wd[:, b:e])
-        sig = jax.nn.sigmoid(gate_act)
-        silu = gate_act * sig
-        hidden[:, b:e] = (silu * up_act).astype(bf16)
-        dgate[:, b:e] = (d_hidden * up_act * sig * (1.0 + gate_act * (1.0 - sig))).astype(bf16)
-        dup[:, b:e] = (d_hidden * silu).astype(bf16)
+
+    def feed_forward(half):
+        at = sides[half]
+        for index, span in enumerate(spans):
+            if half == 0:
+                if index == 0:
+                    loads["n2"].wait()
+                loads["g", index].wait()
+                loads["u", index].wait()
+            gate_act = nn_dot(n2[at, :], wg[:, span])
+            up_act = nn_dot(n2[at, :], wu[:, span])
+            if half == 0:
+                if index == 0:
+                    loads["og"].wait()
+                loads["d", index].wait()
+            d_hidden = nn_dot(og[at, :], wd[:, span])
+            sig = jax.nn.sigmoid(gate_act)
+            silu = gate_act * sig
+            hidden[at, span] = (silu * up_act).astype(bf16)
+            d_gate = d_hidden * up_act * sig * (1.0 + gate_act * (1.0 - sig))
+            dgate[at, span] = d_gate.astype(bf16)
+            dup[at, span] = (d_hidden * silu).astype(bf16)
+
+        @pl.loop(0, width // 512)
+        def _(j):
+            of = pl.ds(pl.multiple_of(j * 512, 512), 512)
+            summed = nt_dot(dgate[at, :], wg[of, :]) + nt_dot(dup[at, :], wu[of, :])
+            part[at, of] = summed.astype(bf16)
+
+    feed_forward(0)
+    line_steps(scatter, 0)
+    loads["n2b"].wait()
+    loads["ogb"].wait()
+    feed_forward(1)
+    line_steps(scatter, 1)
 
     @pl.loop(0, width // 512)
     def _(j):
-        at = pl.ds(pl.multiple_of(j * 512, 512), 512)
-        part[:, at] = (nt_dot(dgate[...], wg[at, :]) + nt_dot(dup[...], wu[at, :])).astype(bf16)
-
-    scatter.step(0)
-
-    @pl.loop(0, width // 512)
-    def _(j):
-        at = pl.ds(pl.multiple_of(j * 512, 512), 512)
-        branch[:, at] = nt_dot(hidden[...], wd[at, :]).astype(bf16)
+        of = pl.ds(pl.multiple_of(j * 512, 512), 512)
+        branch[:, of] = nt_dot(hidden[...], wd[of, :]).astype(bf16)
+
+    links.keep_later(branch, branch_o)
 
     piece = CTX * rows
-    room = (width // piece) // (shards - 1)
-
-    def others(grad, index, before):
-        handles = []
+
+    def others(grad, room):
         for step in range(1, shards):
-            at = ((index % room) * (shards - 1) + step - 1) * piece
-            if before:
-                links.sent(before[step - 1])
-            handles.append(grad.other(step, wd.at[pl.ds(at, piece)]))
-        return handles
-
-    held = [others(down, 0, None)]
-    held.append(others(gate, 1, held[1 - room] if room <= 1 else None))
-    scatter.step(1)
+            grad.other(step, room.at[pl.ds((step - 1) * piece, piece)])
+
+    others(down, wd)
+    line_steps(scatter, 2)
+    others(gate, wg)
     down.own()
     down.exchange()
-    gate.own()
-    gate.exchange()
-    others(up, 2, held[2 - room] if room <= 2 else None)
-    scatter.step(2)
-    up.own()
-    up.exchange()
-    scatter.arrive()
+    loads["mid"].wait()
     gain_rows[...] = jnp.zeros_like(gain_rows)
 
-    @pl.loop(0, tokens // ROWS)
-    def _(i):
-        r = pl.ds(pl.multiple_of(i * ROWS, ROWS), ROWS)
-        q = pl.ds(pl.multiple_of(t * tokens + i * ROWS, ROWS), ROWS)
-        middle = mid[r, :]
+    def finish_rows(r, d_normed):
+        at = pl.ds(r, ROWS)
+        q = pl.ds(pl.multiple_of(place(t) * tokens + r, ROWS), ROWS)
+        middle = mid[at, :]
         inverse = lax.rsqrt(jnp.mean(middle * middle, -1, keepdims=True) + epsilon)
         unit = middle * inverse
-        d_normed = scatter.rows(i)
         gain_rows[...] += d_normed * unit
         d_unit = d_normed * gains[1:2, :]
         back = inverse * (d_unit - unit * jnp.mean(d_unit * unit, -1, keepdims=True))
         d_middle = og[q, :].astype(f32) + back
-        dmid[r, :] = d_middle
-        dsend[r, :] = d_middle.astype(bf16)
-
-    gather.send(1)
-    scatter_out.step(0)
-    links.keep_later(dsend, dmid_all_o.at[pl.ds(pl.multiple_of(t * tokens, tokens), tokens)])
+        dmid[at, :] = d_middle
+        dsend[at, :] = d_middle.astype(bf16)
+
+    line_finish(scatter, finish_rows, gather)
+    links.keep_later(dsend, dmid_all_o.at[own_rows])
     links.keep_later(dmid, dmid_o)
+    gate.own()
+    gate.exchange()
+    others(up, wu)
     gain_sum[...] = jnp.sum(gain_rows[...], 0, keepdims=True)
+    line_spread(gather, 1)
+    up.own()
+    links.keep_later(up_in.at[0], gu_part_o)
+    line_spread(gather, 2)
     down.fold()
-    gather.recv(1)
-    gather.send(2)
-    scatter_out.step(1)
+    line_spread(gather, 3)
     gate.fold()
-    gather.recv(2)
-    gather.send(3)
-    scatter_out.step(2)
-    up.fold()
     down.total()
     links.keep_later(down.out, gd_o)
     gate.total()
     links.keep_later(gate.out, gg_o)
-    scatter_out.arrive()
-
-    @pl.loop(0, tokens // ROWS)
-    def _(i):
-        r = pl.ds(pl.multiple_of(i * ROWS, ROWS), ROWS)
-        layer[r, :] = (mid[r, :] + scatter_out.rows(i)).astype(bf16)
-
-    links.keep_later(layer, out_o)
-    gather.recv(3)
-    up.total()
-    links.keep_later(up.out, gu_o)
     links.finish()
 
 
@@ -836,15 +904,15 @@
     wide = (queries, columns)
     block = (LINE - 1,) + token
     outs = [
-        struct(token, bf16),
         struct(token, f32),
         struct((queries, width), bf16),
         struct((rows, columns), f32),
         struct((rows, columns), f32),
-        struct((rows, columns), f32),
+        struct((queries, width), bf16),
+        struct((CTX * rows, columns), bf16),
         struct((1, width), f32),
     ]
-    count = 3 * 6 + 3 * (shards - 1 + 6)
+    count = 12 * PIECES + 3 * (shards - 1 + 6)
     return pl.pallas_call(
         functools.partial(middle_kernel, shards, rows),
         out_shape=outs,
@@ -864,18 +932,15 @@
             pltpu.VMEM((queries, width), bf16),
             pltpu.VMEM(block, bf16),
             pltpu.VMEM(block, bf16),
-            pltpu.VMEM(block, bf16),
-            pltpu.VMEM(block, bf16),
             pltpu.VMEM(token, f32),
             pltpu.VMEM(token, bf16),
-            pltpu.VMEM(token, bf16),
             pltpu.VMEM((ROWS, width), f32),
-            *PlaneScatter.scratch(shards, rows, columns),
+            pltpu.VMEM((shards - 1, CTX * rows, columns), bf16),
             *PlaneScatter.scratch(shards, rows, columns),
             *PlaneScatter.scratch(shards, rows, columns),
             pltpu.SemaphoreType.DMA((count,)),
             pltpu.SemaphoreType.DMA((count,)),
-            pltpu.SemaphoreType.DMA((16,)),
+            pltpu.SemaphoreType.DMA((40,)),
         ],
         compiler_params=pltpu.CompilerParams(
             collective_id=1, has_side_effects=True, vmem_limit_bytes=63 * 2**20
@@ -887,15 +952,16 @@
 def backward_kernel(
     shards, rows,
     dmid_all_in, wo_in, wq_in, wkv_in, n1_in, qaug_in, kaug_in, kv_in, att_in, x_in, dmid_in,
-    lse, gains, gain_mlp, cos, sin,
-    in_o, gq_o, gkv_o, go_o, gain_o,
+    branch_in, gu_part_in, mid_in, lse, gains, gain_mlp, cos, sin,
+    in_o, gq_o, gkv_o, go_o, gu_o, out_o, gain_o,
     dmid_all, wo, wq, wkv, n1, qaug, kaug, kv, att, x, dmid,
     d_out, attn_rows, v_rows, d_keys, d_values, d_query, d_query_rows, kv_send, kv_recv, d_kv, part,
     left, right, gain_rows, pair, plane_in, line_in, total, stage_o, stage_q, stage_kv,
+    branch, left_b, right_b, mid, layer,
     *rest,
 ):
     grads, (send_sems, recv_sems, local_sems) = rest[:-3], rest[-3:]
-    tokens, width = x.shape
+    tokens, width = dmid.shape
     queries = n1.shape[0]
     heads = qaug.shape[0]
     length = kaug.shape[0]
@@ -904,21 +970,24 @@
     links = Links(shards, send_sems, recv_sems, local_sems)
     s, c, t = links.s, links.c, links.t
 
-    loads = [
-        links.keep(src, dst)
-        for src, dst in (
-            (dmid_all_in, dmid_all), (wo_in, wo), (att_in, att), (kv_in, kv), (qaug_in, qaug),
-            (kaug_in, kaug), (n1_in, n1), (wq_in, wq), (wkv_in, wkv), (x_in, x), (dmid_in, dmid),
-        )
-    ]
-    scatter = LineScatter(links, part, tokens, left, right)
+    scatter = LineScatter(links, part, tokens, left, right, PIECES)
+    scatter_out = LineScatter(links, branch, tokens, left_b, right_b)
     g_o = PlaneScatter(links, dmid_all, attn_rows, rows, *grads[0:6])
     g_q = PlaneScatter(links, n1, d_query_rows, rows, *grads[6:12])
     g_kv = PlaneScatter(links, n1, d_kv, rows, *grads[12:18])
+    g_u = PlaneScatter(links, None, None, rows, *grads[18:24])
     kv_slot = links.slots(CTX - 1)
     plane_slot = links.slots(plane - 1)
     line_slot = links.slots(LINE - 1)
     piece = CTX * rows
+    loads = [
+        links.keep(src, dst)
+        for src, dst in (
+            (branch_in, branch), (dmid_all_in, dmid_all), (wo_in, wo), (gu_part_in, g_u.core_in.at[0]),
+            (att_in, att), (kv_in, kv), (qaug_in, qaug), (kaug_in, kaug), (n1_in, n1), (wq_in, wq),
+            (wkv_in, wkv), (x_in, x), (dmid_in, dmid), (mid_in, mid),
+        )
+    ]
 
     def others(grad, stage):
         for step in range(1, shards):
@@ -926,10 +995,16 @@
 
     links.barrier(whole_line=True)
     scatter.clear()
-    for load in loads:
+    scatter_out.clear()
+    loads[0].wait()
+    scatter_out.step(0)
+    for load in loads[1:3]:
         load.wait()
-
     d_out[...] = nn_dot(dmid_all[...], wo[...]).astype(bf16).T
+    loads[3].wait()
+    g_u.exchange()
+    for load in loads[4:8]:
+        load.wait()
     attn_rows[...] = att[...].T
     for other in range(CTX):
         v_rows[other * queries : (other + 1) * queries, :] = kv[other, HD : 2 * HD, :].T
@@ -955,11 +1030,13 @@
             d_q = d_q + nn_dot(kv[b // queries, 0:HD, at_b : at_b + BLOCK], d_scores)
         d_query[at, :] = d_q * (HD ** (-0.5))
 
-    pl.loop(0, heads // 2)(head)
+    quarter = heads // 4
+    pl.loop(0, quarter)(head)
     g_o.own()
     g_o.exchange()
-    pl.loop(heads // 2, heads)(head)
-    g_o.fold()
+    pl.loop(quarter, 2 * quarter)(head)
+    scatter_out.step(1)
+    pl.loop(2 * quarter, heads)(head)
 
     for other in range(CTX):
         block = slice(other * queries, (other + 1) * queries)
@@ -968,6 +1045,9 @@
     for step in range(1, CTX):
         peer = lax.rem(c + step, CTX)
         links.send(kv_send.at[peer], kv_recv.at[step - 1], (s, peer, t), kv_slot + step - 1)
+    scatter_out.step(2)
+    for load in loads[8:]:
+        load.wait()
 
     cosine, sine = cos[...], sin[...]
     for h in range(heads):
@@ -995,42 +1075,27 @@
         summed = nt_dot(d_query_rows[...], wq[at, :]) + nt_dot(d_kv[...], wkv[at, :])
         part[:, at] = summed.astype(bf16)
 
-    scatter.step(0)
-    others(g_kv, stage_kv)
-    g_q.own()
-    g_q.exchange()
-    g_kv.own()
-    g_kv.exchange()
-    g_o.total()
-    links.keep_later(g_o.out, go_o)
-    scatter.step(1)
-    g_q.fold()
-    g_kv.fold()
-    scatter.step(2)
-    g_q.total()
-    links.keep_later(g_q.out, gq_o)
-    g_kv.total()
-    links.keep_later(g_kv.out, gkv_o)
+    line_steps(scatter, 0)
+    g_u.fold()
+    g_o.fold()
+
     gain_rows[...] = jnp.zeros_like(gain_rows)
-    scatter.arrive()
-
-    @pl.loop(0, tokens // ROWS)
+
+    @pl.loop(0, queries // ROWS)
     def _(i):
         r = pl.ds(pl.multiple_of(i * ROWS, ROWS), ROWS)
         v = x[r, :].astype(f32)
         inverse = lax.rsqrt(jnp.mean(v * v, -1, keepdims=True) + epsilon)
-        unit = v * inverse
-        d_normed = scatter.rows(i)
-        gain_rows[...] += d_normed * unit
-        d_unit = d_normed * gains[0:1, :]
-        back = inverse * (d_unit - unit * jnp.mean(d_unit * unit, -1, keepdims=True))
-        dmid[r, :] = dmid[r, :] + back
+        gain_rows[...] += part[r, :].astype(f32) * (v * inverse)
 
     pair[0:1, :] = jnp.sum(gain_rows[...], 0, keepdims=True)
     pair[1:2, :] = gain_mlp[...]
     for step in range(1, plane):
         links.send(pair, plane_in.at[step - 1], links.plane_peer(step), plane_slot + step - 1)
-    links.keep_later(dmid, in_o)
+    others(g_kv, stage_kv)
+    g_q.own()
+    g_q.exchange()
+    line_steps(scatter, 1)
     summed = pair[...]
     for step in range(1, plane):
         links.recv(plane_in.at[step - 1], plane_slot + step - 1)
@@ -1038,6 +1103,39 @@
     total[...] = summed
     for step in range(1, LINE):
         links.send(total, line_in.at[step - 1], links.line_peer(step), line_slot + step - 1)
+    g_kv.own()
+    g_kv.exchange()
+    line_steps(scatter, 2)
+    scatter_out.arrive()
+
+    def layer_rows(r, total_rows):
+        layer[pl.ds(r, ROWS), :] = (mid[pl.ds(r, ROWS), :] + total_rows).astype(bf16)
+
+    scatter_out.owned(0, layer_rows)
+    links.keep_later(layer, out_o)
+    g_o.total()
+    links.keep_later(g_o.out, go_o)
+    g_q.fold()
+    g_kv.fold()
+
+    def finish_rows(r, d_normed):
+        at = pl.ds(r, ROWS)
+        q = pl.ds(pl.multiple_of(place(t) * tokens + r, ROWS), ROWS)
+        v = x[q, :].astype(f32)
+        inverse = lax.rsqrt(jnp.mean(v * v, -1, keepdims=True) + epsilon)
+        unit = v * inverse
+        d_unit = d_normed * gains[0:1, :]
+        back = inverse * (d_unit - unit * jnp.mean(d_unit * unit, -1, keepdims=True))
+        dmid[at, :] = dmid[at, :] + back
+
+    line_finish(scatter, finish_rows)
+    links.keep_later(dmid, in_o)
+    g_u.total()
+    links.keep_later(g_u.out, gu_o)
+    g_q.total()
+    links.keep_later(g_q.out, gq_o)
+    g_kv.total()
+    links.keep_later(g_kv.out, gkv_o)
     for step in range(1, LINE):
         links.recv(line_in.at[step - 1], line_slot + step - 1)
         summed = summed + line_in[step - 1]
@@ -1046,14 +1144,15 @@
 
 
 def backward_call(
-    shards, rows, dmid_all, wo, wq, wkv, n1, qaug, kaug, kv, att, x, dmid, lse, gains, gain_mlp,
-    cos, sin,
+    shards, rows, dmid_all, wo, wq, wkv, n1, qaug, kaug, kv, att, x, dmid, branch, gu_part, mid,
+    lse, gains, gain_mlp, cos, sin,
 ):
-    tokens, width = x.shape
+    tokens, width = dmid.shape
     queries = n1.shape[0]
     heads = qaug.shape[0]
     length = kaug.shape[0]
     inner = heads * HD
+    columns = gu_part.shape[1]
     plane = shards * CTX
     piece = CTX * rows * (shards - 1)
     token = (tokens, width)
@@ -1063,14 +1162,16 @@
         struct((rows, inner), f32),
         struct((rows, 2 * HD), f32),
         struct((rows, inner), f32),
+        struct((rows, columns), f32),
+        struct(token, bf16),
         struct((2, width), f32),
     ]
-    count = 6 + 3 * (shards - 1 + 6) + CTX - 1 + plane - 1 + LINE - 1
+    count = 6 + 6 * PIECES + 4 * (shards - 1 + 6) + CTX - 1 + plane - 1 + LINE - 1
     return pl.pallas_call(
         functools.partial(backward_kernel, shards, rows),
         out_shape=outs,
-        in_specs=[any_spec()] * 11 + [vmem_spec()] * 5,
-        out_specs=[any_spec()] * 4 + [vmem_spec()],
+        in_specs=[any_spec()] * 14 + [vmem_spec()] * 5,
+        out_specs=[any_spec()] * 6 + [vmem_spec()],
         scratch_shapes=[
             pltpu.VMEM((queries, width), bf16),
             pltpu.VMEM((width, inner), bf16),
@@ -1081,7 +1182,7 @@
             pltpu.VMEM(kaug.shape, bf16),
             pltpu.VMEM(kv.shape, bf16),
             pltpu.VMEM((inner, queries), bf16),
-            pltpu.VMEM(token, bf16),
+            pltpu.VMEM((queries, width), bf16),
             pltpu.VMEM(token, f32),
             pltpu.VMEM((inner, queries), bf16),
             pltpu.VMEM((queries, inner), bf16),
@@ -1104,19 +1205,26 @@
             pltpu.VMEM((piece, inner), bf16),
             pltpu.VMEM((piece, inner), bf16),
             pltpu.VMEM((piece, 2 * HD), bf16),
+            pltpu.VMEM((queries, width), bf16),
+            pltpu.VMEM(block, bf16),
+            pltpu.VMEM(block, bf16),
+            pltpu.VMEM(token, f32),
+            pltpu.VMEM(token, bf16),
             *PlaneScatter.scratch(shards, rows, inner),
             *PlaneScatter.scratch(shards, rows, inner),
             *PlaneScatter.scratch(shards, rows, 2 * HD),
+            *PlaneScatter.scratch(1 + 1, rows, columns),
             pltpu.SemaphoreType.DMA((count,)),
             pltpu.SemaphoreType.DMA((count,)),
-            pltpu.SemaphoreType.DMA((16,)),
+            pltpu.SemaphoreType.DMA((32,)),
         ],
         compiler_params=pltpu.CompilerParams(
             collective_id=2, has_side_effects=True, vmem_limit_bytes=60 * 2**20
         ),
         name="backward",
     )(
-        dmid_all, wo, wq, wkv, n1, qaug, kaug, kv, att, x, dmid, lse, gains, gain_mlp, cos, sin
+        dmid_all, wo, wq, wkv, n1, qaug, kaug, kv, att, x, dmid, branch, gu_part, mid,
+        lse, gains, gain_mlp, cos, sin,
     )
 
 
@@ -1130,9 +1238,11 @@
     order = block_order[0]
     s, c = lax.axis_index("shard"), lax.axis_index("ctx")
     per = queries // BLOCK
+    owners = [owner for at in range(LINE) for owner in range(LINE) if place(owner) == at]
+    slots = np.concatenate([owner * tokens + np.arange(tokens) for owner in owners])
     here = lax.dynamic_slice_in_dim(order, c * per, per)
-    block_here = jnp.repeat(here, BLOCK)
-    position = block_here * BLOCK + jnp.tile(jnp.arange(BLOCK, dtype=jnp.int32), per)
+    block_here = sum(jnp.where(slots // BLOCK == i, here[i], 0) for i in range(per))
+    position = block_here * BLOCK + (slots % BLOCK).astype(np.int32)
     half = HD // 2
     frequency = 10000.0 ** (-jnp.arange(half, dtype=f32) * 2.0 / HD)
     angles = frequency[:, None] * position.astype(f32)[None, :]
@@ -1143,15 +1253,15 @@
     gpad = lax.dynamic_update_slice(
         jnp.zeros((2, width), f32), jnp.stack([gain_attn, gain_mlp]).astype(f32), (0, start)
     )
-    (wq, wkv, wo, wg, wu, wd, n1, og_all, n2, mid, qaug, kaug, kv, att, lse, gains) = forward_call(
+    (wq, wkv, wo, wg, wu, wd, n1, og_all, n2, mid, qaug, kaug, kv, att, x_all, lse, gains) = forward_call(
         shards, x, og, (w_query, w_keyval, w_output, w_gate, w_up, w_down), gpad, cos, sin, bias
     )
-    (layer_out, dmid, dmid_all, grad_gate, grad_up, grad_down, gm) = middle_call(
+    (dmid, dmid_all, grad_gate, grad_down, branch, gu_part, gm) = middle_call(
         shards, w_gate.shape[0], n2, og_all, wg, wu, wd, mid, gains
     )
-    (input_grad, grad_query, grad_keyval, grad_output, both) = backward_call(
-        shards, w_query.shape[0], dmid_all, wo, wq, wkv, n1, qaug, kaug, kv, att, x, dmid,
-        lse, gains, gm, cos, sin,
+    (input_grad, grad_query, grad_keyval, grad_output, grad_up, layer_out, both) = backward_call(
+        shards, w_query.shape[0], dmid_all, wo, wq, wkv, n1, qaug, kaug, kv, att, x_all, dmid,
+        branch, gu_part, mid, lse, gains, gm, cos, sin,
     )
     both = lax.dynamic_slice(both, (0, start), (2, gain_attn.shape[0]))
     return (

time: 457 us -> 423 us (0.926)
  Pallas kernels: 437 us -> 396 us
    pallas_call x1, Pallas kernels: 179 us -> 142 us  [forward_call(): pl.pallas_call(functools.partial(forward_kernel, shards), out_shape=outs,...]
    pallas_call x1, Pallas kernels: 146 us -> 128 us  [middle_call(): pl.pallas_call(functools.partial(middle_kernel, shards, rows), out_shape=...]
    pallas_call x1, Pallas kernels: 113 us -> 126 us  [backward_call(): pl.pallas_call(functools.partial(backward_kernel, shards, rows), out_shap...]
    unnamed x28 -> x22, local copies, waits for them, and re-layouts: 9.64 us -> 11.3 us
where the time goes in v3:
time: 423 us; the launch traced here: 416 us
  Pallas kernels  396 us (94%)
  local copies, waits for them, and re-layouts  16 us (4%)
    pallas_call x1, Pallas kernels, forward_call(): pl.pallas_call(functools.partial(forward_kernel, shards), out_shape=outs,...  142 us
    pallas_call x1, Pallas kernels, middle_call(): pl.pallas_call(functools.partial(middle_kernel, shards, rows), out_shape=...  128 us
    pallas_call x1, Pallas kernels, backward_call(): pl.pallas_call(functools.partial(backward_kernel, shards, rows), out_shap...  126 us
    unnamed x22, local copies, waits for them, and re-layouts  11.3 us

profile of v3, /device:TPU:9, one launch (start us, length us, event | category | flops | bytes accessed | tf_op | source)
XLA Modules:
  0.0 416.4 jit_solution(18190597737138262298)
XLA Ops:
  0.6 0.7 constant_dynamic-slice_fusion.1
  1.4 0.6 fusion.1
  2.0 2.0 select_add_fusion
  4.0 1.0 multiply_sine_fusion
  5.0 0.7 select_convert_fusion
  5.7 0.6 concatenate.3.bias
  6.3 0.7 stack.10
  7.0 0.7 stack.9
  7.7 0.0 copy-start.6
  7.7 0.6 copy-done.6
  8.3 141.7 %forward.1 = (bf16[2048,512]{1,0:T(8,128)(2,1)}, bf16[2048,128]{1,0:T(8,128)(2,1)}, bf16[2048,512]{1,0:T(8,128)(2,1)}, bf16[2048,1408]{1,0:T(8,128)(2,1)}, bf16[...) custom-call(bf16[128,2048]{1,0:T(8,128)(2,1)} %bitcast.10, ...), custom_call_target="tpu_custom_call" | custom-call | tf_op jit(solution)/shard_map/forward/pallas_call | solution.py:733
  150.0 127.5 %middle.1 = (f32[128,2048]{1,0:T(8,128)}, bf16[512,2048]{1,0:T(8,128)(2,1)}, f32[256,1408]{1,0:T(8,128)}, f32[256,1408]{1,0:T(8,128)}, bf16[512,2048]{1,0:T(8,12...) custom-call(bf16[512,2048]{1,0:T(8,128)(2,1)} %get-tuple-element.41.n2_in, ...), custom_call_target="tpu_custom_call" | custom-call | tf_op jit(solution)/shard_map/middle/pallas_call | solution.py:916
  277.5 126.3 %backward.1 = (f32[128,2048]{1,0:T(8,128)}, f32[256,512]{1,0:T(8,128)}, f32[256,128]{1,0:T(8,128)}, f32[256,512]{1,0:T(8,128)}, f32[256,1408]{1,0:T(8,128)}, /*i...) custom-call(bf16[512,2048]{1,0:T(8,128)(2,1)} %get-tuple-element.48.dmid_all_in, bf16[2048,512]{1,0:T(8,128)(2,1)} %get-tuple-element.49.wo_in, ...), custom_call_target="tpu_custom_call" | custom-call | tf_op jit(solution)/shard_map/backward/pallas_call | solution.py:1170
  403.8 0.0 copy-start.4
  403.8 1.4 fusion
  405.2 0.0 copy-start.5
  405.2 0.0 copy-start.3
  405.2 1.9 copy.33
  407.2 0.0 copy-start.1
  407.2 2.4 copy.34
  409.6 0.0 copy-done.4
  409.6 0.8 copy.35
  410.4 0.0 copy-done.5
  410.4 0.0 copy-start.2
  410.4 0.7 copy.36
  411.0 0.0 copy-done.3
  411.0 0.8 copy.37
  411.8 0.0 copy-done.1
  411.8 1.1 copy.38
  412.9 0.0 copy-done.2
  412.9 0.0 copy-start
  412.9 1.1 copy.39
  414.0 0.8 copy-done
  414.8 1.1 copy.40
  (3 shorter events, 0.0 us)
Async XLA Ops:
  7.7 0.6 copy-start.6
  403.8 5.8 %copy-start.4 = (f32[256,512]{1,0:T(8,128)S(1)}, f32[256,512]{1,0:T(8,128)}, u32[]{:S(2)}) copy-start(f32[256,512]{1,0:T(8,128)} %get-tuple-element.93) | copy-start | bytes 1572868
  405.2 5.2 %copy-start.5 = (f32[256,128]{1,0:T(8,128)S(1)}, f32[256,128]{1,0:T(8,128)}, u32[]{:S(2)}) copy-start(f32[256,128]{1,0:T(8,128)} %get-tuple-element.94) | copy-start | bytes 393220
  405.2 5.8 %copy-start.3 = (f32[256,512]{1,0:T(8,128)S(1)}, f32[256,512]{1,0:T(8,128)}, u32[]{:S(2)}) copy-start(f32[256,512]{1,0:T(8,128)} %get-tuple-element.95) | copy-start | bytes 1572868
  407.2 4.7 %copy-start.1 = (f32[256,1408]{1,0:T(8,128)S(1)}, f32[256,1408]{1,0:T(8,128)}, u32[]{:S(2)}) copy-start(f32[256,1408]{1,0:T(8,128)} %get-tuple-element.97) | copy-start | bytes 4325380
  410.4 2.6 copy-start.2
  412.9 1.9 copy-start

commit v4 on v3

--- a/solution.py
+++ b/solution.py
@@ -306,32 +306,26 @@
             summed = mine + arrived[k, pl.ds(r, ROWS), :].astype(f32)
             arrived[k, pl.ds(r, ROWS), :] = summed.astype(arrived.dtype)
 
-    def step(self, k, p=0):
+    def stage(self, now, p=0):
         links = self.links
-        t = links.t
-        slot_r, slot_l = self.slot(0, k, p), self.slot(1, k, p)
-        owner_r, owner_l = LINE - 1 - k, k
-        piece_r, piece_l = self.piece(self.from_left, k, p), self.piece(self.from_right, k, p)
-
-        @pl.when(t < owner_r)
-        def _():
-            @pl.when(t > 0)
+        t, u = links.t, LINE - 1 - links.t
+        for side, behind, arrived, device in (
+            (0, t, self.from_left, links.right),
+            (1, u, self.from_right, links.left),
+        ):
+            k = now - behind
+            owner = LINE - 1 - k if side == 0 else k
+            piece, slot = self.piece(arrived, k, p), self.slot(side, k, p)
+
+            @pl.when(k >= 0)
             def _():
-                links.recv(piece_r, slot_r)
-
-            self.total(owner_r, k, p, self.from_left)
-
-        links.send(piece_r, piece_r, links.right, slot_r, t < owner_r)
-
-        @pl.when(t > owner_l)
-        def _():
-            @pl.when(t < LINE - 1)
-            def _():
-                links.recv(piece_l, slot_l)
-
-            self.total(owner_l, k, p, self.from_right)
-
-        links.send(piece_l, piece_l, links.left, slot_l, t > owner_l)
+                @pl.when(behind > 0)
+                def _():
+                    links.recv(piece, slot)
+
+                self.total(owner, k, p, arrived)
+
+            links.send(piece, piece, device, slot, k >= 0)
 
     def arrive(self, p=0):
         links = self.links
@@ -368,7 +362,7 @@
 
 def line_steps(scatter, k, hooks=()):
     for p in range(scatter.pieces):
-        scatter.step(k, p)
+        scatter.stage(k, p)
     for hook in hooks:
         hook()
 
@@ -512,9 +506,9 @@
 
 def forward_kernel(
     shards,
-    x, og, wq, wkv, wo, wg, wu, wd, gpad, cos, sin, bias,
+    x, og, wq, wkv, wo, wg, wu, wd, gpad, frequency, order,
     wq_o, wkv_o, wo_o, wg_o, wu_o, wd_o, n1_o, og_o, n2_o, mid_o, qaug_o, kaug_o, kv_o, att_o, x_o,
-    lse, gains,
+    lse, gains, cos, sin,
     x_all, n1_all, wq_all, wkv_all, wo_all, gains_all, qaug, kv_all, kaug, v_all, scores, weights,
     attn, part, from_left, from_right, mid, n2, og_stage, wg_stage, wu_stage, wd_stage,
     send_sems, recv_sems, local_sems,
@@ -549,6 +543,29 @@
     for gather in small:
         gather.start()
     scatter.clear()
+
+    per = queries // BLOCK
+    lane = lax.broadcasted_iota(jnp.int32, (1, queries), 1)
+    owner = jnp.zeros((1, queries), jnp.int32)
+    for index in range(LINE):
+        owner = jnp.where(lane // tokens == place(index), index, owner)
+    slot = owner * tokens + lax.rem(lane, tokens)
+    block_here = jnp.zeros((1, queries), jnp.int32)
+    for index in range(per):
+        block_here = jnp.where(slot // BLOCK == index, order[c * per + index], block_here)
+    position = (block_here * BLOCK + lax.rem(slot, BLOCK)).astype(f32)
+    angles = frequency[...] * position
+    cos[...] = jnp.cos(angles)
+    sin[...] = jnp.sin(angles)
+    row = lax.broadcasted_iota(jnp.int32, (HD, queries), 0)
+    bias = jnp.zeros((HD, queries), f32)
+    for index in range(BLOCKS):
+        barred = jnp.logical_and(row == index, order[index] > block_here)
+        bias = jnp.where(barred, blocked, bias)
+    bias = bias.astype(bf16)
+    for h in range(heads):
+        qaug[h, HD:, :] = bias
+
     own_gain.wait()
     for step in range(1, plane):
         other = lax.rem(me + plane - step, plane)
@@ -609,7 +626,6 @@
         v1, v2 = q_t[h * HD : h * HD + half], q_t[h * HD + half : (h + 1) * HD]
         qaug[h, 0:half, :] = ((v1 * cosine - v2 * sine).astype(bf16) * scale).astype(bf16)
         qaug[h, half:HD, :] = ((v2 * cosine + v1 * sine).astype(bf16) * scale).astype(bf16)
-        qaug[h, HD:, :] = bias[...]
     links.keep_later(n1_all, n1_o)
     links.keep_later(x_all, x_o)
     links.keep_later(wq_all, wq_o)
@@ -656,9 +672,11 @@
         for b in range(0, width, 512):
             part[rows, b : b + 512] = nt_dot(attn_rows, wo_all[b : b + 512, :])
 
-    pl.loop(0, heads)(functools.partial(head, 0))
     gather_og.recv(1)
     gather_og.send(2)
+    pl.loop(0, heads)(functools.partial(head, 0))
+    gather_og.recv(2)
+    gather_og.send(3)
     project(0)
     line_steps(scatter, 0)
     large[1].settle()
@@ -675,23 +693,21 @@
         n2[pl.ds(r, ROWS), :] = (middle * inverse * gains[1:2, :]).astype(bf16)
 
     line_steps(scatter, 1)
-    gather_og.recv(2)
-    gather_og.send(3)
     large[0].diagonal()
     line_steps(scatter, 2)
-    large[1].forward()
-    large[2].forward()
     line_finish(scatter, finish_rows, gather_n2)
     links.keep_later(n2, n2_o.at[own_rows])
     links.keep_later(mid, mid_o)
-    gather_og.recv(3)
+    large[1].forward()
+    large[2].forward()
     line_spread(gather_n2, 1)
+    line_spread(gather_n2, 2)
     large[1].diagonal()
     large[2].diagonal()
-    line_spread(gather_n2, 2)
+    gather_og.recv(3)
+    line_spread(gather_n2, 3)
     for gather in large:
         gather.done()
-    line_spread(gather_n2, 3)
     links.finish()
 
 
@@ -707,7 +723,7 @@
         norm_block(t + k)
 
 
-def forward_call(shards, x, og, weights_in, gpad, cos, sin, bias):
+def forward_call(shards, x, og, weights_in, gpad, frequency, order):
     wq, wkv, wo, wg, wu, wd = weights_in
     tokens, width = x.shape
     queries = tokens * LINE
@@ -727,14 +743,18 @@
         struct((queries, width), bf16),
         struct((heads, queries), f32),
         struct((2, width), f32),
+        struct((HD // 2, queries), f32),
+        struct((HD // 2, queries), f32),
     ]
     block = (LINE - 1, tokens, width)
     count = 12 * (1 + PIECES) + 6 * (4 + 4 * (shards - 1)) + plane - 1 + 3
     return pl.pallas_call(
         functools.partial(forward_kernel, shards),
         out_shape=outs,
-        in_specs=[any_spec()] * 8 + [vmem_spec()] * 4,
-        out_specs=[any_spec()] * 15 + [vmem_spec()] * 2,
+        in_specs=[any_spec()] * 8
+        + [vmem_spec()] * 2
+        + [pl.BlockSpec(memory_space=pltpu.SMEM)],
+        out_specs=[any_spec()] * 15 + [vmem_spec()] * 4,
         scratch_shapes=[
             pltpu.VMEM((queries, width), bf16),
             pltpu.VMEM((queries, width), bf16),
@@ -766,7 +786,7 @@
             collective_id=0, has_side_effects=True, vmem_limit_bytes=60 * 2**20
         ),
         name="forward",
-    )(x, og, wq, wkv, wo, wg, wu, wd, gpad, cos, sin, bias)
+    )(x, og, wq, wkv, wo, wg, wu, wd, gpad, frequency, order)
 
 
 def middle_kernel(
@@ -786,18 +806,29 @@
     t = links.t
     own_rows = pl.ds(pl.multiple_of(place(t) * tokens, tokens), tokens)
 
-    spans = [slice(b, min(b + 256, columns)) for b in range(0, columns, 256)]
     sides = [slice(0, side), slice(side, queries)]
-    loads = {"n2": links.keep(n2_in.at[sides[0]], n2.at[sides[0]])}
-    for index, span in enumerate(spans):
-        loads["g", index] = links.keep(wg_in.at[:, span], wg.at[:, span])
-        loads["u", index] = links.keep(wu_in.at[:, span], wu.at[:, span])
+    full, rest_columns = columns // 256, columns % 256
+    weights = ((wg_in, wg), (wu_in, wu), (wd_in, wd))
+
+    def fetch(j, start, size, index):
+        src, dst = weights[j]
+        of = pl.ds(start, size)
+        sem = local_sems.at[3 * index + j]
+        return pltpu.make_async_copy(src.at[:, of], dst.at[:, of], sem)
+
+    links.local_used = 3 * (full + 1)
+    load_n2 = links.keep(n2_in.at[sides[0]], n2.at[sides[0]])
+    for index in range(full):
+        for j in range(3):
+            fetch(j, index * 256, 256, index).start()
         if index == 0:
-            loads["og"] = links.keep(og_in.at[sides[0]], og.at[sides[0]])
-        loads["d", index] = links.keep(wd_in.at[:, span], wd.at[:, span])
-    loads["n2b"] = links.keep(n2_in.at[sides[1]], n2.at[sides[1]])
-    loads["ogb"] = links.keep(og_in.at[sides[1]], og.at[sides[1]])
-    loads["mid"] = links.keep(mid_in, mid)
+            load_og = links.keep(og_in.at[sides[0]], og.at[sides[0]])
+    if rest_columns:
+        for j in range(3):
+            fetch(j, full * 256, rest_columns, full).start()
+    load_n2b = links.keep(n2_in.at[sides[1]], n2.at[sides[1]])
+    load_ogb = links.keep(og_in.at[sides[1]], og.at[sides[1]])
+    load_mid = links.keep(mid_in, mid)
     scatter = LineScatter(links, part, tokens, left, right, PIECES)
     gather = LineGather(links, dsend, dmid_all_o, tokens, PIECES)
     down = PlaneScatter(links, og, hidden, rows, *grads[0:6])
@@ -808,25 +839,30 @@
 
     def feed_forward(half):
         at = sides[half]
-        for index, span in enumerate(spans):
+
+        def tile(start, size, index):
+            of = pl.ds(start, size)
             if half == 0:
-                if index == 0:
-                    loads["n2"].wait()
-                loads["g", index].wait()
-                loads["u", index].wait()
-            gate_act = nn_dot(n2[at, :], wg[:, span])
-            up_act = nn_dot(n2[at, :], wu[:, span])
+                fetch(0, start, size, index).wait()
+                fetch(1, start, size, index).wait()
+            gate_act = nn_dot(n2[at, :], wg[:, of])
+            up_act = nn_dot(n2[at, :], wu[:, of])
             if half == 0:
-                if index == 0:
-                    loads["og"].wait()
-                loads["d", index].wait()
-            d_hidden = nn_dot(og[at, :], wd[:, span])
+                fetch(2, start, size, index).wait()
+            d_hidden = nn_dot(og[at, :], wd[:, of])
             sig = jax.nn.sigmoid(gate_act)
             silu = gate_act * sig
-            hidden[at, span] = (silu * up_act).astype(bf16)
+            hidden[at, of] = (silu * up_act).astype(bf16)
             d_gate = d_hidden * up_act * sig * (1.0 + gate_act * (1.0 - sig))
-            dgate[at, span] = d_gate.astype(bf16)
-            dup[at, span] = (d_hidden * silu).astype(bf16)
+            dgate[at, of] = d_gate.astype(bf16)
+            dup[at, of] = (d_hidden * silu).astype(bf16)
+
+        @pl.loop(0, full)
+        def _(index):
+            tile(pl.multiple_of(index * 256, 256), 256, index)
+
+        if rest_columns:
+            tile(full * 256, rest_columns, full)
 
         @pl.loop(0, width // 512)
         def _(j):
@@ -834,12 +870,25 @@
             summed = nt_dot(dgate[at, :], wg[of, :]) + nt_dot(dup[at, :], wu[of, :])
             part[at, of] = summed.astype(bf16)
 
+    piece = CTX * rows
+
+    def others(grad, room):
+        for step in range(1, shards):
+            grad.other(step, room.at[pl.ds((step - 1) * piece, piece)])
+
+    load_n2.wait()
+    load_og.wait()
     feed_forward(0)
     line_steps(scatter, 0)
-    loads["n2b"].wait()
-    loads["ogb"].wait()
+    load_n2b.wait()
+    load_ogb.wait()
     feed_forward(1)
     line_steps(scatter, 1)
+    others(gate, wg)
+    others(up, wu)
+    gate.own()
+    gate.exchange()
+    line_steps(scatter, 2)
 
     @pl.loop(0, width // 512)
     def _(j):
@@ -847,19 +896,8 @@
         branch[:, of] = nt_dot(hidden[...], wd[of, :]).astype(bf16)
 
     links.keep_later(branch, branch_o)
-
-    piece = CTX * rows
-
-    def others(grad, room):
-        for step in range(1, shards):
-            grad.other(step, room.at[pl.ds((step - 1) * piece, piece)])
-
     others(down, wd)
-    line_steps(scatter, 2)
-    others(gate, wg)
-    down.own()
-    down.exchange()
-    loads["mid"].wait()
+    load_mid.wait()
     gain_rows[...] = jnp.zeros_like(gain_rows)
 
     def finish_rows(r, d_normed):
@@ -876,23 +914,22 @@
         dsend[at, :] = d_middle.astype(bf16)
 
     line_finish(scatter, finish_rows, gather)
+    down.own()
+    down.exchange()
     links.keep_later(dsend, dmid_all_o.at[own_rows])
     links.keep_later(dmid, dmid_o)
-    gate.own()
-    gate.exchange()
-    others(up, wu)
-    gain_sum[...] = jnp.sum(gain_rows[...], 0, keepdims=True)
     line_spread(gather, 1)
     up.own()
     links.keep_later(up_in.at[0], gu_part_o)
+    gain_sum[...] = jnp.sum(gain_rows[...], 0, keepdims=True)
+    gate.fold()
     line_spread(gather, 2)
     down.fold()
     line_spread(gather, 3)
-    gate.fold()
+    gate.total()
+    links.keep_later(gate.out, gg_o)
     down.total()
     links.keep_later(down.out, gd_o)
-    gate.total()
-    links.keep_later(gate.out, gg_o)
     links.finish()
 
 
@@ -997,7 +1034,7 @@
     scatter.clear()
     scatter_out.clear()
     loads[0].wait()
-    scatter_out.step(0)
+    scatter_out.stage(0)
     for load in loads[1:3]:
         load.wait()
     d_out[...] = nn_dot(dmid_all[...], wo[...]).astype(bf16).T
@@ -1006,11 +1043,13 @@
     for load in loads[4:8]:
         load.wait()
     attn_rows[...] = att[...].T
+    others(g_o, stage_o)
     for other in range(CTX):
         v_rows[other * queries : (other + 1) * queries, :] = kv[other, HD : 2 * HD, :].T
     d_keys[...] = jnp.zeros_like(d_keys)
     d_values[...] = jnp.zeros_like(d_values)
-    others(g_o, stage_o)
+    g_o.own()
+    g_o.exchange()
 
     def head(h):
         at = pl.ds(pl.multiple_of(h * HD, HD), HD)
@@ -1030,13 +1069,9 @@
             d_q = d_q + nn_dot(kv[b // queries, 0:HD, at_b : at_b + BLOCK], d_scores)
         d_query[at, :] = d_q * (HD ** (-0.5))
 
-    quarter = heads // 4
-    pl.loop(0, quarter)(head)
-    g_o.own()
-    g_o.exchange()
-    pl.loop(quarter, 2 * quarter)(head)
-    scatter_out.step(1)
-    pl.loop(2 * quarter, heads)(head)
+    pl.loop(0, heads // 2)(head)
+    scatter_out.stage(1)
+    pl.loop(heads // 2, heads)(head)
 
     for other in range(CTX):
         block = slice(other * queries, (other + 1) * queries)
@@ -1045,7 +1080,7 @@
     for step in range(1, CTX):
         peer = lax.rem(c + step, CTX)
         links.send(kv_send.at[peer], kv_recv.at[step - 1], (s, peer, t), kv_slot + step - 1)
-    scatter_out.step(2)
+    scatter_out.stage(2)
     for load in loads[8:]:
         load.wait()
 
@@ -1234,27 +1269,18 @@
     shards = lax.axis_size("shard")
     x, og = inputs[0], out_grad[0]
     tokens, width = x.shape
-    queries = tokens * LINE
-    order = block_order[0]
     s, c = lax.axis_index("shard"), lax.axis_index("ctx")
-    per = queries // BLOCK
-    owners = [owner for at in range(LINE) for owner in range(LINE) if place(owner) == at]
-    slots = np.concatenate([owner * tokens + np.arange(tokens) for owner in owners])
-    here = lax.dynamic_slice_in_dim(order, c * per, per)
-    block_here = sum(jnp.where(slots // BLOCK == i, here[i], 0) for i in range(per))
-    position = block_here * BLOCK + (slots % BLOCK).astype(np.int32)
-    half = HD // 2
-    frequency = 10000.0 ** (-jnp.arange(half, dtype=f32) * 2.0 / HD)
-    angles = frequency[:, None] * position.astype(f32)[None, :]
-    cos, sin = jnp.cos(angles), jnp.sin(angles)
-    bias = jnp.where(order[:, None] <= block_here[None, :], 0.0, blocked).astype(bf16)
-    bias = jnp.concatenate([bias, jnp.zeros((HD - BLOCKS, queries), bf16)], 0)
-    start = (s * CTX + c) * gain_attn.shape[0]
-    gpad = lax.dynamic_update_slice(
-        jnp.zeros((2, width), f32), jnp.stack([gain_attn, gain_mlp]).astype(f32), (0, start)
-    )
-    (wq, wkv, wo, wg, wu, wd, n1, og_all, n2, mid, qaug, kaug, kv, att, x_all, lse, gains) = forward_call(
-        shards, x, og, (w_query, w_keyval, w_output, w_gate, w_up, w_down), gpad, cos, sin, bias
+    frequency = 10000.0 ** (-jnp.arange(HD // 2, dtype=f32)[:, None] * 2.0 / HD)
+    own = gain_attn.shape[0]
+    start = (s * CTX + c) * own
+    lane = lax.broadcasted_iota(jnp.int32, (2, width), 1)
+    row = lax.broadcasted_iota(jnp.int32, (2, width), 0)
+    spread = lambda gain: jnp.broadcast_to(gain.astype(f32), (width // own, own)).reshape(1, width)
+    gpad = jnp.where(row == 0, spread(gain_attn), spread(gain_mlp))
+    gpad = jnp.where(lane // own == s * CTX + c, gpad, 0.0)
+    (wq, wkv, wo, wg, wu, wd, n1, og_all, n2, mid, qaug, kaug, kv, att, x_all, lse, gains, cos, sin) = forward_call(
+        shards, x, og, (w_query, w_keyval, w_output, w_gate, w_up, w_down), gpad, frequency,
+        block_order[0],
     )
     (dmid, dmid_all, grad_gate, grad_down, branch, gu_part, gm) = middle_call(
         shards, w_gate.shape[0], n2, og_all, wg, wu, wd, mid, gains

time: 423 us -> 324 us (0.77); the launches traced: 416 us -> 322 us
  Pallas kernels: 396 us -> 306 us
    pallas_call x1, Pallas kernels: 126 us -> 83.1 us  [backward_call(): pl.pallas_call(functools.partial(backward_kernel, shards, rows), out_shap...]
    pallas_call x1, Pallas kernels: 128 us -> 96.4 us  [middle_call(): pl.pallas_call(functools.partial(middle_kernel, shards, rows), out_shape=...]
    pallas_call x1, Pallas kernels: 142 us -> 127 us  [forward_call(): pl.pallas_call(functools.partial(forward_kernel, shards), out_shape=outs,...]
    unnamed x22 -> x24, local copies, waits for them, and re-layouts: 11.3 us -> 10.7 us
where the time goes in v4:
time: 324 us; the launch traced here: 322 us
  Pallas kernels  306 us (94%)
  local copies, waits for them, and re-layouts  12.1 us (4%)
    pallas_call x1, Pallas kernels, forward_call(): pl.pallas_call(functools.partial(forward_kernel, shards), out_shape=outs,...  127 us
    pallas_call x1, Pallas kernels, middle_call(): pl.pallas_call(functools.partial(middle_kernel, shards, rows), out_shape=...  96.4 us
    pallas_call x1, Pallas kernels, backward_call(): pl.pallas_call(functools.partial(backward_kernel, shards, rows), out_shap...  83.1 us
    unnamed x24, local copies, waits for them, and re-layouts  10.7 us

profile of v4, /device:TPU:9, one launch (start us, length us, event | category | flops | bytes accessed | tf_op | source)
XLA Modules:
  0.0 321.7 jit_solution(17004364651701284621)
XLA Ops:
  0.7 0.7 convert_element_type.7
  1.3 0.7 convert_element_type.6
  2.0 0.7 compare_select_fusion.gpad
  2.7 0.6 multiply_power_fusion.frequency
  3.3 126.7 %forward.1 = (bf16[2048,512]{1,0:T(8,128)(2,1)}, bf16[2048,128]{1,0:T(8,128)(2,1)}, bf16[2048,512]{1,0:T(8,128)(2,1)}, bf16[2048,1408]{1,0:T(8,128)(2,1)}, bf16[...) custom-call(bf16[128,2048]{1,0:T(8,128)(2,1)} %bitcast.15, ...), custom_call_target="tpu_custom_call" | custom-call | tf_op jit(solution)/shard_map/forward/pallas_call | solution.py:751
  130.1 96.4 %middle.1 = (f32[128,2048]{1,0:T(8,128)}, bf16[512,2048]{1,0:T(8,128)(2,1)}, f32[256,1408]{1,0:T(8,128)}, f32[256,1408]{1,0:T(8,128)}, bf16[512,2048]{1,0:T(8,12...) custom-call(bf16[512,2048]{1,0:T(8,128)(2,1)} %get-tuple-element.43.n2_in, ...), custom_call_target="tpu_custom_call" | custom-call | tf_op jit(solution)/shard_map/middle/pallas_call | solution.py:953
  226.5 83.1 %backward.1 = (f32[128,2048]{1,0:T(8,128)}, f32[256,512]{1,0:T(8,128)}, f32[256,128]{1,0:T(8,128)}, f32[256,512]{1,0:T(8,128)}, f32[256,1408]{1,0:T(8,128)}, /*i...) custom-call(bf16[512,2048]{1,0:T(8,128)(2,1)} %get-tuple-element.50.dmid_all_in, bf16[2048,512]{1,0:T(8,128)(2,1)} %get-tuple-element.51.wo_in, ...), custom_call_target="tpu_custom_call" | custom-call | tf_op jit(solution)/shard_map/backward/pallas_call | solution.py:1205
  309.5 0.0 copy-start.4
  309.5 1.4 fusion.3
  311.0 0.0 copy-start.5
  311.0 0.0 copy-start.3
  311.0 1.9 copy.31
  312.9 0.0 copy-start.1
  312.9 2.4 copy.32
  315.3 0.0 copy-done.4
  315.3 0.8 copy.33
  316.1 0.0 copy-done.5
  316.1 0.0 copy-start.2
  316.1 0.7 copy.34
  316.8 0.0 copy-done.3
  316.8 0.8 copy.35
  317.6 0.0 copy-done.1
  317.6 1.1 copy.36
  318.7 0.0 copy-done.2
  318.7 0.0 copy-start
  318.7 1.1 copy.37
  319.8 0.8 copy-done
  320.6 1.1 copy.38
  (7 shorter events, 0.0 us)
Async XLA Ops:
  309.5 5.8 %copy-start.4 = (f32[256,512]{1,0:T(8,128)S(1)}, f32[256,512]{1,0:T(8,128)}, u32[]{:S(2)}) copy-start(f32[256,512]{1,0:T(8,128)} %get-tuple-element.93) | copy-start | bytes 1572868
  311.0 5.2 %copy-start.5 = (f32[256,128]{1,0:T(8,128)S(1)}, f32[256,128]{1,0:T(8,128)}, u32[]{:S(2)}) copy-start(f32[256,128]{1,0:T(8,128)} %get-tuple-element.94) | copy-start | bytes 393220
  311.0 5.8 %copy-start.3 = (f32[256,512]{1,0:T(8,128)S(1)}, f32[256,512]{1,0:T(8,128)}, u32[]{:S(2)}) copy-start(f32[256,512]{1,0:T(8,128)} %get-tuple-element.95) | copy-start | bytes 1572868
  312.9 4.7 %copy-start.1 = (f32[256,1408]{1,0:T(8,128)S(1)}, f32[256,1408]{1,0:T(8,128)}, u32[]{:S(2)}) copy-start(f32[256,1408]{1,0:T(8,128)} %get-tuple-element.97) | copy-start | bytes 4325380
  316.1 2.6 copy-start.2
  318.7 1.9 copy-start

commit v5 on v4

--- a/solution.py
+++ b/solution.py
@@ -283,20 +283,6 @@
     def piece(self, ref, k, p):
         return ref.at[k, pl.ds(p * self.size, self.size)]
 
-    def clear(self):
-        for cond, ref in (
-            (self.links.t == 0, self.from_left),
-            (self.links.t == LINE - 1, self.from_right),
-        ):
-
-            @pl.when(cond)
-            def _():
-                @pl.loop(0, self.tokens // ROWS)
-                def _(i):
-                    r = pl.multiple_of(i * ROWS, ROWS)
-                    for k in range(LINE - 1):
-                        ref[k, pl.ds(r, ROWS), :] = jnp.zeros((ROWS, ref.shape[2]), ref.dtype)
-
     def total(self, owner, k, p, arrived):
         @pl.loop(0, self.size // ROWS)
         def _(i):
@@ -306,26 +292,46 @@
             summed = mine + arrived[k, pl.ds(r, ROWS), :].astype(f32)
             arrived[k, pl.ds(r, ROWS), :] = summed.astype(arrived.dtype)
 
+    def ends(self, k, p=0):
+        links = self.links
+        for side, behind, arrived, device in self.sides():
+            owner = LINE - 1 - k if side == 0 else k
+            piece, slot = self.piece(arrived, k, p), self.slot(side, k, p)
+
+            @pl.when(behind == 0)
+            def _():
+                self.first_part(owner, k, p, arrived)
+
+            links.send(piece, piece, device, slot, behind == 0)
+
+    def sides(self):
+        links = self.links
+        return (
+            (0, links.t, self.from_left, links.right),
+            (1, LINE - 1 - links.t, self.from_right, links.left),
+        )
+
     def stage(self, now, p=0):
         links = self.links
-        t, u = links.t, LINE - 1 - links.t
-        for side, behind, arrived, device in (
-            (0, t, self.from_left, links.right),
-            (1, u, self.from_right, links.left),
-        ):
+        for side, behind, arrived, device in self.sides():
             k = now - behind
             owner = LINE - 1 - k if side == 0 else k
             piece, slot = self.piece(arrived, k, p), self.slot(side, k, p)
-
-            @pl.when(k >= 0)
+            ready = jnp.logical_and(k >= 0, behind > 0)
+
+            @pl.when(ready)
             def _():
-                @pl.when(behind > 0)
-                def _():
-                    links.recv(piece, slot)
-
+                links.recv(piece, slot)
                 self.total(owner, k, p, arrived)
 
-            links.send(piece, piece, device, slot, k >= 0)
+            links.send(piece, piece, device, slot, ready)
+
+    def first_part(self, owner, k, p, out):
+        @pl.loop(0, self.size // ROWS)
+        def _(i):
+            r = pl.multiple_of(p * self.size + i * ROWS, ROWS)
+            q = pl.multiple_of(place(owner) * self.tokens + p * self.size + i * ROWS, ROWS)
+            out[k, pl.ds(r, ROWS), :] = self.part[pl.ds(q, ROWS), :].astype(out.dtype)
 
     def arrive(self, p=0):
         links = self.links
@@ -360,11 +366,15 @@
             use(r, self.rows(r))
 
 
-def line_steps(scatter, k, hooks=()):
+def line_ends(scatter, *hops):
+    for k in hops:
+        for p in range(scatter.pieces):
+            scatter.ends(k, p)
+
+
+def line_steps(scatter, now):
     for p in range(scatter.pieces):
-        scatter.stage(k, p)
-    for hook in hooks:
-        hook()
+        scatter.stage(now, p)
 
 
 def line_finish(scatter, use, gather=None):
@@ -506,11 +516,11 @@
 
 def forward_kernel(
     shards,
-    x, og, wq, wkv, wo, wg, wu, wd, gpad, frequency, order,
+    x, og, wq, wkv, wo, wg, wu, wd, gain_a, gain_m, frequency, order,
     wq_o, wkv_o, wo_o, wg_o, wu_o, wd_o, n1_o, og_o, n2_o, mid_o, qaug_o, kaug_o, kv_o, att_o, x_o,
     lse, gains, cos, sin,
     x_all, n1_all, wq_all, wkv_all, wo_all, gains_all, qaug, kv_all, kaug, v_all, scores, weights,
-    attn, part, from_left, from_right, mid, n2, og_stage, wg_stage, wu_stage, wd_stage,
+    attn, part, from_left, from_right, mid, n2, og_stage, wg_stage, wu_stage, wd_stage, gpad,
     send_sems, recv_sems, local_sems,
 ):
     tokens, width = x.shape
@@ -532,8 +542,17 @@
     gain_slot = links.slots(plane - 1)
     kv_slot = links.slots(3)
 
+    me = s * CTX + c
+    own = gain_a.shape[1]
+    if own == width:
+        gpad[0:1, :] = gain_a[...].astype(f32)
+        gpad[1:2, :] = gain_m[...].astype(f32)
+    else:
+        gpad[...] = jnp.zeros_like(gpad)
+        own_lanes = pl.ds(pl.multiple_of(me * own, own), own)
+        gpad[0:1, own_lanes] = gain_a[...].astype(f32)
+        gpad[1:2, own_lanes] = gain_m[...].astype(f32)
     links.barrier()
-    me = s * CTX + c
     for step in range(1, plane):
         links.send(gpad, gains_all.at[me], links.plane_peer(step), gain_slot + step - 1)
     own_gain = links.keep(gpad, gains_all.at[me])
@@ -542,7 +561,6 @@
     own_x = links.keep(x, x_all.at[own_rows])
     for gather in small:
         gather.start()
-    scatter.clear()
 
     per = queries // BLOCK
     lane = lax.broadcasted_iota(jnp.int32, (1, queries), 1)
@@ -678,7 +696,7 @@
     gather_og.recv(2)
     gather_og.send(3)
     project(0)
-    line_steps(scatter, 0)
+    line_ends(scatter, 0)
     large[1].settle()
     large[2].settle()
     pl.loop(0, heads)(functools.partial(head, 1))
@@ -692,6 +710,7 @@
         inverse = lax.rsqrt(jnp.mean(middle * middle, -1, keepdims=True) + epsilon)
         n2[pl.ds(r, ROWS), :] = (middle * inverse * gains[1:2, :]).astype(bf16)
 
+    line_ends(scatter, 1, 2)
     line_steps(scatter, 1)
     large[0].diagonal()
     line_steps(scatter, 2)
@@ -723,7 +742,7 @@
         norm_block(t + k)
 
 
-def forward_call(shards, x, og, weights_in, gpad, frequency, order):
+def forward_call(shards, x, og, weights_in, gain_a, gain_m, frequency, order):
     wq, wkv, wo, wg, wu, wd = weights_in
     tokens, width = x.shape
     queries = tokens * LINE
@@ -752,7 +771,7 @@
         functools.partial(forward_kernel, shards),
         out_shape=outs,
         in_specs=[any_spec()] * 8
-        + [vmem_spec()] * 2
+        + [vmem_spec()] * 3
         + [pl.BlockSpec(memory_space=pltpu.SMEM)],
         out_specs=[any_spec()] * 15 + [vmem_spec()] * 4,
         scratch_shapes=[
@@ -778,6 +797,7 @@
             pltpu.VMEM(wg.shape, bf16),
             pltpu.VMEM(wu.shape, bf16),
             pltpu.VMEM(wd.shape, bf16),
+            pltpu.VMEM((2, width), f32),
             pltpu.SemaphoreType.DMA((count,)),
             pltpu.SemaphoreType.DMA((count,)),
             pltpu.SemaphoreType.DMA((32,)),
@@ -786,7 +806,7 @@
             collective_id=0, has_side_effects=True, vmem_limit_bytes=60 * 2**20
         ),
         name="forward",
-    )(x, og, wq, wkv, wo, wg, wu, wd, gpad, frequency, order)
+    )(x, og, wq, wkv, wo, wg, wu, wd, gain_a, gain_m, frequency, order)
 
 
 def middle_kernel(
@@ -835,7 +855,6 @@
     gate = PlaneScatter(links, n2, dgate, rows, *grads[6:12])
     up = PlaneScatter(links, n2, dup, rows, up_in, None, None, None, None, None)
     links.barrier()
-    scatter.clear()
 
     def feed_forward(half):
         at = sides[half]
@@ -879,10 +898,11 @@
     load_n2.wait()
     load_og.wait()
     feed_forward(0)
-    line_steps(scatter, 0)
+    line_ends(scatter, 0)
     load_n2b.wait()
     load_ogb.wait()
     feed_forward(1)
+    line_ends(scatter, 1, 2)
     line_steps(scatter, 1)
     others(gate, wg)
     others(up, wu)
@@ -1031,10 +1051,8 @@
             grad.other(step, stage.at[pl.ds((step - 1) * piece, piece)])
 
     links.barrier(whole_line=True)
-    scatter.clear()
-    scatter_out.clear()
     loads[0].wait()
-    scatter_out.stage(0)
+    line_ends(scatter_out, 0)
     for load in loads[1:3]:
         load.wait()
     d_out[...] = nn_dot(dmid_all[...], wo[...]).astype(bf16).T
@@ -1043,13 +1061,10 @@
     for load in loads[4:8]:
         load.wait()
     attn_rows[...] = att[...].T
-    others(g_o, stage_o)
     for other in range(CTX):
         v_rows[other * queries : (other + 1) * queries, :] = kv[other, HD : 2 * HD, :].T
     d_keys[...] = jnp.zeros_like(d_keys)
     d_values[...] = jnp.zeros_like(d_values)
-    g_o.own()
-    g_o.exchange()
 
     def head(h):
         at = pl.ds(pl.multiple_of(h * HD, HD), HD)
@@ -1070,6 +1085,7 @@
         d_query[at, :] = d_q * (HD ** (-0.5))
 
     pl.loop(0, heads // 2)(head)
+    line_ends(scatter_out, 1, 2)
     scatter_out.stage(1)
     pl.loop(heads // 2, heads)(head)
 
@@ -1092,6 +1108,7 @@
         d_query[at + half : at + HD, :] = d2 * cosine - d1 * sine
     d_query_rows[...] = d_query[...].astype(bf16).T
     others(g_q, stage_q)
+    others(g_o, stage_o)
     for step in range(1, CTX):
         links.recv(kv_recv.at[step - 1], kv_slot + step - 1)
     d_pair = kv_send[c].astype(f32)
@@ -1110,9 +1127,7 @@
         summed = nt_dot(d_query_rows[...], wq[at, :]) + nt_dot(d_kv[...], wkv[at, :])
         part[:, at] = summed.astype(bf16)
 
-    line_steps(scatter, 0)
-    g_u.fold()
-    g_o.fold()
+    line_ends(scatter, 0, 1, 2)
 
     gain_rows[...] = jnp.zeros_like(gain_rows)
 
@@ -1127,9 +1142,9 @@
     pair[1:2, :] = gain_mlp[...]
     for step in range(1, plane):
         links.send(pair, plane_in.at[step - 1], links.plane_peer(step), plane_slot + step - 1)
-    others(g_kv, stage_kv)
-    g_q.own()
-    g_q.exchange()
+    g_u.fold()
+    g_o.own()
+    g_o.exchange()
     line_steps(scatter, 1)
     summed = pair[...]
     for step in range(1, plane):
@@ -1138,9 +1153,13 @@
     total[...] = summed
     for step in range(1, LINE):
         links.send(total, line_in.at[step - 1], links.line_peer(step), line_slot + step - 1)
+    others(g_kv, stage_kv)
+    g_q.own()
+    g_q.exchange()
+    line_steps(scatter, 2)
     g_kv.own()
     g_kv.exchange()
-    line_steps(scatter, 2)
+    g_o.fold()
     scatter_out.arrive()
 
     def layer_rows(r, total_rows):
@@ -1148,8 +1167,6 @@
 
     scatter_out.owned(0, layer_rows)
     links.keep_later(layer, out_o)
-    g_o.total()
-    links.keep_later(g_o.out, go_o)
     g_q.fold()
     g_kv.fold()
 
@@ -1167,6 +1184,8 @@
     links.keep_later(dmid, in_o)
     g_u.total()
     links.keep_later(g_u.out, gu_o)
+    g_o.total()
+    links.keep_later(g_o.out, go_o)
     g_q.total()
     links.keep_later(g_q.out, gq_o)
     g_kv.total()
@@ -1263,6 +1282,35 @@
     )
 
 
+def finish_kernel(layer_in, *refs):
+    count = len(refs) // 2
+    layer_out = refs[count]
+    layer_out[0] = layer_in[...]
+    refs[count + 1][0] = refs[0][...]
+    for src, dst in zip(refs[1:count], refs[count + 2 :]):
+        dst[...] = src[...]
+
+
+def finish_call(arrays, steps=4):
+    rows = [array.shape[0] // steps for array in arrays]
+    wide = [array.shape[1] for array in arrays]
+    shapes = [struct((1,) * (i < 2) + array.shape, array.dtype) for i, array in enumerate(arrays)]
+    return pl.pallas_call(
+        finish_kernel,
+        grid=(steps,),
+        out_shape=shapes,
+        in_specs=[pl.BlockSpec((r, n), lambda i: (i, 0)) for r, n in zip(rows, wide)],
+        out_specs=[
+            pl.BlockSpec((1, r, n), lambda i: (0, i, 0))
+            if index < 2
+            else pl.BlockSpec((r, n), lambda i: (i, 0))
+            for index, (r, n) in enumerate(zip(rows, wide))
+        ],
+        compiler_params=pltpu.CompilerParams(vmem_limit_bytes=40 * 2**20),
+        name="finish",
+    )(*arrays)
+
+
 def body(
     inputs, out_grad, block_order, gain_attn, w_query, w_keyval, w_output, gain_mlp, w_gate, w_up, w_down
 ):
@@ -1270,17 +1318,19 @@
     x, og = inputs[0], out_grad[0]
     tokens, width = x.shape
     s, c = lax.axis_index("shard"), lax.axis_index("ctx")
-    frequency = 10000.0 ** (-jnp.arange(HD // 2, dtype=f32)[:, None] * 2.0 / HD)
+    frequency = np.float32(10000.0) ** (-np.arange(HD // 2, dtype=np.float32)[:, None] * 2.0 / HD)
     own = gain_attn.shape[0]
     start = (s * CTX + c) * own
-    lane = lax.broadcasted_iota(jnp.int32, (2, width), 1)
-    row = lax.broadcasted_iota(jnp.int32, (2, width), 0)
-    spread = lambda gain: jnp.broadcast_to(gain.astype(f32), (width // own, own)).reshape(1, width)
-    gpad = jnp.where(row == 0, spread(gain_attn), spread(gain_mlp))
-    gpad = jnp.where(lane // own == s * CTX + c, gpad, 0.0)
+    if own % 128 == 0:
+        gain_a, gain_m = gain_attn[None], gain_mlp[None]
+    else:
+        place_gain = lambda gain: lax.dynamic_update_slice(
+            jnp.zeros((1, width), f32), gain.astype(f32)[None], (0, start)
+        )
+        gain_a, gain_m = place_gain(gain_attn), place_gain(gain_mlp)
     (wq, wkv, wo, wg, wu, wd, n1, og_all, n2, mid, qaug, kaug, kv, att, x_all, lse, gains, cos, sin) = forward_call(
-        shards, x, og, (w_query, w_keyval, w_output, w_gate, w_up, w_down), gpad, frequency,
-        block_order[0],
+        shards, x, og, (w_query, w_keyval, w_output, w_gate, w_up, w_down), gain_a, gain_m,
+        jnp.asarray(frequency, f32), block_order[0],
     )
     (dmid, dmid_all, grad_gate, grad_down, branch, gu_part, gm) = middle_call(
         shards, w_gate.shape[0], n2, og_all, wg, wu, wd, mid, gains
@@ -1290,8 +1340,13 @@
         branch, gu_part, mid, lse, gains, gm, cos, sin,
     )
     both = lax.dynamic_slice(both, (0, start), (2, gain_attn.shape[0]))
+    (
+        layer_out, input_grad, grad_query, grad_keyval, grad_output, grad_gate, grad_up, grad_down,
+    ) = finish_call([
+        layer_out, input_grad, grad_query, grad_keyval, grad_output, grad_gate, grad_up, grad_down,
+    ])
     return (
-        layer_out[None], input_grad[None], both[0], grad_query, grad_keyval, grad_output,
+        layer_out, input_grad, both[0], grad_query, grad_keyval, grad_output,
         both[1], grad_gate, grad_up, grad_down,
     )
 

time: 324 us -> 316 us (0.975)
    pallas_call x1, Pallas kernels: 83.1 us -> 76.4 us  [backward_call(): pl.pallas_call(functools.partial(backward_kernel, shards, rows), out_shap...]
    unnamed x24 -> x16, local copies, waits for them, and re-layouts: 10.7 us -> 6.61 us
where the time goes in v5:
time: 316 us; the launch traced here: 314 us
  Pallas kernels  303 us (96%)
  local copies, waits for them, and re-layouts  10.4 us (3%)
    pallas_call x1, Pallas kernels, forward_call(): pl.pallas_call(functools.partial(forward_kernel, shards), out_shape=outs,...  127 us
    pallas_call x1, Pallas kernels, middle_call(): pl.pallas_call(functools.partial(middle_kernel, shards, rows), out_shape=...  96.2 us
    pallas_call x1, Pallas kernels, backward_call(): pl.pallas_call(functools.partial(backward_kernel, shards, rows), out_shap...  76.4 us
    unnamed x16, local copies, waits for them, and re-layouts  6.61 us

profile of v5, /device:TPU:9, one launch (start us, length us, event | category | flops | bytes accessed | tf_op | source)
XLA Modules:
  0.0 313.7 jit_solution(7452716466969150143)
XLA Ops:
  0.6 1.2 broadcast_in_dim.6.gain_a
  1.9 1.2 broadcast_in_dim.7.gain_m
  3.1 126.8 %forward.1 = (bf16[2048,512]{1,0:T(8,128)(2,1)}, bf16[2048,128]{1,0:T(8,128)(2,1)}, bf16[2048,512]{1,0:T(8,128)(2,1)}, bf16[2048,1408]{1,0:T(8,128)(2,1)}, bf16[...) custom-call(bf16[128,2048]{1,0:T(8,128)(2,1)} %bitcast.5, ...), custom_call_target="tpu_custom_call" | custom-call | tf_op jit(solution)/shard_map/forward/pallas_call | solution.py:770
  129.9 96.2 %middle.1 = (f32[128,2048]{1,0:T(8,128)}, bf16[512,2048]{1,0:T(8,128)(2,1)}, f32[256,1408]{1,0:T(8,128)}, f32[256,1408]{1,0:T(8,128)}, bf16[512,2048]{1,0:T(8,12...) custom-call(bf16[512,2048]{1,0:T(8,128)(2,1)} %get-tuple-element.51.n2_in, ...), custom_call_target="tpu_custom_call" | custom-call | tf_op jit(solution)/shard_map/middle/pallas_call | solution.py:973
  226.1 0.0 copy-start
  226.2 0.0 copy-start.1
  226.2 76.4 %backward.1 = (f32[128,2048]{1,0:T(8,128)}, f32[256,512]{1,0:T(8,128)}, f32[256,128]{1,0:T(8,128)}, f32[256,512]{1,0:T(8,128)}, f32[256,1408]{1,0:T(8,128)}, /*i...) custom-call(bf16[512,2048]{1,0:T(8,128)(2,1)} %get-tuple-element.58.dmid_all_in, bf16[2048,512]{1,0:T(8,128)(2,1)} %get-tuple-element.59.wo_in, ...), custom_call_target="tpu_custom_call" | custom-call | tf_op jit(solution)/shard_map/backward/pallas_call | solution.py:1224
  302.5 0.0 copy-done
  302.5 0.0 copy-done.1
  302.6 0.0 copy-start.2
  302.6 1.4 copy-done.2
  303.9 0.0 copy-start.3
  303.9 1.2 copy-done.3
  305.1 0.0 copy-start.4
  305.1 1.0 copy-done.4
  306.2 0.0 copy-start.5
  306.2 1.0 copy-done.5
  307.2 0.0 copy-start.6
  307.2 1.0 copy-done.6
  308.3 0.0 copy-start.7
  308.3 0.9 copy-done.7
  309.2 3.2 %finish.1 = (bf16[1,128,2048]{2,1,0:T(8,128)(2,1)}, f32[1,128,2048]{2,1,0:T(8,128)}, f32[256,512]{1,0:T(8,128)}, f32[256,128]{1,0:T(8,128)}, f32[256,512]{1,0:T(...) custom-call(bf16[128,2048]{1,0:T(8,128)(2,1)S(1)} %copy-done.6, f32[128,2048]{1,0:T(8,128)S(1)} %copy-done.3, ...), custom_call_target="tpu_custom_call" | custom-call | tf_op jit(solution)/shard_map/finish/pallas_call | solution.py:1298
  312.3 1.4 fusion
Async XLA Ops:
  226.1 76.4 %copy-start = (f32[256,1408]{1,0:T(8,128)S(1)}, f32[256,1408]{1,0:T(8,128)}, u32[]{:S(2)}) copy-start(f32[256,1408]{1,0:T(8,128)} %get-tuple-element.80.refs_4_) | copy-start | bytes 4325380
  226.2 76.4 %copy-start.1 = (f32[256,1408]{1,0:T(8,128)S(1)}, f32[256,1408]{1,0:T(8,128)}, u32[]{:S(2)}) copy-start(f32[256,1408]{1,0:T(8,128)} %get-tuple-element.82.refs_6_) | copy-start | bytes 4325380
  302.6 1.4 copy-start.2
  303.9 1.2 copy-start.3
  305.1 1.0 copy-start.4
  306.2 1.0 copy-start.5
  307.2 1.0 copy-start.6
  308.3 0.9 copy-start.7

commit v6 on v5

--- a/solution.py
+++ b/solution.py
@@ -461,20 +461,29 @@
             summed = mine + arrived[1, pl.ds(r, ROWS), :].astype(f32)
             self.core_in[0, pl.ds(q, ROWS), :] = summed.astype(bf16)
 
-    def fold(self):
+    def arrived(self):
         links, first = self.links, self.first + self.links.shards - 1
-        links.recv(self.x_in.at[1], first)
+        for ref, offset in ((self.x_in, 0), (self.y_in, 1)):
+            for part in range(2):
+                links.recv(ref.at[1 - part], first + offset + 2 * part)
+
+    def fold(self, here=False):
+        links, first = self.links, self.first + self.links.shards - 1
+        if not here:
+            links.recv(self.x_in.at[1], first)
         self.add(links.c_y, 0, self.x_in)
         links.send(self.half(links.c_y, 0), self.y_last, links.y_dev, first + 4)
-        links.recv(self.y_in.at[1], first + 1)
+        if not here:
+            links.recv(self.y_in.at[1], first + 1)
         self.add(links.c_x, 1, self.y_in)
         links.send(self.half(links.c_x, 1), self.x_last, links.x_dev, first + 5)
 
-    def total(self):
+    def total(self, here=False):
         links, first = self.links, self.first + self.links.shards - 1
         size = self.rows // 2
-        links.recv(self.x_in.at[0], first + 2)
-        links.recv(self.y_in.at[0], first + 3)
+        if not here:
+            links.recv(self.x_in.at[0], first + 2)
+            links.recv(self.y_in.at[0], first + 3)
         links.recv(self.y_last, first + 4)
         links.recv(self.x_last, first + 5)
         for which, arrived, last in ((0, self.x_in, self.y_last), (1, self.y_in, self.x_last)):
@@ -516,7 +525,7 @@
 
 def forward_kernel(
     shards,
-    x, og, wq, wkv, wo, wg, wu, wd, gain_a, gain_m, frequency, order,
+    x, og, wq, wkv, wo, wg, wu, wd, gain_in, frequency, order,
     wq_o, wkv_o, wo_o, wg_o, wu_o, wd_o, n1_o, og_o, n2_o, mid_o, qaug_o, kaug_o, kv_o, att_o, x_o,
     lse, gains, cos, sin,
     x_all, n1_all, wq_all, wkv_all, wo_all, gains_all, qaug, kv_all, kaug, v_all, scores, weights,
@@ -529,7 +538,7 @@
     links = Links(shards, send_sems, recv_sems, local_sems)
     s, c, t = links.s, links.c, links.t
 
-    gather_x = LineGather(links, x, x_all, tokens)
+    gather_x = LineGather(links, x, x_all, tokens, PIECES)
     gather_og = LineGather(links, og, og_o, tokens)
     gather_n2 = LineGather(links, n2, n2_o, tokens, PIECES)
     small = [PlaneGather(links, *pair) for pair in ((wq, wq_all), (wkv, wkv_all), (wo, wo_all))]
@@ -540,23 +549,21 @@
     scatter = LineScatter(links, part, tokens, from_left, from_right, PIECES)
     plane = shards * CTX
     gain_slot = links.slots(plane - 1)
-    kv_slot = links.slots(3)
+    kv_slot = links.slots((CTX - 1) * (2 * LINE - 1))
 
     me = s * CTX + c
-    own = gain_a.shape[1]
-    if own == width:
-        gpad[0:1, :] = gain_a[...].astype(f32)
-        gpad[1:2, :] = gain_m[...].astype(f32)
+    own_gains = gain_in.shape[1]
+    if own_gains == width:
+        gpad[...] = gain_in[...]
     else:
         gpad[...] = jnp.zeros_like(gpad)
-        own_lanes = pl.ds(pl.multiple_of(me * own, own), own)
-        gpad[0:1, own_lanes] = gain_a[...].astype(f32)
-        gpad[1:2, own_lanes] = gain_m[...].astype(f32)
+        gpad[:, pl.ds(pl.multiple_of(me * own_gains, own_gains), own_gains)] = gain_in[...]
     links.barrier()
     for step in range(1, plane):
         links.send(gpad, gains_all.at[me], links.plane_peer(step), gain_slot + step - 1)
     own_gain = links.keep(gpad, gains_all.at[me])
-    gather_x.send(1)
+    for p in range(PIECES):
+        gather_x.send(1, p)
     own_rows = pl.ds(pl.multiple_of(place(t) * tokens, tokens), tokens)
     own_x = links.keep(x, x_all.at[own_rows])
     for gather in small:
@@ -604,55 +611,89 @@
 
     own_og = links.keep(og, og_stage)
     norm_block(t)
-    gather_x.recv(1)
-    gather_x.send(2)
+    line_spread(gather_x, 1)
     for gather in small:
         gather.forward()
-    large[0].start()
     norm_pair(gather_x, norm_block, 1)
-    gather_x.recv(2)
-    gather_x.send(3)
+    line_spread(gather_x, 2)
     gather_og.send(1)
     for gather in small:
         gather.diagonal()
     norm_pair(gather_x, norm_block, 2)
     own_og.wait()
     links.keep_later(og_stage, og_o.at[own_rows])
-    gather_x.recv(3)
-    norm_pair(gather_x, norm_block, 3)
     for gather in small:
         gather.done()
 
-    kv_t = nn_dot(n1_all[...], wkv_all[...]).T
     half = HD // 2
-    cosine, sine = cos[...], sin[...]
-    k1, k2 = kv_t[0:half], kv_t[half:HD]
-    kv_all[c, 0:half, :] = (k1 * cosine - k2 * sine).astype(bf16)
-    kv_all[c, half:HD, :] = (k2 * cosine + k1 * sine).astype(bf16)
-    kv_all[c, HD : 2 * HD, :] = kv_t[HD:].astype(bf16)
-    for step in range(1, CTX):
-        peer = lax.rem(c + step, CTX)
-        links.send(kv_all.at[c], kv_all.at[c], (s, peer, t), kv_slot + step - 1)
-    large[0].settle()
-    large[0].forward()
-    large[1].start()
-    large[2].start()
-
-    q_t = nn_dot(n1_all[...], wq_all[...]).T
     scale = HD ** (-0.5)
-    for h in range(heads):
-        v1, v2 = q_t[h * HD : h * HD + half], q_t[h * HD + half : (h + 1) * HD]
-        qaug[h, 0:half, :] = ((v1 * cosine - v2 * sine).astype(bf16) * scale).astype(bf16)
-        qaug[h, half:HD, :] = ((v2 * cosine + v1 * sine).astype(bf16) * scale).astype(bf16)
+
+    def lanes_of(owner):
+        return pl.ds(pl.multiple_of(place(owner) * tokens, tokens), tokens)
+
+    def turn(v1, v2, cosine, sine):
+        return (v1 * cosine - v2 * sine).astype(bf16), (v2 * cosine + v1 * sine).astype(bf16)
+
+    def project_block(owner):
+        at = lanes_of(owner)
+        cosine, sine = cos[:, at], sin[:, at]
+        kv_t = nn_dot(n1_all[at, :], wkv_all[...]).T
+        k1, k2 = turn(kv_t[0:half], kv_t[half:HD], cosine, sine)
+        kv_all[c, 0:half, at] = k1
+        kv_all[c, half:HD, at] = k2
+        kv_all[c, HD : 2 * HD, at] = kv_t[HD:].astype(bf16)
+        q_t = nn_dot(n1_all[at, :], wq_all[...]).T
+        for h in range(heads):
+            b = h * HD
+            q1, q2 = turn(q_t[b : b + half], q_t[b + half : b + HD], cosine, sine)
+            qaug[h, 0:half, at] = (q1 * scale).astype(bf16)
+            qaug[h, half:HD, at] = (q2 * scale).astype(bf16)
+
+    u = LINE - 1 - t
+    arrivals = [(t, None)]
+    for k in range(1, LINE):
+        arrivals += [(t - k, t >= k), (t + k, u >= k)]
+
+    def send_block(index):
+        owner, cond = arrivals[index]
+        for step in range(1, CTX):
+            peer = lax.rem(c + step, CTX)
+            ref = kv_all.at[c, :, lanes_of(owner)]
+            links.send(ref, ref, (s, peer, t), kv_slot + index * (CTX - 1) + step - 1, cond)
+
+    def recv_block(index):
+        owner, cond = arrivals[index]
+
+        def wait():
+            for step in range(1, CTX):
+                other = lax.rem(c + CTX - step, CTX)
+                slot = kv_slot + index * (CTX - 1) + step - 1
+                links.recv(kv_all.at[other, :, lanes_of(owner)], slot)
+
+        if cond is None:
+            wait()
+        else:
+            pl.when(cond)(wait)
+
+    project_block(t)
+    send_block(0)
+    for k in range(1, LINE):
+        if k == LINE - 1:
+            line_spread(gather_x, k)
+            norm_pair(gather_x, norm_block, k)
+        norm_pair(gather_x, project_block, k)
+        send_block(2 * k - 1)
+        send_block(2 * k)
+    for gather in large:
+        gather.start()
     links.keep_later(n1_all, n1_o)
     links.keep_later(x_all, x_o)
     links.keep_later(wq_all, wq_o)
     links.keep_later(wkv_all, wkv_o)
     links.keep_later(wo_all, wo_o)
     links.keep_later(qaug, qaug_o)
-    for step in range(1, CTX):
-        other = lax.rem(c + CTX - step, CTX)
-        links.recv(kv_all.at[other], kv_slot + step - 1)
+    for index in range(len(arrivals)):
+        recv_block(index)
     for other in range(CTX):
         row = lax.broadcasted_iota(jnp.int32, (HD, queries), 0)
         lane = lax.broadcasted_iota(jnp.int32, (HD, queries), 1)
@@ -665,42 +706,45 @@
 
     length = queries * CTX
 
-    side = queries // 2
-
-    def head(half, h):
-        lanes = slice(half * side, (half + 1) * side)
+    far = pl.multiple_of(jnp.where(t < LINE // 2, tokens, 0), tokens)
+    near = pl.multiple_of(jnp.where(t < LINE // 2, 0, tokens), tokens)
+
+    def head(start, size, h):
+        lanes = pl.ds(start, size)
         query = qaug[h, :, lanes]
-        top = jnp.full((1, side), -jnp.inf, f32)
+        top = jnp.full((1, size), -jnp.inf, f32)
         for b in range(0, length, BLOCK):
             block_scores = nn_dot(kaug[b : b + BLOCK, :], query)
-            scores[b : b + BLOCK, :] = block_scores
+            scores[b : b + BLOCK, 0:size] = block_scores
             top = jnp.maximum(top, jnp.max(block_scores, 0, keepdims=True))
-        norm = jnp.zeros((1, side), f32)
+        norm = jnp.zeros((1, size), f32)
         for b in range(0, length, BLOCK):
-            exponent = jnp.exp(scores[b : b + BLOCK, :] - top)
+            exponent = jnp.exp(scores[b : b + BLOCK, 0:size] - top)
             norm = norm + jnp.sum(exponent, 0, keepdims=True)
-            weights[b : b + BLOCK, :] = exponent.astype(bf16)
-        out = nn_dot(v_all[...], weights[...]) / norm
+            weights[b : b + BLOCK, 0:size] = exponent.astype(bf16)
+        out = nn_dot(v_all[...], weights[:, 0:size]) / norm
         attn[pl.ds(pl.multiple_of(h * HD, HD), HD), lanes] = out.astype(bf16)
-        lse[pl.ds(h, 1), lanes] = top + jnp.log(norm)
-
-    def project(half):
-        rows = slice(half * side, (half + 1) * side)
+        lse[h, :, lanes] = top + jnp.log(norm)
+
+    def attend(start, size):
+        pl.loop(0, heads)(functools.partial(head, start, size))
+        rows = pl.ds(start, size)
         attn_rows = attn[:, rows].T
         for b in range(0, width, 512):
             part[rows, b : b + 512] = nt_dot(attn_rows, wo_all[b : b + 512, :])
 
+    attend(far, tokens)
+    line_ends(scatter, 0)
     gather_og.recv(1)
     gather_og.send(2)
-    pl.loop(0, heads)(functools.partial(head, 0))
+    for gather in large:
+        gather.settle()
+    attend(2 * tokens, 2 * tokens)
+    line_ends(scatter, 1, 2)
     gather_og.recv(2)
     gather_og.send(3)
-    project(0)
-    line_ends(scatter, 0)
-    large[1].settle()
-    large[2].settle()
-    pl.loop(0, heads)(functools.partial(head, 1))
-    project(1)
+    line_steps(scatter, 1)
+    attend(near, tokens)
     links.keep_later(attn, att_o)
 
     def finish_rows(r, summed):
@@ -710,18 +754,17 @@
         inverse = lax.rsqrt(jnp.mean(middle * middle, -1, keepdims=True) + epsilon)
         n2[pl.ds(r, ROWS), :] = (middle * inverse * gains[1:2, :]).astype(bf16)
 
-    line_ends(scatter, 1, 2)
-    line_steps(scatter, 1)
-    large[0].diagonal()
+    large[0].forward()
     line_steps(scatter, 2)
+    large[1].forward()
     line_finish(scatter, finish_rows, gather_n2)
+    large[2].forward()
     links.keep_later(n2, n2_o.at[own_rows])
     links.keep_later(mid, mid_o)
-    large[1].forward()
-    large[2].forward()
     line_spread(gather_n2, 1)
+    large[0].diagonal()
+    large[1].diagonal()
     line_spread(gather_n2, 2)
-    large[1].diagonal()
     large[2].diagonal()
     gather_og.recv(3)
     line_spread(gather_n2, 3)
@@ -742,7 +785,7 @@
         norm_block(t + k)
 
 
-def forward_call(shards, x, og, weights_in, gain_a, gain_m, frequency, order):
+def forward_call(shards, x, og, weights_in, gain_in, frequency, order):
     wq, wkv, wo, wg, wu, wd = weights_in
     tokens, width = x.shape
     queries = tokens * LINE
@@ -760,18 +803,18 @@
         struct((CTX, 2 * HD, queries), bf16),
         struct((heads * HD, queries), bf16),
         struct((queries, width), bf16),
-        struct((heads, queries), f32),
+        struct((heads, 1, queries), f32),
         struct((2, width), f32),
         struct((HD // 2, queries), f32),
         struct((HD // 2, queries), f32),
     ]
     block = (LINE - 1, tokens, width)
-    count = 12 * (1 + PIECES) + 6 * (4 + 4 * (shards - 1)) + plane - 1 + 3
+    count = 6 + 18 * PIECES + 6 * (4 + 4 * (shards - 1)) + plane - 1 + 21
     return pl.pallas_call(
         functools.partial(forward_kernel, shards),
         out_shape=outs,
         in_specs=[any_spec()] * 8
-        + [vmem_spec()] * 3
+        + [vmem_spec()] * 2
         + [pl.BlockSpec(memory_space=pltpu.SMEM)],
         out_specs=[any_spec()] * 15 + [vmem_spec()] * 4,
         scratch_shapes=[
@@ -806,13 +849,13 @@
             collective_id=0, has_side_effects=True, vmem_limit_bytes=60 * 2**20
         ),
         name="forward",
-    )(x, og, wq, wkv, wo, wg, wu, wd, gain_a, gain_m, frequency, order)
+    )(x, og, wq, wkv, wo, wg, wu, wd, gain_in, frequency, order)
 
 
 def middle_kernel(
     shards, rows,
     n2_in, og_in, wg_in, wu_in, wd_in, mid_in, gains,
-    dmid_o, dmid_all_o, gg_o, gd_o, branch_o, gu_part_o, gain_sum,
+    dmid_o, dmid_all_o, gg_o, gd_part_o, gd_x_o, gd_y_o, branch_o, gu_part_o, gain_sum,
     n2, og, wg, wu, wd, mid, hidden, dgate, dup, part, branch,
     left, right, dmid, dsend, gain_rows, up_in,
     *rest,
@@ -821,12 +864,13 @@
     tokens, width = mid.shape
     queries = n2.shape[0]
     columns = wg.shape[1]
-    side = queries // 2
     links = Links(shards, send_sems, recv_sems, local_sems)
     t = links.t
     own_rows = pl.ds(pl.multiple_of(place(t) * tokens, tokens), tokens)
 
-    sides = [slice(0, side), slice(side, queries)]
+    far = pl.multiple_of(jnp.where(t < LINE // 2, tokens, 0), tokens)
+    near = pl.multiple_of(jnp.where(t < LINE // 2, 0, tokens), tokens)
+    sides = [pl.ds(far, tokens), pl.ds(2 * tokens, 2 * tokens), pl.ds(near, tokens)]
     full, rest_columns = columns // 256, columns % 256
     weights = ((wg_in, wg), (wu_in, wu), (wd_in, wd))
 
@@ -837,17 +881,17 @@
         return pltpu.make_async_copy(src.at[:, of], dst.at[:, of], sem)
 
     links.local_used = 3 * (full + 1)
-    load_n2 = links.keep(n2_in.at[sides[0]], n2.at[sides[0]])
+    load_n2 = [links.keep(n2_in.at[sides[0]], n2.at[sides[0]])]
     for index in range(full):
         for j in range(3):
             fetch(j, index * 256, 256, index).start()
         if index == 0:
-            load_og = links.keep(og_in.at[sides[0]], og.at[sides[0]])
+            load_og = [links.keep(og_in.at[sides[0]], og.at[sides[0]])]
     if rest_columns:
         for j in range(3):
             fetch(j, full * 256, rest_columns, full).start()
-    load_n2b = links.keep(n2_in.at[sides[1]], n2.at[sides[1]])
-    load_ogb = links.keep(og_in.at[sides[1]], og.at[sides[1]])
+    load_n2 += [links.keep(n2_in.at[at], n2.at[at]) for at in sides[1:]]
+    load_og += [links.keep(og_in.at[at], og.at[at]) for at in sides[1:]]
     load_mid = links.keep(mid_in, mid)
     scatter = LineScatter(links, part, tokens, left, right, PIECES)
     gather = LineGather(links, dsend, dmid_all_o, tokens, PIECES)
@@ -858,6 +902,8 @@
 
     def feed_forward(half):
         at = sides[half]
+        load_n2[half].wait()
+        load_og[half].wait()
 
         def tile(start, size, index):
             of = pl.ds(start, size)
@@ -895,19 +941,13 @@
         for step in range(1, shards):
             grad.other(step, room.at[pl.ds((step - 1) * piece, piece)])
 
-    load_n2.wait()
-    load_og.wait()
     feed_forward(0)
     line_ends(scatter, 0)
-    load_n2b.wait()
-    load_ogb.wait()
     feed_forward(1)
     line_ends(scatter, 1, 2)
     line_steps(scatter, 1)
+    feed_forward(2)
     others(gate, wg)
-    others(up, wu)
-    gate.own()
-    gate.exchange()
     line_steps(scatter, 2)
 
     @pl.loop(0, width // 512)
@@ -916,6 +956,8 @@
         branch[:, of] = nt_dot(hidden[...], wd[of, :]).astype(bf16)
 
     links.keep_later(branch, branch_o)
+    gate.own()
+    gate.exchange()
     others(down, wd)
     load_mid.wait()
     gain_rows[...] = jnp.zeros_like(gain_rows)
@@ -934,22 +976,24 @@
         dsend[at, :] = d_middle.astype(bf16)
 
     line_finish(scatter, finish_rows, gather)
+    gate.fold()
     down.own()
     down.exchange()
     links.keep_later(dsend, dmid_all_o.at[own_rows])
     links.keep_later(dmid, dmid_o)
+    links.keep_later(down.core_in.at[0], gd_part_o)
     line_spread(gather, 1)
+    others(up, wu)
+    gain_sum[...] = jnp.sum(gain_rows[...], 0, keepdims=True)
+    line_spread(gather, 2)
     up.own()
     links.keep_later(up_in.at[0], gu_part_o)
-    gain_sum[...] = jnp.sum(gain_rows[...], 0, keepdims=True)
-    gate.fold()
-    line_spread(gather, 2)
-    down.fold()
-    line_spread(gather, 3)
     gate.total()
     links.keep_later(gate.out, gg_o)
-    down.total()
-    links.keep_later(down.out, gd_o)
+    line_spread(gather, 3)
+    down.arrived()
+    links.keep_later(down.x_in, gd_x_o)
+    links.keep_later(down.y_in, gd_y_o)
     links.finish()
 
 
@@ -964,7 +1008,9 @@
         struct(token, f32),
         struct((queries, width), bf16),
         struct((rows, columns), f32),
-        struct((rows, columns), f32),
+        struct((CTX * rows, columns), bf16),
+        struct((2, rows // 2, columns), bf16),
+        struct((2, rows // 2, columns), bf16),
         struct((queries, width), bf16),
         struct((CTX * rows, columns), bf16),
         struct((1, width), f32),
@@ -974,7 +1020,7 @@
         functools.partial(middle_kernel, shards, rows),
         out_shape=outs,
         in_specs=[any_spec()] * 6 + [vmem_spec()],
-        out_specs=[any_spec()] * 6 + [vmem_spec()],
+        out_specs=[any_spec()] * 8 + [vmem_spec()],
         scratch_shapes=[
             pltpu.VMEM((queries, width), bf16),
             pltpu.VMEM((queries, width), bf16),
@@ -1009,12 +1055,12 @@
 def backward_kernel(
     shards, rows,
     dmid_all_in, wo_in, wq_in, wkv_in, n1_in, qaug_in, kaug_in, kv_in, att_in, x_in, dmid_in,
-    branch_in, gu_part_in, mid_in, lse, gains, gain_mlp, cos, sin,
-    in_o, gq_o, gkv_o, go_o, gu_o, out_o, gain_o,
+    branch_in, gu_part_in, gd_part_in, gd_x_in, gd_y_in, mid_in, lse, gains, gain_mlp, cos, sin,
+    in_o, gq_o, gkv_o, go_o, gu_o, gd_o, out_o, gain_o,
     dmid_all, wo, wq, wkv, n1, qaug, kaug, kv, att, x, dmid,
     d_out, attn_rows, v_rows, d_keys, d_values, d_query, d_query_rows, kv_send, kv_recv, d_kv, part,
     left, right, gain_rows, pair, plane_in, line_in, total, stage_o, stage_q, stage_kv,
-    branch, left_b, right_b, mid, layer,
+    branch, left_b, right_b, mid, layer, gain_sum, part_query,
     *rest,
 ):
     grads, (send_sems, recv_sems, local_sems) = rest[:-3], rest[-3:]
@@ -1033,6 +1079,7 @@
     g_q = PlaneScatter(links, n1, d_query_rows, rows, *grads[6:12])
     g_kv = PlaneScatter(links, n1, d_kv, rows, *grads[12:18])
     g_u = PlaneScatter(links, None, None, rows, *grads[18:24])
+    g_d = PlaneScatter(links, None, None, rows, *grads[24:30])
     kv_slot = links.slots(CTX - 1)
     plane_slot = links.slots(plane - 1)
     line_slot = links.slots(LINE - 1)
@@ -1041,8 +1088,9 @@
         links.keep(src, dst)
         for src, dst in (
             (branch_in, branch), (dmid_all_in, dmid_all), (wo_in, wo), (gu_part_in, g_u.core_in.at[0]),
-            (att_in, att), (kv_in, kv), (qaug_in, qaug), (kaug_in, kaug), (n1_in, n1), (wq_in, wq),
-            (wkv_in, wkv), (x_in, x), (dmid_in, dmid), (mid_in, mid),
+            (att_in, att), (kv_in, kv), (qaug_in, qaug), (kaug_in, kaug),
+            (gd_part_in, g_d.core_in.at[0]), (gd_x_in, g_d.x_in), (gd_y_in, g_d.y_in), (n1_in, n1),
+            (wq_in, wq), (wkv_in, wkv), (x_in, x), (dmid_in, dmid), (mid_in, mid),
         )
     ]
 
@@ -1065,13 +1113,16 @@
         v_rows[other * queries : (other + 1) * queries, :] = kv[other, HD : 2 * HD, :].T
     d_keys[...] = jnp.zeros_like(d_keys)
     d_values[...] = jnp.zeros_like(d_values)
+    for load in loads[8:11]:
+        load.wait()
+    g_d.fold(here=True)
 
     def head(h):
         at = pl.ds(pl.multiple_of(h * HD, HD), HD)
         query = qaug[h]
         d_head = d_out[at, :]
         delta = jnp.sum(d_head.astype(f32) * att[at, :].astype(f32), 0, keepdims=True)
-        log_sum = lse[pl.ds(h, 1), :]
+        log_sum = lse[h]
         d_q = jnp.zeros((HD, queries), f32)
         for b in range(0, length, BLOCK):
             e = b + BLOCK
@@ -1097,7 +1148,7 @@
         peer = lax.rem(c + step, CTX)
         links.send(kv_send.at[peer], kv_recv.at[step - 1], (s, peer, t), kv_slot + step - 1)
     scatter_out.stage(2)
-    for load in loads[8:]:
+    for load in loads[11:]:
         load.wait()
 
     cosine, sine = cos[...], sin[...]
@@ -1107,6 +1158,8 @@
         d_query[at : at + half, :] = d1 * cosine + d2 * sine
         d_query[at + half : at + HD, :] = d2 * cosine - d1 * sine
     d_query_rows[...] = d_query[...].astype(bf16).T
+    for b in range(0, width, 512):
+        part_query[:, b : b + 512] = nt_dot(d_query_rows[...], wq[b : b + 512, :])
     others(g_q, stage_q)
     others(g_o, stage_o)
     for step in range(1, CTX):
@@ -1121,13 +1174,11 @@
     )
     d_kv[...] = turned.astype(bf16).T
 
-    @pl.loop(0, width // 512)
-    def _(j):
-        at = pl.ds(pl.multiple_of(j * 512, 512), 512)
-        summed = nt_dot(d_query_rows[...], wq[at, :]) + nt_dot(d_kv[...], wkv[at, :])
-        part[:, at] = summed.astype(bf16)
-
-    line_ends(scatter, 0, 1, 2)
+    for b in range(0, width, 512):
+        summed = part_query[:, b : b + 512] + nt_dot(d_kv[...], wkv[b : b + 512, :])
+        part[:, b : b + 512] = summed.astype(bf16)
+
+    line_ends(scatter, 0, 1)
 
     gain_rows[...] = jnp.zeros_like(gain_rows)
 
@@ -1143,9 +1194,9 @@
     for step in range(1, plane):
         links.send(pair, plane_in.at[step - 1], links.plane_peer(step), plane_slot + step - 1)
     g_u.fold()
+    line_steps(scatter, 1)
     g_o.own()
     g_o.exchange()
-    line_steps(scatter, 1)
     summed = pair[...]
     for step in range(1, plane):
         links.recv(plane_in.at[step - 1], plane_slot + step - 1)
@@ -1153,6 +1204,7 @@
     total[...] = summed
     for step in range(1, LINE):
         links.send(total, line_in.at[step - 1], links.line_peer(step), line_slot + step - 1)
+    line_ends(scatter, 2)
     others(g_kv, stage_kv)
     g_q.own()
     g_q.exchange()
@@ -1169,6 +1221,12 @@
     links.keep_later(layer, out_o)
     g_q.fold()
     g_kv.fold()
+    g_u.total()
+    links.keep_later(g_u.out, gu_o)
+    g_o.total()
+    links.keep_later(g_o.out, go_o)
+    g_d.total(here=True)
+    links.keep_later(g_d.out, gd_o)
 
     def finish_rows(r, d_normed):
         at = pl.ds(r, ROWS)
@@ -1182,10 +1240,6 @@
 
     line_finish(scatter, finish_rows)
     links.keep_later(dmid, in_o)
-    g_u.total()
-    links.keep_later(g_u.out, gu_o)
-    g_o.total()
-    links.keep_later(g_o.out, go_o)
     g_q.total()
     links.keep_later(g_q.out, gq_o)
     g_kv.total()
@@ -1193,13 +1247,19 @@
     for step in range(1, LINE):
         links.recv(line_in.at[step - 1], line_slot + step - 1)
         summed = summed + line_in[step - 1]
-    gain_o[...] = summed
+    own_gains = gain_o.shape[1]
+    if own_gains == width:
+        gain_o[...] = summed
+    else:
+        gain_sum[...] = summed
+        me = s * CTX + c
+        gain_o[...] = gain_sum[:, pl.ds(pl.multiple_of(me * own_gains, own_gains), own_gains)]
     links.finish()
 
 
 def backward_call(
-    shards, rows, dmid_all, wo, wq, wkv, n1, qaug, kaug, kv, att, x, dmid, branch, gu_part, mid,
-    lse, gains, gain_mlp, cos, sin,
+    shards, rows, dmid_all, wo, wq, wkv, n1, qaug, kaug, kv, att, x, dmid, branch, gu_part,
+    gd_part, gd_x, gd_y, mid, lse, gains, gain_mlp, cos, sin,
 ):
     tokens, width = dmid.shape
     queries = n1.shape[0]
@@ -1208,6 +1268,7 @@
     inner = heads * HD
     columns = gu_part.shape[1]
     plane = shards * CTX
+    own_gains = width // plane if width // plane % 128 == 0 else width
     piece = CTX * rows * (shards - 1)
     token = (tokens, width)
     block = (LINE - 1,) + token
@@ -1217,15 +1278,16 @@
         struct((rows, 2 * HD), f32),
         struct((rows, inner), f32),
         struct((rows, columns), f32),
+        struct((rows, columns), f32),
         struct(token, bf16),
-        struct((2, width), f32),
+        struct((2, own_gains), f32),
     ]
-    count = 6 + 6 * PIECES + 4 * (shards - 1 + 6) + CTX - 1 + plane - 1 + LINE - 1
+    count = 6 + 6 * PIECES + 5 * (shards - 1 + 6) + CTX - 1 + plane - 1 + LINE - 1
     return pl.pallas_call(
         functools.partial(backward_kernel, shards, rows),
         out_shape=outs,
-        in_specs=[any_spec()] * 14 + [vmem_spec()] * 5,
-        out_specs=[any_spec()] * 6 + [vmem_spec()],
+        in_specs=[any_spec()] * 17 + [vmem_spec()] * 5,
+        out_specs=[any_spec()] * 7 + [vmem_spec()],
         scratch_shapes=[
             pltpu.VMEM((queries, width), bf16),
             pltpu.VMEM((width, inner), bf16),
@@ -1264,9 +1326,12 @@
             pltpu.VMEM(block, bf16),
             pltpu.VMEM(token, f32),
             pltpu.VMEM(token, bf16),
+            pltpu.VMEM((2, width), f32),
+            pltpu.VMEM((queries, width), f32),
             *PlaneScatter.scratch(shards, rows, inner),
             *PlaneScatter.scratch(shards, rows, inner),
             *PlaneScatter.scratch(shards, rows, 2 * HD),
+            *PlaneScatter.scratch(1 + 1, rows, columns),
             *PlaneScatter.scratch(1 + 1, rows, columns),
             pltpu.SemaphoreType.DMA((count,)),
             pltpu.SemaphoreType.DMA((count,)),
@@ -1277,38 +1342,43 @@
         ),
         name="backward",
     )(
-        dmid_all, wo, wq, wkv, n1, qaug, kaug, kv, att, x, dmid, branch, gu_part, mid,
-        lse, gains, gain_mlp, cos, sin,
+        dmid_all, wo, wq, wkv, n1, qaug, kaug, kv, att, x, dmid, branch, gu_part,
+        gd_part, gd_x, gd_y, mid, lse, gains, gain_mlp, cos, sin,
     )
 
 
-def finish_kernel(layer_in, *refs):
-    count = len(refs) // 2
+def finish_kernel(gains, layer_in, *refs):
+    count = (len(refs) - 2) // 2
     layer_out = refs[count]
     layer_out[0] = layer_in[...]
     refs[count + 1][0] = refs[0][...]
-    for src, dst in zip(refs[1:count], refs[count + 2 :]):
+    for src, dst in zip(refs[1:count], refs[count + 2 : -2]):
         dst[...] = src[...]
-
-
-def finish_call(arrays, steps=4):
+    for row, dst in enumerate(refs[-2:]):
+        dst[...] = gains[row : row + 1, :]
+
+
+def finish_call(arrays, gains, steps=4):
     rows = [array.shape[0] // steps for array in arrays]
     wide = [array.shape[1] for array in arrays]
+    own = gains.shape[1]
     shapes = [struct((1,) * (i < 2) + array.shape, array.dtype) for i, array in enumerate(arrays)]
     return pl.pallas_call(
         finish_kernel,
         grid=(steps,),
-        out_shape=shapes,
-        in_specs=[pl.BlockSpec((r, n), lambda i: (i, 0)) for r, n in zip(rows, wide)],
+        out_shape=shapes + [struct((1, own), f32)] * 2,
+        in_specs=[pl.BlockSpec((2, own), lambda i: (0, 0))]
+        + [pl.BlockSpec((r, n), lambda i: (i, 0)) for r, n in zip(rows, wide)],
         out_specs=[
             pl.BlockSpec((1, r, n), lambda i: (0, i, 0))
             if index < 2
             else pl.BlockSpec((r, n), lambda i: (i, 0))
             for index, (r, n) in enumerate(zip(rows, wide))
-        ],
-        compiler_params=pltpu.CompilerParams(vmem_limit_bytes=40 * 2**20),
+        ]
+        + [pl.BlockSpec((1, own), lambda i: (0, 0))] * 2,
+        compiler_params=pltpu.CompilerParams(vmem_limit_bytes=60 * 2**20),
         name="finish",
-    )(*arrays)
+    )(gains, *arrays)
 
 
 def body(
@@ -1321,33 +1391,33 @@
     frequency = np.float32(10000.0) ** (-np.arange(HD // 2, dtype=np.float32)[:, None] * 2.0 / HD)
     own = gain_attn.shape[0]
     start = (s * CTX + c) * own
-    if own % 128 == 0:
-        gain_a, gain_m = gain_attn[None], gain_mlp[None]
-    else:
-        place_gain = lambda gain: lax.dynamic_update_slice(
-            jnp.zeros((1, width), f32), gain.astype(f32)[None], (0, start)
-        )
-        gain_a, gain_m = place_gain(gain_attn), place_gain(gain_mlp)
+    row = lax.broadcasted_iota(jnp.int32, (2, own), 0)
+    gain_in = jnp.where(row == 0, gain_attn.astype(f32), gain_mlp.astype(f32))
+    aligned = own % 128 == 0
+    if not aligned:
+        gain_in = lax.dynamic_update_slice(jnp.zeros((2, width), f32), gain_in, (0, start))
     (wq, wkv, wo, wg, wu, wd, n1, og_all, n2, mid, qaug, kaug, kv, att, x_all, lse, gains, cos, sin) = forward_call(
-        shards, x, og, (w_query, w_keyval, w_output, w_gate, w_up, w_down), gain_a, gain_m,
+        shards, x, og, (w_query, w_keyval, w_output, w_gate, w_up, w_down), gain_in,
         jnp.asarray(frequency, f32), block_order[0],
     )
-    (dmid, dmid_all, grad_gate, grad_down, branch, gu_part, gm) = middle_call(
+    (dmid, dmid_all, grad_gate, gd_part, gd_x, gd_y, branch, gu_part, gm) = middle_call(
         shards, w_gate.shape[0], n2, og_all, wg, wu, wd, mid, gains
     )
-    (input_grad, grad_query, grad_keyval, grad_output, grad_up, layer_out, both) = backward_call(
+    (input_grad, grad_query, grad_keyval, grad_output, grad_up, grad_down, layer_out, both) = backward_call(
         shards, w_query.shape[0], dmid_all, wo, wq, wkv, n1, qaug, kaug, kv, att, x_all, dmid,
-        branch, gu_part, mid, lse, gains, gm, cos, sin,
+        branch, gu_part, gd_part, gd_x, gd_y, mid, lse, gains, gm, cos, sin,
     )
-    both = lax.dynamic_slice(both, (0, start), (2, gain_attn.shape[0]))
+    if not aligned:
+        both = lax.dynamic_slice(both, (0, start), (2, own))
     (
         layer_out, input_grad, grad_query, grad_keyval, grad_output, grad_gate, grad_up, grad_down,
+        *gain_grads,
     ) = finish_call([
         layer_out, input_grad, grad_query, grad_keyval, grad_output, grad_gate, grad_up, grad_down,
-    ])
+    ], both)
     return (
-        layer_out, input_grad, both[0], grad_query, grad_keyval, grad_output,
-        both[1], grad_gate, grad_up, grad_down,
+        layer_out, input_grad, gain_grads[0][0], grad_query, grad_keyval, grad_output,
+        gain_grads[1][0], grad_gate, grad_up, grad_down,
     )
 
 

time: 316 us -> 297 us (0.940)
  local copies, waits for them, and re-layouts: 10.4 us -> 0 us
  Pallas kernels: 303 us -> 293 us
    pallas_call x1, Pallas kernels: 127 us -> 118 us  [forward_call(): pl.pallas_call(functools.partial(forward_kernel, shards), out_shape=outs,...]
    unnamed x16 -> x0, local copies, waits for them, and re-layouts: 6.61 us -> none
    pallas_call x1, Pallas kernels: 96.2 us -> 91 us  [middle_call(): pl.pallas_call(functools.partial(middle_kernel, shards, rows), out_shape=...]
where the time goes in v6:
time: 297 us; the launch traced here: 296 us
  Pallas kernels  293 us (99%)
    pallas_call x1, Pallas kernels, forward_call(): pl.pallas_call(functools.partial(forward_kernel, shards), out_shape=outs,...  118 us
    pallas_call x1, Pallas kernels, middle_call(): pl.pallas_call(functools.partial(middle_kernel, shards, rows), out_shape=...  91 us
    pallas_call x1, Pallas kernels, backward_call(): pl.pallas_call(functools.partial(backward_kernel, shards, rows), out_shap...  78 us
    pallas_call x1, Pallas kernels, finish_call(): pl.pallas_call(finish_kernel, grid=(steps,), out_shape=shapes + [struct((...  6.28 us

profile of v6, /device:TPU:9, one launch (start us, length us, event | category | flops | bytes accessed | tf_op | source)
XLA Modules:
  0.0 295.8 jit_solution(17898977439782082678)
XLA Ops:
  0.7 0.7 convert_element_type.6
  1.3 0.7 convert_element_type.7
  2.0 0.6 broadcast_select_fusion.gain_in
  2.6 117.7 %forward.1 = (bf16[2048,512]{1,0:T(8,128)(2,1)}, bf16[2048,128]{1,0:T(8,128)(2,1)}, bf16[2048,512]{1,0:T(8,128)(2,1)}, bf16[2048,1408]{1,0:T(8,128)(2,1)}, bf16[...) custom-call(bf16[128,2048]{1,0:T(8,128)(2,1)} %bitcast.5, ...), custom_call_target="tpu_custom_call" | custom-call | tf_op jit(solution)/shard_map/forward/pallas_call | solution.py:813
  120.4 91.0 %middle.1 = (f32[128,2048]{1,0:T(8,128)}, bf16[512,2048]{1,0:T(8,128)(2,1)}, f32[256,1408]{1,0:T(8,128)}, bf16[1024,1408]{1,0:T(8,128)(2,1)}, bf16[2,128,1408]{2...) custom-call(bf16[512,2048]{1,0:T(8,128)(2,1)} %get-tuple-element.56., ...), custom_call_target="tpu_custom_call" | custom-call | tf_op jit(solution)/shard_map/middle/pallas_call | solution.py:1019
  211.4 78.0 %backward.1 = (f32[128,2048]{1,0:T(8,128)}, f32[256,512]{1,0:T(8,128)}, f32[256,128]{1,0:T(8,128)}, f32[256,512]{1,0:T(8,128)}, f32[256,1408]{1,0:T(8,128)}, /*i...) custom-call(bf16[512,2048]{1,0:T(8,128)(2,1)} %get-tuple-element.63.dmid_all_in, ...), custom_call_target="tpu_custom_call" | custom-call | tf_op jit(solution)/shard_map/backward/pallas_call | solution.py:1286
  289.3 6.3 %finish.1 = (bf16[1,128,2048]{2,1,0:T(8,128)(2,1)}, f32[1,128,2048]{2,1,0:T(8,128)}, f32[256,512]{1,0:T(8,128)}, f32[256,128]{1,0:T(8,128)}, f32[256,512]{1,0:T(...) custom-call(f32[2,256]{1,0:T(2,128)} %get-tuple-element.83.gains, ...), custom_call_target="tpu_custom_call" | custom-call | tf_op jit(solution)/shard_map/finish/pallas_call | solution.py:1366
  (1 shorter events, 0.0 us)

commit v7 on v6

--- a/solution.py
+++ b/solution.py
@@ -554,10 +554,12 @@
     me = s * CTX + c
     own_gains = gain_in.shape[1]
     if own_gains == width:
-        gpad[...] = gain_in[...]
+        gpad[...] = gain_in[...].astype(f32)
     else:
         gpad[...] = jnp.zeros_like(gpad)
-        gpad[:, pl.ds(pl.multiple_of(me * own_gains, own_gains), own_gains)] = gain_in[...]
+        gpad[:, pl.ds(pl.multiple_of(me * own_gains, own_gains), own_gains)] = gain_in[
+            ...
+        ].astype(f32)
     links.barrier()
     for step in range(1, plane):
         links.send(gpad, gains_all.at[me], links.plane_peer(step), gain_slot + step - 1)
@@ -1108,14 +1110,10 @@
     g_u.exchange()
     for load in loads[4:8]:
         load.wait()
-    attn_rows[...] = att[...].T
     for other in range(CTX):
         v_rows[other * queries : (other + 1) * queries, :] = kv[other, HD : 2 * HD, :].T
     d_keys[...] = jnp.zeros_like(d_keys)
     d_values[...] = jnp.zeros_like(d_values)
-    for load in loads[8:11]:
-        load.wait()
-    g_d.fold(here=True)
 
     def head(h):
         at = pl.ds(pl.multiple_of(h * HD, HD), HD)
@@ -1138,6 +1136,9 @@
     pl.loop(0, heads // 2)(head)
     line_ends(scatter_out, 1, 2)
     scatter_out.stage(1)
+    for load in loads[8:11]:
+        load.wait()
+    g_d.fold(here=True)
     pl.loop(heads // 2, heads)(head)
 
     for other in range(CTX):
@@ -1161,6 +1162,7 @@
     for b in range(0, width, 512):
         part_query[:, b : b + 512] = nt_dot(d_query_rows[...], wq[b : b + 512, :])
     others(g_q, stage_q)
+    attn_rows[...] = att[...].T
     others(g_o, stage_o)
     for step in range(1, CTX):
         links.recv(kv_recv.at[step - 1], kv_slot + step - 1)
@@ -1238,12 +1240,16 @@
         back = inverse * (d_unit - unit * jnp.mean(d_unit * unit, -1, keepdims=True))
         dmid[at, :] = dmid[at, :] + back
 
-    line_finish(scatter, finish_rows)
-    links.keep_later(dmid, in_o)
+    scatter.arrive(0)
+    scatter.owned(0, finish_rows)
     g_q.total()
     links.keep_later(g_q.out, gq_o)
     g_kv.total()
     links.keep_later(g_kv.out, gkv_o)
+    for p in range(1, PIECES):
+        scatter.arrive(p)
+        scatter.owned(p, finish_rows)
+    links.keep_later(dmid, in_o)
     for step in range(1, LINE):
         links.recv(line_in.at[step - 1], line_slot + step - 1)
         summed = summed + line_in[step - 1]
@@ -1358,7 +1364,7 @@
         dst[...] = gains[row : row + 1, :]
 
 
-def finish_call(arrays, gains, steps=4):
+def finish_call(arrays, gains, steps=8):
     rows = [array.shape[0] // steps for array in arrays]
     wide = [array.shape[1] for array in arrays]
     own = gains.shape[1]
@@ -1392,10 +1398,10 @@
     own = gain_attn.shape[0]
     start = (s * CTX + c) * own
     row = lax.broadcasted_iota(jnp.int32, (2, own), 0)
-    gain_in = jnp.where(row == 0, gain_attn.astype(f32), gain_mlp.astype(f32))
+    gain_in = jnp.where(row == 0, gain_attn, gain_mlp)
     aligned = own % 128 == 0
     if not aligned:
-        gain_in = lax.dynamic_update_slice(jnp.zeros((2, width), f32), gain_in, (0, start))
+        gain_in = lax.dynamic_update_slice(jnp.zeros((2, width), bf16), gain_in, (0, start))
     (wq, wkv, wo, wg, wu, wd, n1, og_all, n2, mid, qaug, kaug, kv, att, x_all, lse, gains, cos, sin) = forward_call(
         shards, x, og, (w_query, w_keyval, w_output, w_gate, w_up, w_down), gain_in,
         jnp.asarray(frequency, f32), block_order[0],

time: 297 us -> 297 us (level)
  no operation moved by 1% of the time
where the time goes in v7:
time: 297 us; the launch traced here: 296 us
  Pallas kernels  294 us (99%)
    pallas_call x1, Pallas kernels, forward_call(): pl.pallas_call(functools.partial(forward_kernel, shards), out_shape=outs,...  118 us
    pallas_call x1, Pallas kernels, middle_call(): pl.pallas_call(functools.partial(middle_kernel, shards, rows), out_shape=...  91 us
    pallas_call x1, Pallas kernels, backward_call(): pl.pallas_call(functools.partial(backward_kernel, shards, rows), out_shap...  76.9 us
    pallas_call x1, Pallas kernels, finish_call(): pl.pallas_call(finish_kernel, grid=(steps,), out_shape=shapes + [struct((...  8.2 us

profile of v7, /device:TPU:9, one launch (start us, length us, event | category | flops | bytes accessed | tf_op | source)
XLA Modules:
  0.0 296.0 jit_solution(15834865843223032572)
XLA Ops:
  0.7 1.3 broadcast_select_fusion.gain_in
  2.0 117.7 %forward.1 = (bf16[2048,512]{1,0:T(8,128)(2,1)}, bf16[2048,128]{1,0:T(8,128)(2,1)}, bf16[2048,512]{1,0:T(8,128)(2,1)}, bf16[2048,1408]{1,0:T(8,128)(2,1)}, bf16[...) custom-call(bf16[128,2048]{1,0:T(8,128)(2,1)} %bitcast.5, ...), custom_call_target="tpu_custom_call" | custom-call | tf_op jit(solution)/shard_map/forward/pallas_call | solution.py:815
  119.6 91.0 %middle.1 = (f32[128,2048]{1,0:T(8,128)}, bf16[512,2048]{1,0:T(8,128)(2,1)}, f32[256,1408]{1,0:T(8,128)}, bf16[1024,1408]{1,0:T(8,128)(2,1)}, bf16[2,128,1408]{2...) custom-call(bf16[512,2048]{1,0:T(8,128)(2,1)} %get-tuple-element.56., ...), custom_call_target="tpu_custom_call" | custom-call | tf_op jit(solution)/shard_map/middle/pallas_call | solution.py:1021
  210.7 76.9 %backward.1 = (f32[128,2048]{1,0:T(8,128)}, f32[256,512]{1,0:T(8,128)}, f32[256,128]{1,0:T(8,128)}, f32[256,512]{1,0:T(8,128)}, f32[256,1408]{1,0:T(8,128)}, /*i...) custom-call(bf16[512,2048]{1,0:T(8,128)(2,1)} %get-tuple-element.63.dmid_all_in, ...), custom_call_target="tpu_custom_call" | custom-call | tf_op jit(solution)/shard_map/backward/pallas_call | solution.py:1292
  287.6 8.2 %finish.1 = (bf16[1,128,2048]{2,1,0:T(8,128)(2,1)}, f32[1,128,2048]{2,1,0:T(8,128)}, f32[256,512]{1,0:T(8,128)}, f32[256,128]{1,0:T(8,128)}, f32[256,512]{1,0:T(...) custom-call(f32[2,256]{1,0:T(2,128)} %get-tuple-element.83.gains, ...), custom_call_target="tpu_custom_call" | custom-call | tf_op jit(solution)/shard_map/finish/pallas_call | solution.py:1372
  (1 shorter events, 0.0 us)

commit v8 on v7

--- a/solution.py
+++ b/solution.py
@@ -77,20 +77,19 @@
     def line_peer(self, step):
         return (self.s, self.c, lax.rem(self.t + step, LINE))
 
-    def barrier(self, whole_line=False):
+    def greet(self, whole_line=False):
         sem = pltpu.get_barrier_semaphore()
         count = self.shards * CTX - 1
         for step in range(1, count + 1):
             pl.semaphore_signal(
                 sem, inc=1, device_id=self.plane_peer(step), device_id_type=MESH
             )
-
         if whole_line:
             for step in range(1, LINE):
                 pl.semaphore_signal(
                     sem, inc=1, device_id=self.line_peer(step), device_id_type=MESH
                 )
-            pl.semaphore_wait(sem, count + LINE - 1)
+            self.partners = count + LINE - 1
             return
 
         @pl.when(self.t > 0)
@@ -102,7 +101,10 @@
             pl.semaphore_signal(sem, inc=1, device_id=self.right, device_id_type=MESH)
 
         beside = (self.t + LINE - 1) // LINE + (2 * LINE - 2 - self.t) // LINE
-        pl.semaphore_wait(sem, count + beside)
+        self.partners = count + beside
+
+    def met(self):
+        pl.semaphore_wait(pltpu.get_barrier_semaphore(), self.partners)
 
     def copy(self, src, dst, device, slot):
         return pltpu.make_async_remote_copy(
@@ -551,6 +553,7 @@
     gain_slot = links.slots(plane - 1)
     kv_slot = links.slots((CTX - 1) * (2 * LINE - 1))
 
+    links.greet()
     me = s * CTX + c
     own_gains = gain_in.shape[1]
     if own_gains == width:
@@ -560,7 +563,7 @@
         gpad[:, pl.ds(pl.multiple_of(me * own_gains, own_gains), own_gains)] = gain_in[
             ...
         ].astype(f32)
-    links.barrier()
+    links.met()
     for step in range(1, plane):
         links.send(gpad, gains_all.at[me], links.plane_peer(step), gain_slot + step - 1)
     own_gain = links.keep(gpad, gains_all.at[me])
@@ -711,25 +714,40 @@
     far = pl.multiple_of(jnp.where(t < LINE // 2, tokens, 0), tokens)
     near = pl.multiple_of(jnp.where(t < LINE // 2, 0, tokens), tokens)
 
-    def head(start, size, h):
-        lanes = pl.ds(start, size)
-        query = qaug[h, :, lanes]
+    def soften(query):
+        size = query.shape[1]
         top = jnp.full((1, size), -jnp.inf, f32)
         for b in range(0, length, BLOCK):
             block_scores = nn_dot(kaug[b : b + BLOCK, :], query)
-            scores[b : b + BLOCK, 0:size] = block_scores
+            scores[b : b + BLOCK, :] = block_scores
             top = jnp.maximum(top, jnp.max(block_scores, 0, keepdims=True))
         norm = jnp.zeros((1, size), f32)
         for b in range(0, length, BLOCK):
-            exponent = jnp.exp(scores[b : b + BLOCK, 0:size] - top)
+            exponent = jnp.exp(scores[b : b + BLOCK, :] - top)
             norm = norm + jnp.sum(exponent, 0, keepdims=True)
-            weights[b : b + BLOCK, 0:size] = exponent.astype(bf16)
-        out = nn_dot(v_all[...], weights[:, 0:size]) / norm
-        attn[pl.ds(pl.multiple_of(h * HD, HD), HD), lanes] = out.astype(bf16)
-        lse[h, :, lanes] = top + jnp.log(norm)
+            weights[b : b + BLOCK, :] = exponent.astype(bf16)
+        out = nn_dot(v_all[...], weights[...]) / norm
+        return out.astype(bf16), top + jnp.log(norm)
+
+    def put(h, lanes, out, log_sum):
+        attn[pl.ds(pl.multiple_of(h * HD, HD), HD), lanes] = out
+        lse[h, :, lanes] = log_sum
+
+    def head(lanes, h):
+        put(h, lanes, *soften(qaug[h, :, lanes]))
+
+    def head_pair(lanes, g):
+        h = 2 * g
+        both = jnp.concatenate([qaug[h, :, lanes], qaug[h + 1, :, lanes]], 1)
+        out, log_sum = soften(both)
+        put(h, lanes, out[:, 0:tokens], log_sum[:, 0:tokens])
+        put(h + 1, lanes, out[:, tokens:], log_sum[:, tokens:])
 
     def attend(start, size):
-        pl.loop(0, heads)(functools.partial(head, start, size))
+        if size == tokens:
+            pl.loop(0, heads // 2)(functools.partial(head_pair, pl.ds(start, size)))
+        else:
+            pl.loop(0, heads)(functools.partial(head, pl.ds(start, size)))
         rows = pl.ds(start, size)
         attn_rows = attn[:, rows].T
         for b in range(0, width, 512):
@@ -868,6 +886,7 @@
     columns = wg.shape[1]
     links = Links(shards, send_sems, recv_sems, local_sems)
     t = links.t
+    links.greet()
     own_rows = pl.ds(pl.multiple_of(place(t) * tokens, tokens), tokens)
 
     far = pl.multiple_of(jnp.where(t < LINE // 2, tokens, 0), tokens)
@@ -900,7 +919,6 @@
     down = PlaneScatter(links, og, hidden, rows, *grads[0:6])
     gate = PlaneScatter(links, n2, dgate, rows, *grads[6:12])
     up = PlaneScatter(links, n2, dup, rows, up_in, None, None, None, None, None)
-    links.barrier()
 
     def feed_forward(half):
         at = sides[half]
@@ -944,6 +962,7 @@
             grad.other(step, room.at[pl.ds((step - 1) * piece, piece)])
 
     feed_forward(0)
+    links.met()
     line_ends(scatter, 0)
     feed_forward(1)
     line_ends(scatter, 1, 2)
@@ -1074,6 +1093,7 @@
     plane = shards * CTX
     links = Links(shards, send_sems, recv_sems, local_sems)
     s, c, t = links.s, links.c, links.t
+    links.greet(whole_line=True)
 
     scatter = LineScatter(links, part, tokens, left, right, PIECES)
     scatter_out = LineScatter(links, branch, tokens, left_b, right_b)
@@ -1089,7 +1109,7 @@
     loads = [
         links.keep(src, dst)
         for src, dst in (
-            (branch_in, branch), (dmid_all_in, dmid_all), (wo_in, wo), (gu_part_in, g_u.core_in.at[0]),
+            (dmid_all_in, dmid_all), (wo_in, wo), (branch_in, branch), (gu_part_in, g_u.core_in.at[0]),
             (att_in, att), (kv_in, kv), (qaug_in, qaug), (kaug_in, kaug),
             (gd_part_in, g_d.core_in.at[0]), (gd_x_in, g_d.x_in), (gd_y_in, g_d.y_in), (n1_in, n1),
             (wq_in, wq), (wkv_in, wkv), (x_in, x), (dmid_in, dmid), (mid_in, mid),
@@ -1100,12 +1120,12 @@
         for step in range(1, shards):
             grad.other(step, stage.at[pl.ds((step - 1) * piece, piece)])
 
-    links.barrier(whole_line=True)
-    loads[0].wait()
-    line_ends(scatter_out, 0)
-    for load in loads[1:3]:
+    for load in loads[0:2]:
         load.wait()
     d_out[...] = nn_dot(dmid_all[...], wo[...]).astype(bf16).T
+    links.met()
+    loads[2].wait()
+    line_ends(scatter_out, 0)
     loads[3].wait()
     g_u.exchange()
     for load in loads[4:8]:
@@ -1141,13 +1161,16 @@
     g_d.fold(here=True)
     pl.loop(heads // 2, heads)(head)
 
-    for other in range(CTX):
-        block = slice(other * queries, (other + 1) * queries)
+    def pack(other):
+        block = pl.ds(pl.multiple_of(other * queries, queries), queries)
         both = jnp.concatenate([d_keys[block, :], d_values[block, :]], 1)
         kv_send[other] = both.astype(bf16)
+
     for step in range(1, CTX):
         peer = lax.rem(c + step, CTX)
+        pack(peer)
         links.send(kv_send.at[peer], kv_recv.at[step - 1], (s, peer, t), kv_slot + step - 1)
+    pack(c)
     scatter_out.stage(2)
     for load in loads[11:]:
         load.wait()
@@ -1364,7 +1387,7 @@
         dst[...] = gains[row : row + 1, :]
 
 
-def finish_call(arrays, gains, steps=8):
+def finish_call(arrays, gains, steps=2):
     rows = [array.shape[0] // steps for array in arrays]
     wide = [array.shape[1] for array in arrays]
     own = gains.shape[1]

time: 297 us -> 294 us (0.990)
  Pallas kernels: 294 us -> 291 us
where the time goes in v8:
time: 294 us; the launch traced here: 293 us
  Pallas kernels  291 us (99%)
    pallas_call x1, Pallas kernels, forward_call(): pl.pallas_call(functools.partial(forward_kernel, shards), out_shape=outs,...  119 us
    pallas_call x1, Pallas kernels, middle_call(): pl.pallas_call(functools.partial(middle_kernel, shards, rows), out_shape=...  88.4 us
    pallas_call x1, Pallas kernels, backward_call(): pl.pallas_call(functools.partial(backward_kernel, shards, rows), out_shap...  78.1 us

profile of v8, /device:TPU:9, one launch (start us, length us, event | category | flops | bytes accessed | tf_op | source)
XLA Modules:
  0.0 292.7 jit_solution(1122227167419968488)
XLA Ops:
  0.7 1.3 broadcast_select_fusion.gain_in
  2.0 118.7 %forward.1 = (bf16[2048,512]{1,0:T(8,128)(2,1)}, bf16[2048,128]{1,0:T(8,128)(2,1)}, bf16[2048,512]{1,0:T(8,128)(2,1)}, bf16[2048,1408]{1,0:T(8,128)(2,1)}, bf16[...) custom-call(bf16[128,2048]{1,0:T(8,128)(2,1)} %bitcast.5, ...), custom_call_target="tpu_custom_call" | custom-call | tf_op jit(solution)/shard_map/forward/pallas_call | solution.py:833
  120.6 88.4 %middle.1 = (f32[128,2048]{1,0:T(8,128)}, bf16[512,2048]{1,0:T(8,128)(2,1)}, f32[256,1408]{1,0:T(8,128)}, bf16[1024,1408]{1,0:T(8,128)(2,1)}, bf16[2,128,1408]{2...) custom-call(bf16[512,2048]{1,0:T(8,128)(2,1)} %get-tuple-element.56., ...), custom_call_target="tpu_custom_call" | custom-call | tf_op jit(solution)/shard_map/middle/pallas_call | solution.py:1040
  209.0 78.1 %backward.1 = (f32[128,2048]{1,0:T(8,128)}, f32[256,512]{1,0:T(8,128)}, f32[256,128]{1,0:T(8,128)}, f32[256,512]{1,0:T(8,128)}, f32[256,1408]{1,0:T(8,128)}, /*i...) custom-call(bf16[512,2048]{1,0:T(8,128)(2,1)} %get-tuple-element.63.dmid_all_in, ...), custom_call_target="tpu_custom_call" | custom-call | tf_op jit(solution)/shard_map/backward/pallas_call | solution.py:1315
  287.2 5.3 %finish.1 = (bf16[1,128,2048]{2,1,0:T(8,128)(2,1)}, f32[1,128,2048]{2,1,0:T(8,128)}, f32[256,512]{1,0:T(8,128)}, f32[256,128]{1,0:T(8,128)}, f32[256,512]{1,0:T(...) custom-call(f32[2,256]{1,0:T(2,128)} %get-tuple-element.83.gains, ...), custom_call_target="tpu_custom_call" | custom-call | tf_op jit(solution)/shard_map/finish/pallas_call | solution.py:1395
  (1 shorter events, 0.0 us)

commit v9 on v8

--- a/solution.py
+++ b/solution.py
@@ -395,50 +395,64 @@
 
 
 class PlaneScatter:
-    def __init__(self, links, left, right, rows, core_in, x_in, y_in, x_last, y_last, out):
+    def __init__(
+        self, links, left, right, rows, core_in, x_in, y_in, x_last, y_last, out, parts=1
+    ):
         self.links, self.left, self.right, self.rows = links, left, right, rows
         self.core_in, self.x_in, self.y_in = core_in, x_in, y_in
         self.x_last, self.y_last, self.out = x_last, y_last, out
-        self.first = links.slots(links.shards - 1 + 6)
         self.tile = min(256, CTX * rows)
+        self.parts = parts if CTX * rows // self.tile % parts == 0 else 1
+        self.core_first = links.slots((links.shards - 1) * self.parts)
+        self.first = links.slots(6)
 
     def product(self, shard, i):
         start = pl.multiple_of(shard * (CTX * self.rows) + i * self.tile, self.tile)
         return tn_dot(self.left[:, pl.ds(start, self.tile)], self.right[...])
 
-    @property
-    def tiles(self):
-        return CTX * self.rows // self.tile
-
-    def other(self, step, stage, part=None):
+    def part(self, ref, index):
+        size = CTX * self.rows // self.parts
+        return ref.at[pl.ds(index * size, size)]
+
+    def each_tile(self, index, body):
+        tiles = CTX * self.rows // self.tile // self.parts
+
+        @pl.loop(index * tiles, (index + 1) * tiles)
+        def _(i):
+            body(i, pl.ds(pl.multiple_of(i * self.tile, self.tile), self.tile))
+
+    def other(self, step, stage):
         links = self.links
         target = lax.rem(links.s + step, links.shards)
-        low, high = (0, self.tiles) if part is None else part
-
-        @pl.loop(low, high)
-        def _(i):
-            r = pl.multiple_of(i * self.tile, self.tile)
-            stage[pl.ds(r, self.tile), :] = self.product(target, i).astype(bf16)
-
-        if high == self.tiles:
-            return links.send(
-                stage, self.core_in.at[step - 1], links.core_peer(step), self.first + step - 1
+
+        def tile(i, at):
+            stage[at, :] = self.product(target, i).astype(bf16)
+
+        for index in range(self.parts):
+            self.each_tile(index, tile)
+            links.send(
+                self.part(stage, index),
+                self.part(self.core_in.at[step - 1], index),
+                links.core_peer(step),
+                self.core_first + (step - 1) * self.parts + index,
             )
 
-    def own(self, part=None):
+    def own(self):
         links = self.links
-        low, high = (0, self.tiles) if part is None else part
-        if low == 0:
-            for step in range(1, links.shards):
-                links.recv(self.core_in.at[step - 1], self.first + step - 1)
-
-        @pl.loop(low, high)
-        def _(i):
-            r = pl.multiple_of(i * self.tile, self.tile)
+
+        def tile(i, at):
             summed = self.product(links.s, i)
             for step in range(1, links.shards):
-                summed = summed + self.core_in[step - 1, pl.ds(r, self.tile), :].astype(f32)
-            self.core_in[0, pl.ds(r, self.tile), :] = summed.astype(bf16)
+                summed = summed + self.core_in[step - 1, at, :].astype(f32)
+            self.core_in[0, at, :] = summed.astype(bf16)
+
+        for index in range(self.parts):
+            for step in range(1, links.shards):
+                links.recv(
+                    self.part(self.core_in.at[step - 1], index),
+                    self.core_first + (step - 1) * self.parts + index,
+                )
+            self.each_tile(index, tile)
 
     def half(self, c, which):
         size = self.rows // 2
@@ -446,7 +460,7 @@
         return self.core_in.at[0, pl.ds(start, size)]
 
     def exchange(self):
-        links, first = self.links, self.first + self.links.shards - 1
+        links, first = self.links, self.first
         links.send(self.half(links.c_d, 0), self.x_in.at[1], links.x_dev, first)
         links.send(self.half(links.c_d, 1), self.y_in.at[1], links.y_dev, first + 1)
         links.send(self.half(links.c_x, 0), self.x_in.at[0], links.x_dev, first + 2)
@@ -464,13 +478,13 @@
             self.core_in[0, pl.ds(q, ROWS), :] = summed.astype(bf16)
 
     def arrived(self):
-        links, first = self.links, self.first + self.links.shards - 1
+        links, first = self.links, self.first
         for ref, offset in ((self.x_in, 0), (self.y_in, 1)):
             for part in range(2):
                 links.recv(ref.at[1 - part], first + offset + 2 * part)
 
     def fold(self, here=False):
-        links, first = self.links, self.first + self.links.shards - 1
+        links, first = self.links, self.first
         if not here:
             links.recv(self.x_in.at[1], first)
         self.add(links.c_y, 0, self.x_in)
@@ -481,7 +495,7 @@
         links.send(self.half(links.c_x, 1), self.x_last, links.x_dev, first + 5)
 
     def total(self, here=False):
-        links, first = self.links, self.first + self.links.shards - 1
+        links, first = self.links, self.first
         size = self.rows // 2
         if not here:
             links.recv(self.x_in.at[0], first + 2)
@@ -877,7 +891,7 @@
     n2_in, og_in, wg_in, wu_in, wd_in, mid_in, gains,
     dmid_o, dmid_all_o, gg_o, gd_part_o, gd_x_o, gd_y_o, branch_o, gu_part_o, gain_sum,
     n2, og, wg, wu, wd, mid, hidden, dgate, dup, part, branch,
-    left, right, dmid, dsend, gain_rows, up_in,
+    left, right, dmid, dsend, gain_rows, up_in, first,
     *rest,
 ):
     grads, (send_sems, recv_sems, local_sems) = rest[:-3], rest[-3:]
@@ -917,7 +931,7 @@
     scatter = LineScatter(links, part, tokens, left, right, PIECES)
     gather = LineGather(links, dsend, dmid_all_o, tokens, PIECES)
     down = PlaneScatter(links, og, hidden, rows, *grads[0:6])
-    gate = PlaneScatter(links, n2, dgate, rows, *grads[6:12])
+    gate = PlaneScatter(links, n2, dgate, rows, *grads[6:12], parts=2)
     up = PlaneScatter(links, n2, dup, rows, up_in, None, None, None, None, None)
 
     def feed_forward(half):
@@ -941,6 +955,11 @@
             d_gate = d_hidden * up_act * sig * (1.0 + gate_act * (1.0 - sig))
             dgate[at, of] = d_gate.astype(bf16)
             dup[at, of] = (d_hidden * silu).astype(bf16)
+            if half == 0:
+                for b in range(0, width, 512):
+                    e = b + 512
+                    summed = nt_dot(dgate[at, of], wg[b:e, of]) + nt_dot(dup[at, of], wu[b:e, of])
+                    first[:, b:e] += summed
 
         @pl.loop(0, full)
         def _(index):
@@ -948,6 +967,9 @@
 
         if rest_columns:
             tile(full * 256, rest_columns, full)
+        if half == 0:
+            part[at, :] = first[...].astype(bf16)
+            return
 
         @pl.loop(0, width // 512)
         def _(j):
@@ -961,6 +983,7 @@
         for step in range(1, shards):
             grad.other(step, room.at[pl.ds((step - 1) * piece, piece)])
 
+    first[...] = jnp.zeros_like(first)
     feed_forward(0)
     links.met()
     line_ends(scatter, 0)
@@ -971,14 +994,15 @@
     others(gate, wg)
     line_steps(scatter, 2)
 
+    gate.own()
+    gate.exchange()
+
     @pl.loop(0, width // 512)
     def _(j):
         of = pl.ds(pl.multiple_of(j * 512, 512), 512)
         branch[:, of] = nt_dot(hidden[...], wd[of, :]).astype(bf16)
 
     links.keep_later(branch, branch_o)
-    gate.own()
-    gate.exchange()
     others(down, wd)
     load_mid.wait()
     gain_rows[...] = jnp.zeros_like(gain_rows)
@@ -1036,7 +1060,7 @@
         struct((CTX * rows, columns), bf16),
         struct((1, width), f32),
     ]
-    count = 12 * PIECES + 3 * (shards - 1 + 6)
+    count = 12 * PIECES + 3 * (2 * (shards - 1) + 6)
     return pl.pallas_call(
         functools.partial(middle_kernel, shards, rows),
         out_shape=outs,
@@ -1060,6 +1084,7 @@
             pltpu.VMEM(token, bf16),
             pltpu.VMEM((ROWS, width), f32),
             pltpu.VMEM((shards - 1, CTX * rows, columns), bf16),
+            pltpu.VMEM(token, f32),
             *PlaneScatter.scratch(shards, rows, columns),
             *PlaneScatter.scratch(shards, rows, columns),
             pltpu.SemaphoreType.DMA((count,)),
@@ -1311,7 +1336,7 @@
         struct(token, bf16),
         struct((2, own_gains), f32),
     ]
-    count = 6 + 6 * PIECES + 5 * (shards - 1 + 6) + CTX - 1 + plane - 1 + LINE - 1
+    count = 6 + 6 * PIECES + 5 * (2 * (shards - 1) + 6) + CTX - 1 + plane - 1 + LINE - 1
     return pl.pallas_call(
         functools.partial(backward_kernel, shards, rows),
         out_shape=outs,

time: 294 us -> 295 us (level)
    pallas_call x1, Pallas kernels: 78.1 us -> 81.3 us  [backward_call(): pl.pallas_call(functools.partial(backward_kernel, shards, rows), out_shap...]
where the time goes in v9:
time: 295 us; the launch traced here: 294 us
  Pallas kernels  292 us (99%)
    pallas_call x1, Pallas kernels, forward_call(): pl.pallas_call(functools.partial(forward_kernel, shards), out_shape=outs,...  119 us
    pallas_call x1, Pallas kernels, middle_call(): pl.pallas_call(functools.partial(middle_kernel, shards, rows), out_shape=...  86.9 us
    pallas_call x1, Pallas kernels, backward_call(): pl.pallas_call(functools.partial(backward_kernel, shards, rows), out_shap...  81.3 us

profile of v9, /device:TPU:9, one launch (start us, length us, event | category | flops | bytes accessed | tf_op | source)
XLA Modules:
  0.0 294.3 jit_solution(12039702078768165756)
XLA Ops:
  0.7 1.3 broadcast_select_fusion.gain_in
  2.0 118.7 %forward.1 = (bf16[2048,512]{1,0:T(8,128)(2,1)}, bf16[2048,128]{1,0:T(8,128)(2,1)}, bf16[2048,512]{1,0:T(8,128)(2,1)}, bf16[2048,1408]{1,0:T(8,128)(2,1)}, bf16[...) custom-call(bf16[128,2048]{1,0:T(8,128)(2,1)} %bitcast.5, ...), custom_call_target="tpu_custom_call" | custom-call | tf_op jit(solution)/shard_map/forward/pallas_call | solution.py:847
  120.6 86.9 %middle.1 = (f32[128,2048]{1,0:T(8,128)}, bf16[512,2048]{1,0:T(8,128)(2,1)}, f32[256,1408]{1,0:T(8,128)}, bf16[1024,1408]{1,0:T(8,128)(2,1)}, bf16[2,128,1408]{2...) custom-call(bf16[512,2048]{1,0:T(8,128)(2,1)} %get-tuple-element.56., ...), custom_call_target="tpu_custom_call" | custom-call | tf_op jit(solution)/shard_map/middle/pallas_call | solution.py:1064
  207.5 81.3 %backward.1 = (f32[128,2048]{1,0:T(8,128)}, f32[256,512]{1,0:T(8,128)}, f32[256,128]{1,0:T(8,128)}, f32[256,512]{1,0:T(8,128)}, f32[256,1408]{1,0:T(8,128)}, /*i...) custom-call(bf16[512,2048]{1,0:T(8,128)(2,1)} %get-tuple-element.63.dmid_all_in, ...), custom_call_target="tpu_custom_call" | custom-call | tf_op jit(solution)/shard_map/backward/pallas_call | solution.py:1340
  288.8 5.3 %finish.1 = (bf16[1,128,2048]{2,1,0:T(8,128)(2,1)}, f32[1,128,2048]{2,1,0:T(8,128)}, f32[256,512]{1,0:T(8,128)}, f32[256,128]{1,0:T(8,128)}, f32[256,512]{1,0:T(...) custom-call(f32[2,256]{1,0:T(2,128)} %get-tuple-element.83.gains, ...), custom_call_target="tpu_custom_call" | custom-call | tf_op jit(solution)/shard_map/finish/pallas_call | solution.py:1420
  (1 shorter events, 0.0 us)

commit v10 on v9

--- a/solution.py
+++ b/solution.py
@@ -541,7 +541,7 @@
 
 def forward_kernel(
     shards,
-    x, og, wq, wkv, wo, wg, wu, wd, gain_in, frequency, order,
+    x, og, wq, wkv, wo, wg, wu, wd, gain_a, gain_m, frequency, order,
     wq_o, wkv_o, wo_o, wg_o, wu_o, wd_o, n1_o, og_o, n2_o, mid_o, qaug_o, kaug_o, kv_o, att_o, x_o,
     lse, gains, cos, sin,
     x_all, n1_all, wq_all, wkv_all, wo_all, gains_all, qaug, kv_all, kaug, v_all, scores, weights,
@@ -569,14 +569,14 @@
 
     links.greet()
     me = s * CTX + c
-    own_gains = gain_in.shape[1]
+    own_gains = gain_a.shape[0]
     if own_gains == width:
-        gpad[...] = gain_in[...].astype(f32)
+        own_lanes = slice(0, width)
     else:
         gpad[...] = jnp.zeros_like(gpad)
-        gpad[:, pl.ds(pl.multiple_of(me * own_gains, own_gains), own_gains)] = gain_in[
-            ...
-        ].astype(f32)
+        own_lanes = pl.ds(pl.multiple_of(me * own_gains, own_gains), own_gains)
+    for row, gain in enumerate((gain_a, gain_m)):
+        gpad[row : row + 1, own_lanes] = gain[...].astype(f32).reshape(1, own_gains)
     links.met()
     for step in range(1, plane):
         links.send(gpad, gains_all.at[me], links.plane_peer(step), gain_slot + step - 1)
@@ -819,7 +819,7 @@
         norm_block(t + k)
 
 
-def forward_call(shards, x, og, weights_in, gain_in, frequency, order):
+def forward_call(shards, x, og, weights_in, gain_a, gain_m, frequency, order):
     wq, wkv, wo, wg, wu, wd = weights_in
     tokens, width = x.shape
     queries = tokens * LINE
@@ -848,7 +848,7 @@
         functools.partial(forward_kernel, shards),
         out_shape=outs,
         in_specs=[any_spec()] * 8
-        + [vmem_spec()] * 2
+        + [vmem_spec()] * 3
         + [pl.BlockSpec(memory_space=pltpu.SMEM)],
         out_specs=[any_spec()] * 15 + [vmem_spec()] * 4,
         scratch_shapes=[
@@ -883,7 +883,7 @@
             collective_id=0, has_side_effects=True, vmem_limit_bytes=60 * 2**20
         ),
         name="forward",
-    )(x, og, wq, wkv, wo, wg, wu, wd, gain_in, frequency, order)
+    )(x, og, wq, wkv, wo, wg, wu, wd, gain_a, gain_m, frequency, order)
 
 
 def middle_kernel(
@@ -1445,13 +1445,15 @@
     frequency = np.float32(10000.0) ** (-np.arange(HD // 2, dtype=np.float32)[:, None] * 2.0 / HD)
     own = gain_attn.shape[0]
     start = (s * CTX + c) * own
-    row = lax.broadcasted_iota(jnp.int32, (2, own), 0)
-    gain_in = jnp.where(row == 0, gain_attn, gain_mlp)
+    gain_a, gain_m = gain_attn, gain_mlp
     aligned = own % 128 == 0
     if not aligned:
-        gain_in = lax.dynamic_update_slice(jnp.zeros((2, width), bf16), gain_in, (0, start))
+        gain_a, gain_m = (
+            lax.dynamic_update_slice(jnp.zeros((width,), bf16), gain, (start,))
+            for gain in (gain_attn, gain_mlp)
+        )
     (wq, wkv, wo, wg, wu, wd, n1, og_all, n2, mid, qaug, kaug, kv, att, x_all, lse, gains, cos, sin) = forward_call(
-        shards, x, og, (w_query, w_keyval, w_output, w_gate, w_up, w_down), gain_in,
+        shards, x, og, (w_query, w_keyval, w_output, w_gate, w_up, w_down), gain_a, gain_m,
         jnp.asarray(frequency, f32), block_order[0],
     )
     (dmid, dmid_all, grad_gate, gd_part, gd_x, gd_y, branch, gu_part, gm) = middle_call(

time: 295 us -> 293 us (level)
  no operation moved by 1% of the time
where the time goes in v10:
time: 293 us
  Pallas kernels  292 us (100%)
    pallas_call x1, Pallas kernels, forward_call(): pl.pallas_call(functools.partial(forward_kernel, shards), out_shape=outs,...  119 us
    pallas_call x1, Pallas kernels, middle_call(): pl.pallas_call(functools.partial(middle_kernel, shards, rows), out_shape=...  86.9 us
    pallas_call x1, Pallas kernels, backward_call(): pl.pallas_call(functools.partial(backward_kernel, shards, rows), out_shap...  81.3 us

profile of v10, /device:TPU:9, one launch (start us, length us, event | category | flops | bytes accessed | tf_op | source)
XLA Modules:
  0.0 293.1 jit_solution(17714512064973919225)
XLA Ops:
  0.6 118.8 %forward.1 = (bf16[2048,512]{1,0:T(8,128)(2,1)}, bf16[2048,128]{1,0:T(8,128)(2,1)}, bf16[2048,512]{1,0:T(8,128)(2,1)}, bf16[2048,1408]{1,0:T(8,128)(2,1)}, bf16[...) custom-call(bf16[128,2048]{1,0:T(8,128)(2,1)} %bitcast.5, ...), custom_call_target="tpu_custom_call" | custom-call | tf_op jit(solution)/shard_map/forward/pallas_call | solution.py:847
  119.4 86.9 %middle.1 = (f32[128,2048]{1,0:T(8,128)}, bf16[512,2048]{1,0:T(8,128)(2,1)}, f32[256,1408]{1,0:T(8,128)}, bf16[1024,1408]{1,0:T(8,128)(2,1)}, bf16[2,128,1408]{2...) custom-call(bf16[512,2048]{1,0:T(8,128)(2,1)} %get-tuple-element.56., ...), custom_call_target="tpu_custom_call" | custom-call | tf_op jit(solution)/shard_map/middle/pallas_call | solution.py:1064
  206.3 81.3 %backward.1 = (f32[128,2048]{1,0:T(8,128)}, f32[256,512]{1,0:T(8,128)}, f32[256,128]{1,0:T(8,128)}, f32[256,512]{1,0:T(8,128)}, f32[256,1408]{1,0:T(8,128)}, /*i...) custom-call(bf16[512,2048]{1,0:T(8,128)(2,1)} %get-tuple-element.63.dmid_all_in, ...), custom_call_target="tpu_custom_call" | custom-call | tf_op jit(solution)/shard_map/backward/pallas_call | solution.py:1340
  287.6 5.3 %finish.1 = (bf16[1,128,2048]{2,1,0:T(8,128)(2,1)}, f32[1,128,2048]{2,1,0:T(8,128)}, f32[256,512]{1,0:T(8,128)}, f32[256,128]{1,0:T(8,128)}, f32[256,512]{1,0:T(...) custom-call(f32[2,256]{1,0:T(2,128)} %get-tuple-element.83.gains, ...), custom_call_target="tpu_custom_call" | custom-call | tf_op jit(solution)/shard_map/finish/pallas_call | solution.py:1420

commit v11 on v10

--- a/solution.py
+++ b/solution.py
@@ -1269,14 +1269,14 @@
 
     scatter_out.owned(0, layer_rows)
     links.keep_later(layer, out_o)
-    g_q.fold()
-    g_kv.fold()
     g_u.total()
     links.keep_later(g_u.out, gu_o)
+    g_q.fold()
+    g_d.total(here=True)
+    links.keep_later(g_d.out, gd_o)
+    g_kv.fold()
     g_o.total()
     links.keep_later(g_o.out, go_o)
-    g_d.total(here=True)
-    links.keep_later(g_d.out, gd_o)
 
     def finish_rows(r, d_normed):
         at = pl.ds(r, ROWS)

time: 293 us -> 293 us (level)
  no operation moved by 1% of the time
where the time goes in v11:
time: 293 us
  Pallas kernels  292 us (100%)
    pallas_call x1, Pallas kernels, forward_call(): pl.pallas_call(functools.partial(forward_kernel, shards), out_shape=outs,...  119 us
    pallas_call x1, Pallas kernels, middle_call(): pl.pallas_call(functools.partial(middle_kernel, shards, rows), out_shape=...  86.9 us
    pallas_call x1, Pallas kernels, backward_call(): pl.pallas_call(functools.partial(backward_kernel, shards, rows), out_shap...  81.3 us

profile of v11, /device:TPU:9, one launch (start us, length us, event | category | flops | bytes accessed | tf_op | source)
XLA Modules:
  0.0 293.1 jit_solution(16576740932148611657)
XLA Ops:
  0.6 118.8 %forward.1 = (bf16[2048,512]{1,0:T(8,128)(2,1)}, bf16[2048,128]{1,0:T(8,128)(2,1)}, bf16[2048,512]{1,0:T(8,128)(2,1)}, bf16[2048,1408]{1,0:T(8,128)(2,1)}, bf16[...) custom-call(bf16[128,2048]{1,0:T(8,128)(2,1)} %bitcast.5, ...), custom_call_target="tpu_custom_call" | custom-call | tf_op jit(solution)/shard_map/forward/pallas_call | solution.py:847
  119.4 86.9 %middle.1 = (f32[128,2048]{1,0:T(8,128)}, bf16[512,2048]{1,0:T(8,128)(2,1)}, f32[256,1408]{1,0:T(8,128)}, bf16[1024,1408]{1,0:T(8,128)(2,1)}, bf16[2,128,1408]{2...) custom-call(bf16[512,2048]{1,0:T(8,128)(2,1)} %get-tuple-element.56., ...), custom_call_target="tpu_custom_call" | custom-call | tf_op jit(solution)/shard_map/middle/pallas_call | solution.py:1064
  206.3 81.3 %backward.1 = (f32[128,2048]{1,0:T(8,128)}, f32[256,512]{1,0:T(8,128)}, f32[256,128]{1,0:T(8,128)}, f32[256,512]{1,0:T(8,128)}, f32[256,1408]{1,0:T(8,128)}, /*i...) custom-call(bf16[512,2048]{1,0:T(8,128)(2,1)} %get-tuple-element.63.dmid_all_in, ...), custom_call_target="tpu_custom_call" | custom-call | tf_op jit(solution)/shard_map/backward/pallas_call | solution.py:1340
  287.6 5.3 %finish.1 = (bf16[1,128,2048]{2,1,0:T(8,128)(2,1)}, f32[1,128,2048]{2,1,0:T(8,128)}, f32[256,512]{1,0:T(8,128)}, f32[256,128]{1,0:T(8,128)}, f32[256,512]{1,0:T(...) custom-call(f32[2,256]{1,0:T(2,128)} %get-tuple-element.83.gains, ...), custom_call_target="tpu_custom_call" | custom-call | tf_op jit(solution)/shard_map/finish/pallas_call | solution.py:1420

commit v12 on v11

--- a/solution.py
+++ b/solution.py
@@ -477,11 +477,10 @@
             summed = mine + arrived[1, pl.ds(r, ROWS), :].astype(f32)
             self.core_in[0, pl.ds(q, ROWS), :] = summed.astype(bf16)
 
-    def arrived(self):
+    def arrived(self, part):
         links, first = self.links, self.first
         for ref, offset in ((self.x_in, 0), (self.y_in, 1)):
-            for part in range(2):
-                links.recv(ref.at[1 - part], first + offset + 2 * part)
+            links.recv(ref.at[1 - part], first + offset + 2 * part)
 
     def fold(self, here=False):
         links, first = self.links, self.first
@@ -1035,10 +1034,13 @@
     links.keep_later(up_in.at[0], gu_part_o)
     gate.total()
     links.keep_later(gate.out, gg_o)
+    down.arrived(0)
+    links.keep_later(down.x_in.at[1], gd_x_o.at[1])
+    links.keep_later(down.y_in.at[1], gd_y_o.at[1])
     line_spread(gather, 3)
-    down.arrived()
-    links.keep_later(down.x_in, gd_x_o)
-    links.keep_later(down.y_in, gd_y_o)
+    down.arrived(1)
+    links.keep_later(down.x_in.at[0], gd_x_o.at[0])
+    links.keep_later(down.y_in.at[0], gd_y_o.at[0])
     links.finish()
 
 
@@ -1412,7 +1414,7 @@
         dst[...] = gains[row : row + 1, :]
 
 
-def finish_call(arrays, gains, steps=2):
+def finish_call(arrays, gains, steps=1):
     rows = [array.shape[0] // steps for array in arrays]
     wide = [array.shape[1] for array in arrays]
     own = gains.shape[1]

time: 293 us -> 294 us (level)
  no operation moved by 1% of the time
where the time goes in v12:
time: 294 us; the launch traced here: 293 us
  Pallas kernels  293 us (100%)
    pallas_call x1, Pallas kernels, forward_call(): pl.pallas_call(functools.partial(forward_kernel, shards), out_shape=outs,...  119 us
    pallas_call x1, Pallas kernels, middle_call(): pl.pallas_call(functools.partial(middle_kernel, shards, rows), out_shape=...  86.9 us
    pallas_call x1, Pallas kernels, backward_call(): pl.pallas_call(functools.partial(backward_kernel, shards, rows), out_shap...  81 us
    pallas_call x1, Pallas kernels, finish_call(): pl.pallas_call(finish_kernel, grid=(steps,), out_shape=shapes + [struct((...  6.08 us

profile of v12, /device:TPU:9, one launch (start us, length us, event | category | flops | bytes accessed | tf_op | source)
XLA Modules:
  0.0 293.5 jit_solution(3692807179402709326)
XLA Ops:
  0.6 118.8 %forward.1 = (bf16[2048,512]{1,0:T(8,128)(2,1)}, bf16[2048,128]{1,0:T(8,128)(2,1)}, bf16[2048,512]{1,0:T(8,128)(2,1)}, bf16[2048,1408]{1,0:T(8,128)(2,1)}, bf16[...) custom-call(bf16[128,2048]{1,0:T(8,128)(2,1)} %bitcast.5, ...), custom_call_target="tpu_custom_call" | custom-call | tf_op jit(solution)/shard_map/forward/pallas_call | solution.py:846
  119.4 86.9 %middle.1 = (f32[128,2048]{1,0:T(8,128)}, bf16[512,2048]{1,0:T(8,128)(2,1)}, f32[256,1408]{1,0:T(8,128)}, bf16[1024,1408]{1,0:T(8,128)(2,1)}, bf16[2,128,1408]{2...) custom-call(bf16[512,2048]{1,0:T(8,128)(2,1)} %get-tuple-element.56., ...), custom_call_target="tpu_custom_call" | custom-call | tf_op jit(solution)/shard_map/middle/pallas_call | solution.py:1066
  206.3 81.0 %backward.1 = (f32[128,2048]{1,0:T(8,128)}, f32[256,512]{1,0:T(8,128)}, f32[256,128]{1,0:T(8,128)}, f32[256,512]{1,0:T(8,128)}, f32[256,1408]{1,0:T(8,128)}, /*i...) custom-call(bf16[512,2048]{1,0:T(8,128)(2,1)} %get-tuple-element.63.dmid_all_in, ...), custom_call_target="tpu_custom_call" | custom-call | tf_op jit(solution)/shard_map/backward/pallas_call | solution.py:1342
  287.4 6.1 %finish.1 = (bf16[1,128,2048]{2,1,0:T(8,128)(2,1)}, f32[1,128,2048]{2,1,0:T(8,128)}, f32[256,512]{1,0:T(8,128)}, f32[256,128]{1,0:T(8,128)}, f32[256,512]{1,0:T(...) custom-call(f32[2,256]{1,0:T(2,128)} %get-tuple-element.83.gains, ...), custom_call_target="tpu_custom_call" | custom-call | tf_op jit(solution)/shard_map/finish/pallas_call | solution.py:1422
